TPU v7x, 32 devices: a whole 2x2x4 slice. The times are simulated.
32 devices in a mesh: groups: 2 (over x), ctx: 16 (over z, y, core).
Axes of the slice: x: 2, y: 2, z: 4, core: 2. Of those that a mesh axis runs over, the one named last changes fastest.
Arguments:
- query_rows: bfloat16 [8192, 1024], P(('groups', 'ctx')), parts along dimension 0, may hold values from -6 to 6
- key_rows: bfloat16 [8192, 1024], P(('groups', 'ctx')), parts along dimension 0, may hold values from -6 to 6
- value_rows: bfloat16 [8192, 1024], P(('groups', 'ctx')), parts along dimension 0, may hold values from -6 to 6
- gate_values: bfloat16 [8192, 1024], P(('groups', 'ctx')), parts along dimension 0, may hold values from -6 to 6
- out_grad: bfloat16 [8192, 1024], P(('groups', 'ctx')), parts along dimension 0, may hold values from -6 to 6
- out_weight: bfloat16 [1024, 1024], replicated, may hold values from -0.1875 to 0.1875
- time_bias: float32 [16, 8], replicated, may hold values from -1 to 1
- route_slot: int32 [8192], P(('groups', 'ctx')), parts along dimension 0, may hold values from 0 to 511, as said below
- history_id: int32 [8192], P(('groups', 'ctx')), parts along dimension 0, may hold values from 0 to 3
- event_time: int32 [8192], P(('groups', 'ctx')), parts along dimension 0, may hold values from 0 to 32767
Outputs:
- layer_out: bfloat16 [8192, 1024], P(('groups', 'ctx')), parts along dimension 0
- query_grad: bfloat16 [8192, 1024], P(('groups', 'ctx')), parts along dimension 0
- key_grad: bfloat16 [8192, 1024], P(('groups', 'ctx')), parts along dimension 0
- value_grad: bfloat16 [8192, 1024], P(('groups', 'ctx')), parts along dimension 0
- gate_grad: bfloat16 [8192, 1024], P(('groups', 'ctx')), parts along dimension 0
- weight_grad: float32 [2048, 1024], P(('groups', 'ctx')), parts along dimension 0
- bias_grad: float32 [32, 8], P('groups'), parts along dimension 0
There are 2 independent parts, one for each index of `groups`. A program takes and returns all parts, laid end to end along the dimension named above; an argument that names none is the same for every part. Nothing has to cross between parts.
Inputs may be any that keep to these rules, and one draw needn't show every extreme that they name: Token t lies on loader device t // 256; route_slot values of one loader device are distinct, and the owner of token t is route_slot[t] // 32, so at most 32 tokens of one loader device go to one owner. In every draw one owner receives 32 tokens from every loader device.
All inputs are finite; a program needn't handle non-finite values.
Results may differ from a plain program's by a relative error of at most 0.0066.
Values may be sent and summed in bfloat16 or wider, within the bound.
No kernel may reach another device: no remote copies, remote signals or barrier semaphores. Data moves between devices by JAX's collectives and lax.ppermute only.
A program may use at most 128 MiB of HBM per device.

v0:
```python
import jax
import jax.numpy as jnp
from jax import lax
from jax.experimental import pallas as pl
from jax.experimental.pallas import tpu as pltpu
from jax.sharding import PartitionSpec as P

norm_epsilon = 1e-05
masked_score = -1e30
key_tile = 256
bf16 = jnp.bfloat16
f32 = jnp.float32
i32 = jnp.int32


def whole(ndim):
    return lambda *_: (0,) * ndim


def vmem_spec(shape):
    return pl.BlockSpec(tuple(shape), whole(len(shape)))


def shaped(shape, dtype):
    return jax.ShapeDtypeStruct(tuple(shape), dtype)


def dot(a, b, dims=((1,), (0,))):
    return lax.dot_general(a, b, (dims, ((), ())), preferred_element_type=f32)


def params(steps=0):
    semantics = ("arbitrary",) * steps if steps else None
    return pltpu.CompilerParams(dimension_semantics=semantics, vmem_limit_bytes=56 << 20)


def slot_ranks(slot_row):
    count = slot_row.shape[1]
    down = lax.broadcasted_iota(i32, (count, count), 0)
    across = lax.broadcasted_iota(i32, (count, count), 1)
    slot_col = jnp.sum(jnp.where(down == across, slot_row, 0), axis=1, keepdims=True)
    return slot_col, down, across


def sort_matrix(slot_row):
    slot_col, down, _ = slot_ranks(slot_row)
    rank_row = jnp.sum((slot_col < slot_row).astype(i32), axis=0, keepdims=True)
    return jnp.where(down == rank_row, 1.0, 0.0).astype(bf16)


def unsort_matrix(slot_row):
    slot_col, _, across = slot_ranks(slot_row)
    rank_col = jnp.sum((slot_row < slot_col).astype(i32), axis=1, keepdims=True)
    return jnp.where(across == rank_col, 1.0, 0.0).astype(bf16)


def pack_rows(peer_head, slot_row, query_rows, key_rows, value_rows, head_count):
    tokens, width = query_rows.shape
    size = width // head_count

    def body(peer, slot_ref, q_ref, k_ref, v_ref, *outs):
        order = sort_matrix(slot_ref[...])
        for k in range(head_count):
            cols = pl.ds(pl.multiple_of(peer[k] * size, size), size)
            outs[2 * k][:, :size] = dot(order, k_ref[:, cols]).astype(bf16)
            outs[2 * k][:, size:] = dot(order, v_ref[:, cols]).astype(bf16)
            outs[2 * k + 1][...] = dot(order, q_ref[:, cols]).astype(bf16)

    out_shape = [shaped((tokens, 2 * size), bf16), shaped((tokens, size), bf16)] * head_count
    outs = pl.pallas_call(
        body,
        grid_spec=pltpu.PrefetchScalarGridSpec(
            num_scalar_prefetch=1,
            grid=(1,),
            in_specs=[vmem_spec(slot_row.shape)] + [vmem_spec(query_rows.shape)] * 3,
            out_specs=[vmem_spec(s.shape) for s in out_shape],
        ),
        out_shape=out_shape,
        compiler_params=params(1),
        name="pack_rows",
    )(peer_head, slot_row, query_rows, key_rows, value_rows)
    return outs[0::2], outs[1::2]


def bias_tiles(head_bias, counts, history, stamps, query_max):
    owners, _, key_max = history.shape
    query_tile = min(128, query_max)
    buckets = head_bias.shape[0]

    def body(bias, count, hist_ref, time_ref, out_ref):
        owner = pl.program_id(0)
        eye = lax.broadcasted_iota(i32, (query_max, query_max), 0) == lax.broadcasted_iota(
            i32, (query_max, query_max), 1
        )
        hist_col = jnp.sum(jnp.where(eye, hist_ref[0, :, :query_max], 0), axis=1, keepdims=True)
        time_col = jnp.sum(jnp.where(eye, time_ref[0, :, :query_max], 0), axis=1, keepdims=True)
        for qt in range(query_max // query_tile):
            for kt in range(key_max // key_tile):

                @pl.when((qt * query_tile < count[owner]) & (kt * key_tile < count[owners + owner]))
                def _():
                    rows = slice(qt * query_tile, (qt + 1) * query_tile)
                    cols = slice(kt * key_tile, (kt + 1) * key_tile)
                    hist_row = hist_ref[0, :, cols]
                    gap = time_col[rows] - time_ref[0, :, cols]
                    allowed = (hist_col[rows] == hist_row) & (hist_row >= 0) & (gap >= 0)
                    level = jnp.full(gap.shape, bias[0], f32)
                    for e in range(buckets - 1):
                        level = jnp.where(gap >= 2**e, bias[e + 1], level)
                    out_ref[0, rows, cols] = jnp.where(allowed, level, masked_score)

    return pl.pallas_call(
        body,
        grid_spec=pltpu.PrefetchScalarGridSpec(
            num_scalar_prefetch=2,
            grid=(owners,),
            in_specs=[pl.BlockSpec((1, 1, key_max), lambda o, *_: (o, 0, 0))] * 2,
            out_specs=pl.BlockSpec((1, query_max, key_max), lambda o, *_: (o, 0, 0)),
        ),
        out_shape=shaped((owners, query_max, key_max), f32),
        compiler_params=params(1),
        name="bias_tiles",
    )(head_bias, counts, history, stamps)


def one_hot_rows(first, count, place):
    ids = lax.broadcasted_iota(i32, (count, place.shape[1]), 0) + first
    return jnp.where(ids == place, 1.0, 0.0).astype(bf16)


def gate_of(score):
    return 1.0 / (1.0 + jnp.exp(-jnp.maximum(score, -87.0)))


def attend_forward(starts, counts, place, bias, queries, pairs, window, query_max):
    owners, _, spots = place.shape
    head_count, loaders = len(queries), len(pairs)
    tokens, size = queries[0].shape
    key_max = bias.shape[2]
    query_tile = min(128, query_max)
    scale = size ** (-0.5)
    near = head_count * window

    def body(start, count, place_ref, bias_ref, *refs):
        q_refs = refs[:head_count]
        kv_refs = refs[head_count : head_count + loaders]
        outs = refs[head_count + loaders :]
        mixed_refs = outs[:head_count]
        qs_ref, kvs_ref, q_win, kv_win, acc, back = outs[head_count:]
        owner = pl.program_id(0)

        @pl.when(owner == 0)
        def _():
            for ref in mixed_refs:
                ref[...] = jnp.zeros(ref.shape, ref.dtype)

        query_count = count[owner]
        key_count = count[owners + owner]
        begin = [pl.multiple_of(start[owner * loaders + i], 16) for i in range(loaders)]
        for i in range(loaders):
            kv_win[i * window : (i + 1) * window, :] = kv_refs[i][pl.ds(begin[i], window), :]
        for i in range(head_count):
            q_win[i * window : (i + 1) * window, :] = q_refs[i][pl.ds(begin[i], window), :]
        for kt in range(key_max // key_tile):

            @pl.when(kt * key_tile < key_count)
            def _():
                chosen = one_hot_rows(kt * key_tile, key_tile, place_ref[0])
                kvs_ref[0, kt * key_tile : (kt + 1) * key_tile, :] = dot(
                    chosen, kv_win[...]
                ).astype(bf16)

        for qt in range(query_max // query_tile):

            @pl.when(qt * query_tile < query_count)
            def _():
                rows = slice(qt * query_tile, (qt + 1) * query_tile)
                chosen = one_hot_rows(qt * query_tile, query_tile, place_ref[0, :, :near])
                query = dot(chosen, q_win[...]).astype(bf16)
                qs_ref[0, rows, :] = query
                for kt in range(key_max // key_tile):

                    @pl.when(kt * key_tile < key_count)
                    def _():
                        cols = slice(kt * key_tile, (kt + 1) * key_tile)
                        score = (
                            dot(query, kvs_ref[0, cols, :size], ((1,), (1,))) * scale
                            + bias_ref[0, rows, cols]
                        )
                        weight = jnp.where(
                            score > 0.1 * masked_score, score * gate_of(score), 0.0
                        ).astype(bf16)
                        part = dot(weight, kvs_ref[0, cols, size:])
                        acc[...] = part if kt == 0 else acc[...] + part

                moved = dot(chosen, acc[...].astype(bf16), ((0,), (0,)))
                back[...] = moved if qt == 0 else back[...] + moved

        @pl.when(query_count > 0)
        def _():
            for i in range(head_count):
                spot = pl.ds(begin[i], window)
                mixed_refs[i][spot, :] = mixed_refs[i][spot, :] + back[
                    i * window : (i + 1) * window, :
                ].astype(bf16)

    out_shape = [shaped((tokens, size), bf16)] * head_count + [
        shaped((owners, query_max, size), bf16),
        shaped((owners, key_max, 2 * size), bf16),
    ]
    by_owner = lambda o, *_: (o, 0, 0)
    outs = pl.pallas_call(
        body,
        grid_spec=pltpu.PrefetchScalarGridSpec(
            num_scalar_prefetch=2,
            grid=(owners,),
            in_specs=[
                pl.BlockSpec((1, 1, spots), by_owner),
                pl.BlockSpec((1, query_max, key_max), by_owner),
            ]
            + [vmem_spec(x.shape) for x in queries]
            + [vmem_spec(x.shape) for x in pairs],
            out_specs=[vmem_spec((tokens, size))] * head_count
            + [
                pl.BlockSpec((1, query_max, size), by_owner),
                pl.BlockSpec((1, key_max, 2 * size), by_owner),
            ],
            scratch_shapes=[
                pltpu.VMEM((near, size), bf16),
                pltpu.VMEM((loaders * window, 2 * size), bf16),
                pltpu.VMEM((query_tile, size), f32),
                pltpu.VMEM((near, size), f32),
            ],
        ),
        out_shape=out_shape,
        compiler_params=params(1),
        name="attend_forward",
    )(starts, counts, place, bias, *queries, *pairs)
    return outs[:head_count], outs[head_count], outs[head_count + 1]


def norm_gate(peer_head, slot_row, gate_values, fresh_grad, mixed_parts):
    tokens, width = gate_values.shape
    head_count = len(mixed_parts)
    size = width // head_count

    def body(peer, slot_ref, gate_ref, grad_ref, *refs):
        parts = refs[:head_count]
        fresh_ref, gate_grad_ref = refs[head_count : head_count + 2]
        outs = refs[head_count + 2 : 2 * head_count + 2]
        joined, moved = refs[2 * head_count + 2 :]
        slot = slot_ref[...]
        unsort = unsort_matrix(slot)
        for k in range(head_count):
            cols = pl.ds(pl.multiple_of(peer[k] * size, size), size)
            joined[:, cols] = dot(unsort, parts[k][...])
        mixed = joined[...]
        centered = mixed - jnp.mean(mixed, axis=1, keepdims=True)
        inverse = lax.rsqrt(jnp.mean(centered * centered, axis=1, keepdims=True) + norm_epsilon)
        normed = centered * inverse
        gate = gate_ref[...].astype(f32)
        grad = grad_ref[...].astype(f32)
        fresh_ref[...] = (normed * gate).astype(bf16)
        gate_grad_ref[...] = (grad * normed).astype(bf16)
        normed_grad = grad * gate
        moved[...] = (
            inverse
            * (
                normed_grad
                - jnp.mean(normed_grad, axis=1, keepdims=True)
                - normed * jnp.mean(normed_grad * normed, axis=1, keepdims=True)
            )
        ).astype(bf16)
        order = sort_matrix(slot)
        for k in range(head_count):
            cols = pl.ds(pl.multiple_of(peer[k] * size, size), size)
            outs[k][...] = dot(order, moved[:, cols]).astype(bf16)

    out_shape = [shaped((tokens, width), bf16)] * 2 + [shaped((tokens, size), bf16)] * head_count
    outs = pl.pallas_call(
        body,
        grid_spec=pltpu.PrefetchScalarGridSpec(
            num_scalar_prefetch=1,
            grid=(1,),
            in_specs=[vmem_spec(slot_row.shape)]
            + [vmem_spec(gate_values.shape)] * 2
            + [vmem_spec(x.shape) for x in mixed_parts],
            out_specs=[vmem_spec(s.shape) for s in out_shape],
            scratch_shapes=[pltpu.VMEM((tokens, width), f32), pltpu.VMEM((tokens, width), bf16)],
        ),
        out_shape=out_shape,
        compiler_params=params(1),
        name="norm_gate",
    )(peer_head, slot_row, gate_values, fresh_grad, *mixed_parts)
    return outs[0], outs[1], outs[2:]


def attend_backward(
    starts, counts, place, bias, stamps, sorted_query, sorted_pair, grads, window, loaders, buckets
):
    owners, _, spots = place.shape
    head_count = len(grads)
    tokens, size = grads[0].shape
    query_max, key_max = bias.shape[1:]
    query_tile = min(128, query_max)
    scale = size ** (-0.5)
    near = head_count * window

    def body(start, count, place_ref, bias_ref, time_ref, qs_ref, kvs_ref, *refs):
        grad_refs = refs[:head_count]
        outs = refs[head_count:]
        dq_refs = outs[:head_count]
        dkv_refs = outs[head_count : head_count + loaders]
        sums_ref, grad_win, dq_acc, dkv_acc, dq_back, dkv_back = outs[head_count + loaders :]
        owner = pl.program_id(0)

        @pl.when(owner == 0)
        def _():
            for ref in tuple(dq_refs) + tuple(dkv_refs) + (sums_ref,):
                ref[...] = jnp.zeros(ref.shape, ref.dtype)

        query_count = count[owner]
        key_count = count[owners + owner]
        begin = [pl.multiple_of(start[owner * loaders + i], 16) for i in range(loaders)]
        for i in range(head_count):
            grad_win[i * window : (i + 1) * window, :] = grad_refs[i][pl.ds(begin[i], window), :]
        eye = lax.broadcasted_iota(i32, (query_max, query_max), 0) == lax.broadcasted_iota(
            i32, (query_max, query_max), 1
        )
        time_col = jnp.sum(jnp.where(eye, time_ref[0, :, :query_max], 0), axis=1, keepdims=True)
        for qt in range(query_max // query_tile):

            @pl.when(qt * query_tile < query_count)
            def _():
                rows = slice(qt * query_tile, (qt + 1) * query_tile)
                chosen = one_hot_rows(qt * query_tile, query_tile, place_ref[0, :, :near])
                grad = dot(chosen, grad_win[...]).astype(bf16)
                query = qs_ref[0, rows, :]
                for kt in range(key_max // key_tile):

                    @pl.when(kt * key_tile < key_count)
                    def _():
                        cols = slice(kt * key_tile, (kt + 1) * key_tile)
                        key = kvs_ref[0, cols, :size]
                        value = kvs_ref[0, cols, size:]
                        score = dot(query, key, ((1,), (1,))) * scale + bias_ref[0, rows, cols]
                        allowed = score > 0.1 * masked_score
                        gate = gate_of(score)
                        weight = jnp.where(allowed, score * gate, 0.0).astype(bf16)
                        product = dot(grad, value, ((1,), (1,)))
                        score_grad = jnp.where(
                            allowed, product * gate * (1.0 + score * (1.0 - gate)), 0.0
                        )
                        rounded = score_grad.astype(bf16)
                        dv = dot(weight, grad, ((0,), (0,)))
                        dk = dot(rounded, query, ((0,), (0,)))
                        dq = dot(rounded, key)
                        if qt == 0:
                            dkv_acc[cols, :size] = dk
                            dkv_acc[cols, size:] = dv
                        else:
                            dkv_acc[cols, :size] = dkv_acc[cols, :size] + dk
                            dkv_acc[cols, size:] = dkv_acc[cols, size:] + dv
                        dq_acc[...] = dq if kt == 0 else dq_acc[...] + dq
                        gap = time_col[rows] - time_ref[0, :, cols]
                        for level in range(buckets):
                            held = score_grad
                            if level > 0:
                                held = jnp.where(gap >= 2 ** (level - 1), score_grad, 0.0)
                            folded = jnp.sum(
                                held.reshape(query_tile // 8, 8, key_tile), axis=0
                            )
                            folded = folded[:, :128] + folded[:, 128:]
                            sums_ref[level] = sums_ref[level] + folded

                moved = dot(chosen, (dq_acc[...] * scale).astype(bf16), ((0,), (0,)))
                dq_back[...] = moved if qt == 0 else dq_back[...] + moved

        @pl.when(query_count > 0)
        def _():
            for i in range(head_count):
                spot = pl.ds(begin[i], window)
                dq_refs[i][spot, :] = dq_refs[i][spot, :] + dq_back[
                    i * window : (i + 1) * window, :
                ].astype(bf16)
            for kt in range(key_max // key_tile):

                @pl.when(kt * key_tile < key_count)
                def _():
                    cols = slice(kt * key_tile, (kt + 1) * key_tile)
                    chosen = one_hot_rows(kt * key_tile, key_tile, place_ref[0])
                    for half, factor in ((slice(0, size), scale), (slice(size, 2 * size), 1.0)):
                        moved = dot(
                            chosen, (dkv_acc[cols, half] * factor).astype(bf16), ((0,), (0,))
                        )
                        dkv_back[:, half] = moved if kt == 0 else dkv_back[:, half] + moved

            for i in range(loaders):
                spot = pl.ds(begin[i], window)
                dkv_refs[i][spot, :] = dkv_refs[i][spot, :] + dkv_back[
                    i * window : (i + 1) * window, :
                ].astype(bf16)

    out_shape = (
        [shaped((tokens, size), bf16)] * head_count
        + [shaped((tokens, 2 * size), bf16)] * loaders
        + [shaped((buckets, 8, 128), f32)]
    )
    by_owner = lambda o, *_: (o, 0, 0)
    outs = pl.pallas_call(
        body,
        grid_spec=pltpu.PrefetchScalarGridSpec(
            num_scalar_prefetch=2,
            grid=(owners,),
            in_specs=[
                pl.BlockSpec((1, 1, spots), by_owner),
                pl.BlockSpec((1, query_max, key_max), by_owner),
                pl.BlockSpec((1, 1, key_max), by_owner),
                pl.BlockSpec((1, query_max, size), by_owner),
                pl.BlockSpec((1, key_max, 2 * size), by_owner),
            ]
            + [vmem_spec(x.shape) for x in grads],
            out_specs=[vmem_spec(s.shape) for s in out_shape],
            scratch_shapes=[
                pltpu.VMEM((near, size), bf16),
                pltpu.VMEM((query_tile, size), f32),
                pltpu.VMEM((key_max, 2 * size), f32),
                pltpu.VMEM((near, size), f32),
                pltpu.VMEM((loaders * window, 2 * size), f32),
            ],
        ),
        out_shape=out_shape,
        compiler_params=params(1),
        name="attend_backward",
    )(starts, counts, place, bias, stamps, sorted_query, sorted_pair, *grads)
    return outs[:head_count], outs[head_count : head_count + loaders], outs[-1]


def weight_parts(rows_at, fresh_list, grad_list, piece, factor):
    tokens, width = fresh_list[0].shape
    sources = len(fresh_list)
    targets = rows_at.shape[0]

    def body(at, *refs):
        fresh_refs = refs[:sources]
        grad_refs = refs[sources : 2 * sources]
        outs = refs[2 * sources : 2 * sources + targets]
        (total,) = refs[2 * sources + targets :]
        for i in range(sources):
            part = dot(fresh_refs[i][...], grad_refs[i][...], ((0,), (0,)))
            total[...] = part if i == 0 else total[...] + part
        for j in range(targets):
            rows = pl.ds(pl.multiple_of(at[j] * piece, piece), piece)
            outs[j][...] = (total[rows, :] * factor).astype(bf16)

    out_shape = [shaped((piece, width), bf16)] * targets
    return pl.pallas_call(
        body,
        grid_spec=pltpu.PrefetchScalarGridSpec(
            num_scalar_prefetch=1,
            grid=(1,),
            in_specs=[vmem_spec((tokens, width))] * (2 * sources),
            out_specs=[vmem_spec((piece, width))] * targets,
            scratch_shapes=[pltpu.VMEM((width, width), f32)],
        ),
        out_shape=out_shape,
        compiler_params=params(1),
        name="weight_parts",
    )(rows_at, *fresh_list, *grad_list)


def unpack_rows(peer_head, slot_row, queries, pairs):
    head_count = len(queries)
    tokens, size = queries[0].shape
    width = head_count * size

    def body(peer, slot_ref, *refs):
        q_parts = refs[:head_count]
        kv_parts = refs[head_count : 2 * head_count]
        q_out, k_out, v_out = refs[2 * head_count :]
        unsort = unsort_matrix(slot_ref[...])
        for k in range(head_count):
            cols = pl.ds(pl.multiple_of(peer[k] * size, size), size)
            q_out[:, cols] = dot(unsort, q_parts[k][...]).astype(bf16)
            k_out[:, cols] = dot(unsort, kv_parts[k][:, :size]).astype(bf16)
            v_out[:, cols] = dot(unsort, kv_parts[k][:, size:]).astype(bf16)

    return pl.pallas_call(
        body,
        grid_spec=pltpu.PrefetchScalarGridSpec(
            num_scalar_prefetch=1,
            grid=(1,),
            in_specs=[vmem_spec(slot_row.shape)]
            + [vmem_spec(x.shape) for x in queries]
            + [vmem_spec(x.shape) for x in pairs],
            out_specs=[vmem_spec((tokens, width))] * 3,
        ),
        out_shape=[shaped((tokens, width), bf16)] * 3,
        compiler_params=params(1),
        name="unpack_rows",
    )(peer_head, slot_row, *queries, *pairs)


def on_device(
    query_rows,
    key_rows,
    value_rows,
    gate_values,
    out_grad,
    out_weight,
    time_bias,
    route_slot,
    history_id,
    event_time,
):
    ranks = lax.axis_size("ctx")
    tokens, width = query_rows.shape
    buckets, head_count = time_bias.shape
    slot_count = 2 * tokens
    capacity = slot_count // ranks
    siblings = ranks // head_count
    window = (capacity + 30) // 16 * 16
    query_max = head_count * capacity
    piece = width // ranks
    grad_scale = (tokens * ranks) ** (-0.5)
    me = lax.axis_index("ctx")
    head = me // siblings
    sibling = me % siblings
    peer_head = head ^ jnp.arange(head_count, dtype=i32)
    slot_row = route_slot.reshape(1, tokens)
    far_first = sorted(range(1, head_count), reverse=True)

    def flip(array, mask):
        return lax.ppermute(array, "ctx", [(i, i ^ mask) for i in range(ranks)])

    def exchange(parts):
        got = {k: flip(parts[k], k * siblings) for k in far_first}
        return [parts[0]] + [got[k] for k in range(1, head_count)]

    pair_parts, query_parts = pack_rows(
        peer_head, slot_row, query_rows, key_rows, value_rows, head_count
    )

    taken = route_slot[:, None] == jnp.arange(slot_count, dtype=i32)[None, :]
    slot_meta = jnp.stack(
        [
            jnp.sum(jnp.where(taken, history_id[:, None] + 1, 0), axis=0) - 1,
            jnp.sum(jnp.where(taken, event_time[:, None], 0), axis=0),
        ]
    )[None]
    mask = siblings
    while mask < ranks:
        slot_meta = jnp.concatenate([slot_meta, flip(slot_meta, mask)], axis=0)
        mask *= 2
    mask = 1
    while mask < siblings:
        slot_meta = jnp.concatenate([slot_meta, flip(slot_meta, mask)], axis=0)
        mask *= 2

    pairs = exchange(pair_parts)
    queries = exchange(query_parts)
    mask = 1
    while mask < siblings:
        pairs = pairs + [flip(x, mask) for x in pairs]
        mask *= 2

    def by_owner(table):
        return jnp.transpose(table.reshape(ranks, ranks, capacity), (1, 0, 2))

    hist_slots = by_owner(slot_meta[:, 0])
    time_slots = by_owner(slot_meta[:, 1])
    present = (hist_slots >= 0).astype(i32)
    each = jnp.sum(present, axis=2)
    before = jnp.arange(ranks)[:, None] < jnp.arange(ranks)[None, :]
    first = jnp.sum(jnp.where(before[:, :, None], each[:, None, :], 0), axis=0)
    base = jnp.sum(jnp.where(before[None], each[:, :, None], 0), axis=1)
    start = jnp.minimum(first // 16 * 16, tokens - window)
    offset = first - start
    step = jnp.arange(window, dtype=i32)[None, None]
    inside = (step >= offset[..., None]) & (step < (offset + each)[..., None])
    place = jnp.where(inside, step + (base - offset)[..., None], -1)
    place = place.reshape(ranks, 1, ranks * window)
    earlier = jnp.arange(capacity)[:, None] < jnp.arange(capacity)[None, :]
    within = jnp.sum(jnp.where(earlier[None, None], present[..., None], 0), axis=2)
    compact = jnp.where(present > 0, within + base[..., None], -1).reshape(ranks, slot_count)
    match = compact[:, :, None] == jnp.arange(slot_count, dtype=i32)[None, None, :]
    flat_hist = hist_slots.reshape(ranks, slot_count)[:, :, None]
    flat_time = time_slots.reshape(ranks, slot_count)[:, :, None]
    history = (jnp.sum(jnp.where(match, flat_hist + 1, 0), axis=1) - 1)[:, None, :]
    stamps = jnp.sum(jnp.where(match, flat_time, 0), axis=1)[:, None, :]
    counts = jnp.concatenate([jnp.sum(each[:, :head_count], axis=1), jnp.sum(each, axis=1)])
    starts = start.reshape(-1)

    head_bias = lax.dynamic_index_in_dim(time_bias, head, axis=1, keepdims=False)
    bias = bias_tiles(head_bias, counts, history, stamps, query_max)
    fresh_grad = lax.dot_general(
        out_grad, out_weight, (((1,), (1,)), ((), ())), preferred_element_type=f32
    ).astype(bf16)

    mixed, sorted_query, sorted_pair = attend_forward(
        starts, counts, place, bias, queries, pairs, window, query_max
    )
    fresh, gate_grad, grad_parts = norm_gate(
        peer_head, slot_row, gate_values, fresh_grad, exchange(mixed)
    )
    grads = exchange(grad_parts)
    layer_out = jnp.dot(fresh, out_weight, preferred_element_type=f32).astype(bf16)

    joint = list(range(2 * siblings))
    weight_targets = list(range(0, head_count, 2))
    out_grads = [out_grad] + [flip(out_grad, m) for m in joint[1:]]
    freshes = [fresh] + [flip(fresh, m) for m in joint[1:]]
    rows_at = (head ^ jnp.asarray(weight_targets, i32)) * siblings + sibling
    weight_sent = weight_parts(rows_at, freshes, out_grads, piece, grad_scale)
    weight_grad = weight_sent[0].astype(f32)
    for index in range(1, len(weight_targets)):
        weight_grad = weight_grad + flip(
            weight_sent[index], weight_targets[index] * siblings
        ).astype(f32)

    query_back, pair_back, sums = attend_backward(
        starts,
        counts,
        place,
        bias,
        stamps,
        sorted_query,
        sorted_pair,
        grads,
        window,
        ranks,
        buckets,
    )
    query_home = exchange(query_back)
    pair_sum = []
    for k in range(head_count):
        total = pair_back[k].astype(f32)
        for other in range(1, siblings):
            total = total + flip(pair_back[other * head_count + k], other).astype(f32)
        pair_sum.append(total.astype(bf16))
    pair_home = exchange(pair_sum)
    query_grad, key_grad, value_grad = unpack_rows(peer_head, slot_row, query_home, pair_home)

    above = jnp.sum(sums, axis=(1, 2))
    head_part = above - jnp.concatenate([above[1:], jnp.zeros((1,), f32)])
    bias_grad = jnp.where(
        jnp.arange(head_count)[None, :] == head, head_part[:, None] * grad_scale, 0.0
    )
    mask = 1
    while mask < ranks:
        bias_grad = bias_grad + flip(bias_grad, mask)
        mask *= 2
    return (layer_out, query_grad, key_grad, value_grad, gate_grad, weight_grad, bias_grad)


def solution(mesh):
    rows = P(("groups", "ctx"), None)
    flat = P(("groups", "ctx"))
    in_specs = (rows, rows, rows, rows, rows, P(), P(), flat, flat, flat)
    out_specs = (rows, rows, rows, rows, rows, rows, P("groups", None))
    return jax.shard_map(
        on_device, mesh=mesh, in_specs=in_specs, out_specs=out_specs, check_vma=False
    )
```

profile of v0, /device:TPU:0, one launch (start us, length us, event | category | flops | bytes accessed | tf_op | source)
XLA Modules:
  0.0 288.2 jit_solution(3947957712589639762)
XLA Ops:
  2.4 3.0 %collective-permute-start = (s32[1,2,512]{2,0,1:T(1,128)S(1)}, s32[1,2,512]{2,0,1:T(1,128)S(1)}, u32[]{:S(2)}, u32[]{:S(2)}) collective-permute-start(s32[1,2,512]{2,0,1:T(1,128)S(1)} %broadcast_in_dim.157), channel_id=1, source_target_pairs={{0,2},{1,3},{2,0},{3,1},{4,6},{5,7},{6,4},{7,5},{8,10},{9,11},{10,... | collective-permute-start | bytes 12296 | tf_op jit(solution)/shard_map/ppermute | solution.py:534
  5.9 4.0 %pack_rows.1 = (bf16[256,256]{1,0:T(8,128)(2,1)}, bf16[256,128]{1,0:T(8,128)(2,1)}, bf16[256,256]{1,0:T(8,128)(2,1)}, bf16[256,128]{1,0:T(8,128)(2,1)}, bf16[256...) custom-call(s32[8]{0:T(128)} %iota_xor_fusion.peer, ...), custom_call_target="tpu_custom_call" | custom-call | tf_op jit(solution)/shard_map/pack_rows/pallas_call | solution.py:70
  9.9 3.6 %collective-permute-start.10 = (bf16[256,128]{1,0:T(8,128)(2,1)}, bf16[256,128]{1,0:T(8,128)(2,1)S(1)}, u32[]{:S(2)}, u32[]{:S(2)}) collective-permute-start(bf16[256,128]{1,0:T(8,128)(2,1)} %get-tuple-element.82), channel_id=1, source_target_pairs={{0,14},{1,15},{2,12},{3,13},{4,10},{5,11},{6,8},{7,9},{8,6},{9,7},... | collective-permute-start | bytes 196616 | tf_op jit(solution)/shard_map/ppermute | solution.py:534
  17.1 3.6 %collective-permute-done.1 = s32[2,2,512]{2,0,1:T(2,128)S(1)} collective-permute-done((s32[2,2,512]{2,0,1:T(2,128)S(1)}, s32[2,2,512]{2,0,1:T(2,128)S(1)}, u32[]{:S(2)}, u32[]{:S(2)}) %collective-permute-start.1) | collective-permute-done | bytes 8224 | tf_op jit(solution)/shard_map/ppermute | solution.py:534
  20.8 4.6 %collective-permute-done.2 = s32[4,2,512]{2,0,1:T(4,128)S(1)} collective-permute-done((s32[4,2,512]{2,0,1:T(4,128)S(1)}, s32[4,2,512]{2,0,1:T(4,128)S(1)}, u32[]{:S(2)}, u32[]{:S(2)}) %collective-permute-start.2) | collective-permute-done | bytes 16416 | tf_op jit(solution)/shard_map/ppermute | solution.py:534
  30.2 4.7 %select_reduce_fusion = (s32[16,512]{1,0:T(8,128)S(1)}, s32[16,512]{1,0:T(8,128)S(1)}) fusion(s32[16,512]{1,0:T(8,128)S(1)} %broadcast_in_dim.169, s32[16,512]{1,0:T(8,128)S(1)} %eq.42, s32[16,512]{1,0:T(8,128)S(1)} %add.165), kind=kLoop, calls=%fused_computation | loop fusion | flops 20955136 | bytes 163840 | tf_op jit(solution)/shard_map/reduce_sum | solution.py:590
  35.0 3.9 %collective-permute-start.8 = (bf16[256,128]{1,0:T(8,128)(2,1)}, bf16[256,128]{1,0:T(8,128)(2,1)S(1)}, u32[]{:S(2)}, u32[]{:S(2)}) collective-permute-start(bf16[256,128]{1,0:T(8,128)(2,1)} %get-tuple-element.80), channel_id=1, source_target_pairs={{0,10},{1,11},{2,8},{3,9},{4,14},{5,15},{6,12},{7,13},{8,2},{9,3},... | collective-permute-start | bytes 196616 | tf_op jit(solution)/shard_map/ppermute | solution.py:534
  51.8 13.0 %bias_tiles.1.bias_ref = f32[16,256,512]{2,1,0:T(8,128)} custom-call(f32[16]{0:T(128)} %dynamic-slice_bitcast_fusion.bias, s32[32]{0:T(128)} %pad_add_fusion.4.count, s32[16,1,512]{2,1,0:T(1,128)} %sub.59.hist_ref, s32[16,1,512]{2,1,0:T(1,128)} %broadcast_in_dim.171.time_ref), custom_call_target="tpu_custom_call" | custom-call | tf_op jit(solution)/shard_map/bias_tiles/pallas_call | solution.py:112
  64.9 4.0 %collective-permute-start.16 = (bf16[256,256]{1,0:T(8,128)(2,1)S(1)}, bf16[256,256]{1,0:T(8,128)(2,1)S(1)}, u32[]{:S(2)}, u32[]{:S(2)}) collective-permute-start(bf16[256,256]{1,0:T(8,128)(2,1)S(1)} %copy-done.66), channel_id=1, source_target_pairs={{0,12},{1,13},{2,14},{3,15},{4,8},{5,9},{6,10},{7,11},{8,4},{9,5},... | collective-permute-start | bytes 393224 | tf_op jit(solution)/shard_map/ppermute | solution.py:534
  73.0 3.7 %collective-permute-done.17.refs_15_ = bf16[256,256]{1,0:T(8,128)(2,1)S(1)} collective-permute-done((bf16[256,256]{1,0:T(8,128)(2,1)S(1)}, bf16[256,256]{1,0:T(8,128)(2,1)S(1)}, u32[]{:S(2)}, u32[]{:S(2)}) %collective-permute-start.17) | collective-permute-done | bytes 131104 | tf_op jit(solution)/shard_map/ppermute | solution.py:534
  79.4 26.6 %attend_forward.1 = (bf16[256,128]{1,0:T(8,128)(2,1)}, bf16[256,128]{1,0:T(8,128)(2,1)}, bf16[256,128]{1,0:T(8,128)(2,1)}, bf16[256,128]{1,0:T(8,128)(2,1)}, bf1...) custom-call(s32[256]{0:T(256)} %multiply_minimum_fusion.start, ...), custom_call_target="tpu_custom_call" | custom-call | tf_op jit(solution)/shard_map/attend_forward/pallas_call | solution.py:212
  106.6 2.7 collective-permute-start.27
  114.6 2.7 collective-permute-start.32
  119.8 2.9 collective-permute-done.30.refs_5_
  123.4 4.5 %norm_gate.1 = (bf16[256,1024]{1,0:T(8,128)(2,1)}, bf16[256,1024]{1,0:T(8,128)(2,1)}, bf16[256,128]{1,0:T(8,128)(2,1)}, bf16[256,128]{1,0:T(8,128)(2,1)}, bf16[2...) custom-call(s32[8]{0:T(128)} %iota_xor_fusion.peer, ...), custom_call_target="tpu_custom_call" | custom-call | tf_op jit(solution)/shard_map/norm_gate/pallas_call | solution.py:280
  145.1 40.0 %attend_backward.1 = (bf16[256,128]{1,0:T(8,128)(2,1)}, bf16[256,128]{1,0:T(8,128)(2,1)}, bf16[256,128]{1,0:T(8,128)(2,1)}, bf16[256,128]{1,0:T(8,128)(2,1)}, bf...) custom-call(s32[256]{0:T(256)} %multiply_minimum_fusion.start, ...), custom_call_target="tpu_custom_call" | custom-call | tf_op jit(solution)/shard_map/attend_backward/pallas_call | solution.py:410
  208.8 3.5 %collective-permute-done.43.refs_4_ = bf16[256,128]{1,0:T(8,128)(2,1)S(1)} collective-permute-done((bf16[256,128]{1,0:T(8,128)(2,1)}, bf16[256,128]{1,0:T(8,128)(2,1)S(1)}, u32[]{:S(2)}, u32[]{:S(2)}) %collective-permute-start.43) | collective-permute-done | bytes 65568 | tf_op jit(solution)/shard_map/ppermute | solution.py:534
  216.1 4.7 %collective-permute-done.44.refs_5_ = bf16[256,128]{1,0:T(8,128)(2,1)S(1)} collective-permute-done((bf16[256,128]{1,0:T(8,128)(2,1)}, bf16[256,128]{1,0:T(8,128)(2,1)S(1)}, u32[]{:S(2)}, u32[]{:S(2)}) %collective-permute-start.44) | collective-permute-done | bytes 65568 | tf_op jit(solution)/shard_map/ppermute | solution.py:534
  224.5 4.7 %collective-permute-done.46.refs_7_ = bf16[256,128]{1,0:T(8,128)(2,1)S(1)} collective-permute-done((bf16[256,128]{1,0:T(8,128)(2,1)S(1)}, bf16[256,128]{1,0:T(8,128)(2,1)S(1)}, u32[]{:S(2)}, u32[]{:S(2)}) %collective-permute-start.46) | collective-permute-done | bytes 65568 | tf_op jit(solution)/shard_map/ppermute | solution.py:534
  232.8 3.5 %collective-permute-done.67.refs_7_ = bf16[256,1024]{1,0:T(8,128)(2,1)S(1)} collective-permute-done((bf16[256,1024]{1,0:T(8,128)(2,1)S(1)}, bf16[256,1024]{1,0:T(8,128)(2,1)S(1)}, u32[]{:S(2)}, u32[]{:S(2)}) %collective-permute-start.67) | collective-permute-done | bytes 524320 | tf_op jit(solution)/shard_map/ppermute | solution.py:534
  242.1 7.7 %collective-permute-done.63.refs_2_ = bf16[256,1024]{1,0:T(8,128)(2,1)S(1)} collective-permute-done((bf16[256,1024]{1,0:T(8,128)(2,1)S(1)}, bf16[256,1024]{1,0:T(8,128)(2,1)S(1)}, u32[]{:S(2)}, u32[]{:S(2)}) %collective-permute-start.63) | collective-permute-done | bytes 524320 | tf_op jit(solution)/shard_map/ppermute | solution.py:534
  249.8 14.4 %collective-permute-done.64.refs_3_ = bf16[256,1024]{1,0:T(8,128)(2,1)S(1)} collective-permute-done((bf16[256,1024]{1,0:T(8,128)(2,1)S(1)}, bf16[256,1024]{1,0:T(8,128)(2,1)S(1)}, u32[]{:S(2)}, u32[]{:S(2)}) %collective-permute-start.64) | collective-permute-done | bytes 524320 | tf_op jit(solution)/shard_map/ppermute | solution.py:534
  265.0 6.0 %weight_parts.1 = (bf16[64,1024]{1,0:T(8,128)(2,1)}, bf16[64,1024]{1,0:T(8,128)(2,1)}, bf16[64,1024]{1,0:T(8,128)(2,1)}, bf16[64,1024]{1,0:T(8,128)(2,1)}) custom-call(s32[4]{0:T(128)} %multiply_add_fusion.at, bf16[256,1024]{1,0:T(8,128)(2,1)} %get-tuple-element.99.refs_0_, bf16[256,1024]{1,0:T(8,128)(2,1)} %copy-done.5, bf16[256,1024]{1,0:T(8,128)(2,1)} %copy-done.6, ...), custom_call_target="tpu_custom_call" | custom-call | tf_op jit(solution)/shard_map/weight_parts/pallas_call | solution.py:457
  279.7 4.3 %unpack_rows.1 = (bf16[256,1024]{1,0:T(8,128)(2,1)}, bf16[256,1024]{1,0:T(8,128)(2,1)}, bf16[256,1024]{1,0:T(8,128)(2,1)}) custom-call(s32[8]{0:T(128)} %iota_xor_fusion.peer, s32[1,256]{1,0:T(1,128)} %bitcast.27, bf16[256,128]{1,0:T(8,128)(2,1)} %get-tuple-element.110.refs_0_, bf16[256,128]{1,0:T(8,128)(2,1)} %copy-done.51, bf16[256,128]{1,0:T(8,128)(2,1)} %copy-done.52, ...), custom_call_target="tpu_custom_call" | custom-call | tf_op jit(solution)/shard_map/unpack_rows/pallas_call | solution.py:488
  (353 shorter events, 110.4 us)
Async XLA Ops:
  2.4 14.5 %collective-permute-start = (s32[1,2,512]{2,0,1:T(1,128)S(1)}, s32[1,2,512]{2,0,1:T(1,128)S(1)}, u32[]{:S(2)}, u32[]{:S(2)}) collective-permute-start(s32[1,2,512]{2,0,1:T(1,128)S(1)} %broadcast_in_dim.157), channel_id=1, source_target_pairs={{0,2},{1,3},{2,0},{3,1},{4,6},{5,7},{6,4},{7,5},{8,10},{9,11},{10,... | collective-permute-start | bytes 12296 | tf_op jit(solution)/shard_map/ppermute | solution.py:534
  9.9 25.2 %collective-permute-start.10 = (bf16[256,128]{1,0:T(8,128)(2,1)}, bf16[256,128]{1,0:T(8,128)(2,1)S(1)}, u32[]{:S(2)}, u32[]{:S(2)}) collective-permute-start(bf16[256,128]{1,0:T(8,128)(2,1)} %get-tuple-element.82), channel_id=1, source_target_pairs={{0,14},{1,15},{2,12},{3,13},{4,10},{5,11},{6,8},{7,9},{8,6},{9,7},... | collective-permute-start | bytes 196616 | tf_op jit(solution)/shard_map/ppermute | solution.py:534
  13.4 25.5 %collective-permute-start.4 = (bf16[256,128]{1,0:T(8,128)(2,1)}, bf16[256,128]{1,0:T(8,128)(2,1)S(1)}, u32[]{:S(2)}, u32[]{:S(2)}) collective-permute-start(bf16[256,128]{1,0:T(8,128)(2,1)} %get-tuple-element.76), channel_id=1, source_target_pairs={{0,2},{1,3},{2,0},{3,1},{4,6},{5,7},{6,4},{7,5},{8,10},{9,11},{10,... | collective-permute-start | bytes 196616 | tf_op jit(solution)/shard_map/ppermute | solution.py:534
  15.0 24.4 %collective-permute-start.5 = (bf16[256,128]{1,0:T(8,128)(2,1)}, bf16[256,128]{1,0:T(8,128)(2,1)S(1)}, u32[]{:S(2)}, u32[]{:S(2)}) collective-permute-start(bf16[256,128]{1,0:T(8,128)(2,1)} %get-tuple-element.77), channel_id=1, source_target_pairs={{0,4},{1,5},{2,6},{3,7},{4,0},{5,1},{6,2},{7,3},{8,12},{9,13},{10,... | collective-permute-start | bytes 196616 | tf_op jit(solution)/shard_map/ppermute | solution.py:534
  15.0 25.3 %collective-permute-start.6 = (bf16[256,128]{1,0:T(8,128)(2,1)}, bf16[256,128]{1,0:T(8,128)(2,1)S(1)}, u32[]{:S(2)}, u32[]{:S(2)}) collective-permute-start(bf16[256,128]{1,0:T(8,128)(2,1)} %get-tuple-element.78), channel_id=1, source_target_pairs={{0,6},{1,7},{2,4},{3,5},{4,2},{5,3},{6,0},{7,1},{8,14},{9,15},{10,... | collective-permute-start | bytes 196616 | tf_op jit(solution)/shard_map/ppermute | solution.py:534
  26.8 13.8 %collective-permute-start.7 = (bf16[256,128]{1,0:T(8,128)(2,1)}, bf16[256,128]{1,0:T(8,128)(2,1)S(1)}, u32[]{:S(2)}, u32[]{:S(2)}) collective-permute-start(bf16[256,128]{1,0:T(8,128)(2,1)} %get-tuple-element.79), channel_id=1, source_target_pairs={{0,8},{1,9},{2,10},{3,11},{4,12},{5,13},{6,14},{7,15},{8,0},{9,1},... | collective-permute-start | bytes 196616 | tf_op jit(solution)/shard_map/ppermute | solution.py:534
  39.4 25.4 %collective-permute-start.11 = (bf16[256,256]{1,0:T(8,128)(2,1)}, bf16[256,256]{1,0:T(8,128)(2,1)S(1)}, u32[]{:S(2)}, u32[]{:S(2)}) collective-permute-start(bf16[256,256]{1,0:T(8,128)(2,1)} %get-tuple-element.84), channel_id=1, source_target_pairs={{0,2},{1,3},{2,0},{3,1},{4,6},{5,7},{6,4},{7,5},{8,10},{9,11},{10,... | collective-permute-start | bytes 393224 | tf_op jit(solution)/shard_map/ppermute | solution.py:534
  40.2 28.6 %collective-permute-start.12 = (bf16[256,256]{1,0:T(8,128)(2,1)}, bf16[256,256]{1,0:T(8,128)(2,1)S(1)}, u32[]{:S(2)}, u32[]{:S(2)}) collective-permute-start(bf16[256,256]{1,0:T(8,128)(2,1)} %get-tuple-element.85), channel_id=1, source_target_pairs={{0,4},{1,5},{2,6},{3,7},{4,0},{5,1},{6,2},{7,3},{8,12},{9,13},{10,... | collective-permute-start | bytes 393224 | tf_op jit(solution)/shard_map/ppermute | solution.py:534
  40.6 29.2 %collective-permute-start.13 = (bf16[256,256]{1,0:T(8,128)(2,1)}, bf16[256,256]{1,0:T(8,128)(2,1)S(1)}, u32[]{:S(2)}, u32[]{:S(2)}) collective-permute-start(bf16[256,256]{1,0:T(8,128)(2,1)} %get-tuple-element.86), channel_id=1, source_target_pairs={{0,6},{1,7},{2,4},{3,5},{4,2},{5,3},{6,0},{7,1},{8,14},{9,15},{10,... | collective-permute-start | bytes 393224 | tf_op jit(solution)/shard_map/ppermute | solution.py:534
  43.4 26.5 %collective-permute-start.14 = (bf16[256,256]{1,0:T(8,128)(2,1)}, bf16[256,256]{1,0:T(8,128)(2,1)S(1)}, u32[]{:S(2)}, u32[]{:S(2)}) collective-permute-start(bf16[256,256]{1,0:T(8,128)(2,1)} %get-tuple-element.87), channel_id=1, source_target_pairs={{0,8},{1,9},{2,10},{3,11},{4,12},{5,13},{6,14},{7,15},{8,0},{9,1},... | collective-permute-start | bytes 393224 | tf_op jit(solution)/shard_map/ppermute | solution.py:534
  46.5 23.9 %collective-permute-start.15 = (bf16[256,256]{1,0:T(8,128)(2,1)}, bf16[256,256]{1,0:T(8,128)(2,1)S(1)}, u32[]{:S(2)}, u32[]{:S(2)}) collective-permute-start(bf16[256,256]{1,0:T(8,128)(2,1)} %get-tuple-element.88), channel_id=1, source_target_pairs={{0,10},{1,11},{2,8},{3,9},{4,14},{5,15},{6,12},{7,13},{8,2},{9,3},... | collective-permute-start | bytes 393224 | tf_op jit(solution)/shard_map/ppermute | solution.py:534
  189.7 39.4 %collective-permute-start.65 = (bf16[256,1024]{1,0:T(8,128)(2,1)S(1)}, bf16[256,1024]{1,0:T(8,128)(2,1)}, u32[]{:S(2)}, u32[]{:S(2)}) collective-permute-start(bf16[256,1024]{1,0:T(8,128)(2,1)S(1)} %copy-done.1), channel_id=1, source_target_pairs={{0,1},{1,0},{2,3},{3,2},{4,5},{5,4},{6,7},{7,6},{8,9},{9,8},{10,11... | collective-permute-start | bytes 1572872 | tf_op jit(solution)/shard_map/ppermute | solution.py:534
  201.5 28.7 %collective-permute-start.66 = (bf16[256,1024]{1,0:T(8,128)(2,1)S(1)}, bf16[256,1024]{1,0:T(8,128)(2,1)S(1)}, u32[]{:S(2)}, u32[]{:S(2)}) collective-permute-start(bf16[256,1024]{1,0:T(8,128)(2,1)S(1)} %copy-done.1), channel_id=1, source_target_pairs={{0,2},{1,3},{2,0},{3,1},{4,6},{5,7},{6,4},{7,5},{8,10},{9,11},{10,... | collective-permute-start | bytes 1572872 | tf_op jit(solution)/shard_map/ppermute | solution.py:534
  208.8 13.3 %collective-permute-start.56 = (bf16[256,256]{1,0:T(8,128)(2,1)}, bf16[256,256]{1,0:T(8,128)(2,1)S(1)}, u32[]{:S(2)}, u32[]{:S(2)}) collective-permute-start(bf16[256,256]{1,0:T(8,128)(2,1)} %get-tuple-element.129), channel_id=1, source_target_pairs={{0,1},{1,0},{2,3},{3,2},{4,5},{5,4},{6,7},{7,6},{8,9},{9,8},{10,11... | collective-permute-start | bytes 393224 | tf_op jit(solution)/shard_map/ppermute | solution.py:534
  220.8 15.5 %collective-permute-start.67 = (bf16[256,1024]{1,0:T(8,128)(2,1)S(1)}, bf16[256,1024]{1,0:T(8,128)(2,1)S(1)}, u32[]{:S(2)}, u32[]{:S(2)}) collective-permute-start(bf16[256,1024]{1,0:T(8,128)(2,1)S(1)} %copy-done.1), channel_id=1, source_target_pairs={{0,3},{1,2},{2,1},{3,0},{4,7},{5,6},{6,5},{7,4},{8,11},{9,10},{10,... | collective-permute-start | bytes 1572872 | tf_op jit(solution)/shard_map/ppermute | solution.py:534
  229.1 12.9 %collective-permute-start.62 = (bf16[256,1024]{1,0:T(8,128)(2,1)S(1)}, bf16[256,1024]{1,0:T(8,128)(2,1)S(1)}, u32[]{:S(2)}, u32[]{:S(2)}) collective-permute-start(bf16[256,1024]{1,0:T(8,128)(2,1)S(1)} %copy-done.2), channel_id=1, source_target_pairs={{0,1},{1,0},{2,3},{3,2},{4,5},{5,4},{6,7},{7,6},{8,9},{9,8},{10,11... | collective-permute-start | bytes 1572872 | tf_op jit(solution)/shard_map/ppermute | solution.py:534
  229.1 20.7 %collective-permute-start.63 = (bf16[256,1024]{1,0:T(8,128)(2,1)S(1)}, bf16[256,1024]{1,0:T(8,128)(2,1)S(1)}, u32[]{:S(2)}, u32[]{:S(2)}) collective-permute-start(bf16[256,1024]{1,0:T(8,128)(2,1)S(1)} %copy-done.2), channel_id=1, source_target_pairs={{0,2},{1,3},{2,0},{3,1},{4,6},{5,7},{6,4},{7,5},{8,10},{9,11},{10,... | collective-permute-start | bytes 1572872 | tf_op jit(solution)/shard_map/ppermute | solution.py:534
  230.2 34.0 %collective-permute-start.64 = (bf16[256,1024]{1,0:T(8,128)(2,1)S(1)}, bf16[256,1024]{1,0:T(8,128)(2,1)S(1)}, u32[]{:S(2)}, u32[]{:S(2)}) collective-permute-start(bf16[256,1024]{1,0:T(8,128)(2,1)S(1)} %copy-done.2), channel_id=1, source_target_pairs={{0,3},{1,2},{2,1},{3,0},{4,7},{5,6},{6,5},{7,4},{8,11},{9,10},{10,... | collective-permute-start | bytes 1572872 | tf_op jit(solution)/shard_map/ppermute | solution.py:534
  237.7 33.2 %collective-permute-start.61 = (bf16[256,256]{1,0:T(8,128)(2,1)S(1)}, bf16[256,256]{1,0:T(8,128)(2,1)S(1)}, u32[]{:S(2)}, u32[]{:S(2)}) collective-permute-start(bf16[256,256]{1,0:T(8,128)(2,1)S(1)} %add_convert_fusion), channel_id=1, source_target_pairs={{0,14},{1,15},{2,12},{3,13},{4,10},{5,11},{6,8},{7,9},{8,6},{9,7},... | collective-permute-start | bytes 393224 | tf_op jit(solution)/shard_map/ppermute | solution.py:534
  240.2 32.6 %collective-permute-start.59 = (bf16[256,256]{1,0:T(8,128)(2,1)S(1)}, bf16[256,256]{1,0:T(8,128)(2,1)S(1)}, u32[]{:S(2)}, u32[]{:S(2)}) collective-permute-start(bf16[256,256]{1,0:T(8,128)(2,1)S(1)} %add_convert_fusion.1), channel_id=1, source_target_pairs={{0,12},{1,13},{2,14},{3,15},{4,8},{5,9},{6,10},{7,11},{8,4},{9,5},... | collective-permute-start | bytes 393224 | tf_op jit(solution)/shard_map/ppermute | solution.py:534
  242.1 31.8 %collective-permute-start.57 = (bf16[256,256]{1,0:T(8,128)(2,1)S(1)}, bf16[256,256]{1,0:T(8,128)(2,1)S(1)}, u32[]{:S(2)}, u32[]{:S(2)}) collective-permute-start(bf16[256,256]{1,0:T(8,128)(2,1)S(1)} %add_convert_fusion.2), channel_id=1, source_target_pairs={{0,10},{1,11},{2,8},{3,9},{4,14},{5,15},{6,12},{7,13},{8,2},{9,3},... | collective-permute-start | bytes 393224 | tf_op jit(solution)/shard_map/ppermute | solution.py:534
  249.8 24.3 %collective-permute-start.55 = (bf16[256,256]{1,0:T(8,128)(2,1)S(1)}, bf16[256,256]{1,0:T(8,128)(2,1)S(1)}, u32[]{:S(2)}, u32[]{:S(2)}) collective-permute-start(bf16[256,256]{1,0:T(8,128)(2,1)S(1)} %add_convert_fusion.3), channel_id=1, source_target_pairs={{0,8},{1,9},{2,10},{3,11},{4,12},{5,13},{6,14},{7,15},{8,0},{9,1},... | collective-permute-start | bytes 393224 | tf_op jit(solution)/shard_map/ppermute | solution.py:534
  264.2 12.2 %collective-permute-start.53 = (bf16[256,256]{1,0:T(8,128)(2,1)S(1)}, bf16[256,256]{1,0:T(8,128)(2,1)S(1)}, u32[]{:S(2)}, u32[]{:S(2)}) collective-permute-start(bf16[256,256]{1,0:T(8,128)(2,1)S(1)} %add_convert_fusion.4), channel_id=1, source_target_pairs={{0,6},{1,7},{2,4},{3,5},{4,2},{5,3},{6,0},{7,1},{8,14},{9,15},{10,... | collective-permute-start | bytes 393224 | tf_op jit(solution)/shard_map/ppermute | solution.py:534
  274.1 12.5 %collective-permute-start.69 = (bf16[64,1024]{1,0:T(8,128)(2,1)}, bf16[64,1024]{1,0:T(8,128)(2,1)S(1)}, u32[]{:S(2)}, u32[]{:S(2)}) collective-permute-start(bf16[64,1024]{1,0:T(8,128)(2,1)} %get-tuple-element.140), channel_id=1, source_target_pairs={{0,8},{1,9},{2,10},{3,11},{4,12},{5,13},{6,14},{7,15},{8,0},{9,1},... | collective-permute-start | bytes 393224 | tf_op jit(solution)/shard_map/ppermute | solution.py:534
  (124 other events, 1744.5 us)
where the time goes:
time: 290 us; the launch traced here: 288 us
  Pallas kernels  98.5 us (34%)
  starting transfers between devices  84.1 us (29%)
  waiting for transfers between devices  72.7 us (25%)
  other arithmetic  19.1 us (7%)
  local copies, waits for them, and re-layouts  9.25 us (3%)
  matrix products  3.04 us (1%)
    ppermute x75, starting transfers between devices, flip(): return lax.ppermute(array, 'ctx', [(i, i ^ mask) for i in range(ranks)])  84.1 us
    ppermute x75, waiting for transfers between devices, flip(): return lax.ppermute(array, 'ctx', [(i, i ^ mask) for i in range(ranks)])  72.7 us
    pallas_call x1, Pallas kernels, attend_backward(): pl.pallas_call(body, grid_spec=pltpu.PrefetchScalarGridSpec(num_scalar_pr...  40 us
    pallas_call x1, Pallas kernels, attend_forward(): pl.pallas_call(body, grid_spec=pltpu.PrefetchScalarGridSpec(num_scalar_pr...  26.6 us
    pallas_call x1, Pallas kernels, bias_tiles(): pl.pallas_call(body, grid_spec=pltpu.PrefetchScalarGridSpec(num_scalar_pr...  13 us
    pallas_call x1, Pallas kernels, weight_parts(): pl.pallas_call(body, grid_spec=pltpu.PrefetchScalarGridSpec(num_scalar_pr...  6 us
  transfers between devices with their start and end apart: 75, of which 26 were waited for; matrix products, arithmetic and copies ran while one was open for 7% of the time, Pallas kernels for 9%

commit v1 on v0

v1 whole, which is shorter than its diff:
```python
import jax
import jax.numpy as jnp
from jax import lax
from jax.experimental import pallas as pl
from jax.experimental.pallas import tpu as pltpu
from jax.sharding import PartitionSpec as P

norm_epsilon = 1e-05
masked_score = -1e30
key_tile = 256
bf16 = jnp.bfloat16
f32 = jnp.float32
i32 = jnp.int32


def whole(ndim):
    return lambda *_: (0,) * ndim


def vmem_spec(shape):
    return pl.BlockSpec(tuple(shape), whole(len(shape)))


def shaped(shape, dtype):
    return jax.ShapeDtypeStruct(tuple(shape), dtype)


def dot(a, b, dims=((1,), (0,))):
    return lax.dot_general(a, b, (dims, ((), ())), preferred_element_type=f32)


def params(steps=0):
    semantics = ("arbitrary",) * steps if steps else None
    return pltpu.CompilerParams(dimension_semantics=semantics, vmem_limit_bytes=56 << 20)


def slot_ranks(slot_row):
    count = slot_row.shape[1]
    down = lax.broadcasted_iota(i32, (count, count), 0)
    across = lax.broadcasted_iota(i32, (count, count), 1)
    slot_col = jnp.sum(jnp.where(down == across, slot_row, 0), axis=1, keepdims=True)
    return slot_col, down, across


def sort_matrix(slot_row):
    slot_col, down, _ = slot_ranks(slot_row)
    rank_row = jnp.sum((slot_col < slot_row).astype(i32), axis=0, keepdims=True)
    return jnp.where(down == rank_row, 1.0, 0.0).astype(bf16)


def unsort_matrix(slot_row):
    slot_col, _, across = slot_ranks(slot_row)
    rank_col = jnp.sum((slot_row < slot_col).astype(i32), axis=1, keepdims=True)
    return jnp.where(across == rank_col, 1.0, 0.0).astype(bf16)


def pack_rows(peer_head, slot_row, query_rows, key_rows, value_rows, head_count):
    tokens, width = query_rows.shape
    size = width // head_count

    def body(peer, slot_ref, q_ref, k_ref, v_ref, *outs):
        order = sort_matrix(slot_ref[...])
        for k in range(head_count):
            cols = pl.ds(pl.multiple_of(peer[k] * size, size), size)
            outs[k][:, :size] = dot(order, k_ref[:, cols]).astype(bf16)
            outs[k][:, size : 2 * size] = dot(order, v_ref[:, cols]).astype(bf16)
            outs[k][:, 2 * size :] = dot(order, q_ref[:, cols]).astype(bf16)

    out_shape = [shaped((tokens, 3 * size), bf16)] * head_count
    return pl.pallas_call(
        body,
        grid_spec=pltpu.PrefetchScalarGridSpec(
            num_scalar_prefetch=1,
            grid=(1,),
            in_specs=[vmem_spec(slot_row.shape)] + [vmem_spec(query_rows.shape)] * 3,
            out_specs=[vmem_spec(s.shape) for s in out_shape],
        ),
        out_shape=out_shape,
        compiler_params=params(1),
        name="pack_rows",
    )(peer_head, slot_row, query_rows, key_rows, value_rows)


def batch_of(owners):
    return 4 if owners % 4 == 0 else 1


def tiles_of(query_max, key_max, query_tile):
    return [
        (qt, kt) for qt in range(query_max // query_tile) for kt in range(key_max // key_tile)
    ][1:]


def bias_tiles(head_bias, counts, history, stamps, query_max):
    owners, _, key_max = history.shape
    query_tile = min(128, query_max)
    buckets = head_bias.shape[0]
    batch = batch_of(owners)

    def body(bias, count, hist_ref, time_ref, out_ref):
        eye = lax.broadcasted_iota(i32, (query_tile, query_tile), 0) == lax.broadcasted_iota(
            i32, (query_tile, query_tile), 1
        )

        def fill(g, qt, kt):
            rows = slice(qt * query_tile, (qt + 1) * query_tile)
            cols = slice(kt * key_tile, (kt + 1) * key_tile)
            hist_col = jnp.sum(jnp.where(eye, hist_ref[g, :, rows], 0), axis=1, keepdims=True)
            time_col = jnp.sum(jnp.where(eye, time_ref[g, :, rows], 0), axis=1, keepdims=True)
            hist_row = hist_ref[g, :, cols]
            gap = time_col - time_ref[g, :, cols]
            allowed = (hist_col == hist_row) & (hist_row >= 0) & (gap >= 0)
            level = jnp.full(gap.shape, bias[0], f32)
            for e in range(buckets - 1):
                level = jnp.where(gap >= 2**e, bias[e + 1], level)
            out_ref[g, rows, cols] = jnp.where(allowed, level, masked_score)

        for g in range(batch):
            fill(g, 0, 0)
        for g in range(batch):
            owner = pl.program_id(0) * batch + g
            for qt, kt in tiles_of(query_max, key_max, query_tile):

                @pl.when((qt * query_tile < count[owner]) & (kt * key_tile < count[owners + owner]))
                def _():
                    fill(g, qt, kt)

    return pl.pallas_call(
        body,
        grid_spec=pltpu.PrefetchScalarGridSpec(
            num_scalar_prefetch=2,
            grid=(owners // batch,),
            in_specs=[pl.BlockSpec((batch, 1, key_max), lambda o, *_: (o, 0, 0))] * 2,
            out_specs=pl.BlockSpec((batch, query_max, key_max), lambda o, *_: (o, 0, 0)),
        ),
        out_shape=shaped((owners, query_max, key_max), f32),
        compiler_params=params(1),
        name="bias_tiles",
    )(head_bias, counts, history, stamps)


def gather_matrix(first, count, place):
    ids = lax.broadcasted_iota(i32, (count, place.shape[1]), 0) + first
    return jnp.where(ids == place, 1.0, 0.0).astype(bf16)


def scatter_matrix(first, count, spans, window):
    step = lax.broadcasted_iota(i32, (window, 128), 0)
    reach = lax.broadcasted_iota(i32, (window, 128), 1) - step + first
    stack = []
    for low, high, shift in spans:
        inside = (step >= low) & (step < high)
        lanes = [
            jnp.where(inside & (reach == shift - lane), 1.0, 0.0) for lane in range(0, count, 128)
        ]
        stack.append(jnp.concatenate(lanes, axis=1)[:, :count])
    return jnp.concatenate(stack, axis=0).astype(bf16)


def gate_of(score):
    return 1.0 / (1.0 + jnp.exp(-jnp.maximum(score, -87.0)))


def read_plan(plan, owner, owners, loaders):
    at = lambda field, i: plan[(field * owners + owner) * loaders + i]
    begin = [pl.multiple_of(at(0, i), 16) for i in range(loaders)]
    spans = [(at(1, i), at(2, i), at(3, i)) for i in range(loaders)]
    return begin, spans


def attend_forward(plan, counts, place, bias, packs, window, head_count):
    owners, _, spots = place.shape
    loaders = len(packs)
    tokens = packs[0].shape[0]
    size = packs[0].shape[1] // 3
    query_max, key_max = bias.shape[1:]
    query_tile = min(128, query_max)
    scale = size ** (-0.5)
    near = head_count * window
    batch = batch_of(owners)

    def body(plan_ref, count, place_ref, bias_ref, *refs):
        pack_refs = refs[:loaders]
        mixed_refs = refs[loaders : loaders + head_count]
        qs_ref, kvs_ref, q_win, kv_win, acc, back = refs[loaders + head_count :]

        @pl.when(pl.program_id(0) == 0)
        def _():
            for ref in mixed_refs:
                ref[...] = jnp.zeros(ref.shape, ref.dtype)

        def attend(g, qt, kt):
            rows = slice(qt * query_tile, (qt + 1) * query_tile)
            cols = slice(kt * key_tile, (kt + 1) * key_tile)
            score = (
                dot(qs_ref[g, rows, :], kvs_ref[g, cols, :size], ((1,), (1,))) * scale
                + bias_ref[g, rows, cols]
            )
            weight = jnp.where(
                score > 0.1 * masked_score, score * gate_of(score), 0.0
            ).astype(bf16)
            part = dot(weight, kvs_ref[g, cols, size:])
            acc[g, rows, :] = part if kt == 0 else acc[g, rows, :] + part

        def load_keys(g, kt):
            chosen = gather_matrix(kt * key_tile, key_tile, place_ref[g])
            kvs_ref[g, kt * key_tile : (kt + 1) * key_tile, :] = dot(chosen, kv_win[g]).astype(bf16)

        def load_queries(g, qt):
            chosen = gather_matrix(qt * query_tile, query_tile, place_ref[g, :, :near])
            qs_ref[g, qt * query_tile : (qt + 1) * query_tile, :] = dot(chosen, q_win[g]).astype(bf16)

        owner_of = [pl.program_id(0) * batch + g for g in range(batch)]
        plans = [read_plan(plan_ref, owner, owners, loaders) for owner in owner_of]
        for g in range(batch):
            begin = plans[g][0]
            for i in range(loaders):
                spot = slice(i * window, (i + 1) * window)
                kv_win[g, spot, :] = pack_refs[i][pl.ds(begin[i], window), : 2 * size]
                if i < head_count:
                    q_win[g, spot, :] = pack_refs[i][pl.ds(begin[i], window), 2 * size :]
        for g in range(batch):
            load_keys(g, 0)
            load_queries(g, 0)
        for g in range(batch):
            attend(g, 0, 0)
        for g in range(batch):
            query_count = count[owner_of[g]]
            key_count = count[owners + owner_of[g]]

            @pl.when((query_count > query_tile) | (key_count > key_tile))
            def _():
                for kt in range(1, key_max // key_tile):
                    pl.when(kt * key_tile < key_count)(lambda: load_keys(g, kt))
                for qt in range(1, query_max // query_tile):
                    pl.when(qt * query_tile < query_count)(lambda: load_queries(g, qt))
                for qt, kt in tiles_of(query_max, key_max, query_tile):
                    pl.when((qt * query_tile < query_count) & (kt * key_tile < key_count))(
                        lambda: attend(g, qt, kt)
                    )

        for g in range(batch):
            chosen = scatter_matrix(0, query_tile, plans[g][1][:head_count], window)
            back[g] = dot(chosen, acc[g, :query_tile, :].astype(bf16))
        for g in range(batch):
            for qt in range(1, query_max // query_tile):

                @pl.when(qt * query_tile < count[owner_of[g]])
                def _():
                    chosen = scatter_matrix(
                        qt * query_tile, query_tile, plans[g][1][:head_count], window
                    )
                    rows = slice(qt * query_tile, (qt + 1) * query_tile)
                    back[g] = back[g] + dot(chosen, acc[g, rows, :].astype(bf16))

        for g in range(batch):
            for i in range(head_count):
                spot = pl.ds(plans[g][0][i], window)
                mixed_refs[i][spot, :] = mixed_refs[i][spot, :] + back[
                    g, i * window : (i + 1) * window, :
                ].astype(bf16)

    out_shape = [shaped((tokens, size), bf16)] * head_count + [
        shaped((owners, query_max, size), bf16),
        shaped((owners, key_max, 2 * size), bf16),
    ]
    by_owner = lambda o, *_: (o, 0, 0)
    outs = pl.pallas_call(
        body,
        grid_spec=pltpu.PrefetchScalarGridSpec(
            num_scalar_prefetch=2,
            grid=(owners // batch,),
            in_specs=[
                pl.BlockSpec((batch, 1, spots), by_owner),
                pl.BlockSpec((batch, query_max, key_max), by_owner),
            ]
            + [vmem_spec(x.shape) for x in packs],
            out_specs=[vmem_spec((tokens, size))] * head_count
            + [
                pl.BlockSpec((batch, query_max, size), by_owner),
                pl.BlockSpec((batch, key_max, 2 * size), by_owner),
            ],
            scratch_shapes=[
                pltpu.VMEM((batch, near, size), bf16),
                pltpu.VMEM((batch, loaders * window, 2 * size), bf16),
                pltpu.VMEM((batch, query_max, size), f32),
                pltpu.VMEM((batch, near, size), f32),
            ],
        ),
        out_shape=out_shape,
        compiler_params=params(1),
        name="attend_forward",
    )(plan, counts, place, bias, *packs)
    return outs[:head_count], outs[head_count], outs[head_count + 1]


def norm_gate(peer_head, slot_row, gate_values, fresh_grad, mixed_parts):
    tokens, width = gate_values.shape
    head_count = len(mixed_parts)
    size = width // head_count

    def body(peer, slot_ref, gate_ref, grad_ref, *refs):
        parts = refs[:head_count]
        fresh_ref, gate_grad_ref = refs[head_count : head_count + 2]
        outs = refs[head_count + 2 : 2 * head_count + 2]
        joined, moved = refs[2 * head_count + 2 :]
        slot = slot_ref[...]
        unsort = unsort_matrix(slot)
        for k in range(head_count):
            cols = pl.ds(pl.multiple_of(peer[k] * size, size), size)
            joined[:, cols] = dot(unsort, parts[k][...])
        mixed = joined[...]
        centered = mixed - jnp.mean(mixed, axis=1, keepdims=True)
        inverse = lax.rsqrt(jnp.mean(centered * centered, axis=1, keepdims=True) + norm_epsilon)
        normed = centered * inverse
        gate = gate_ref[...].astype(f32)
        grad = grad_ref[...].astype(f32)
        fresh_ref[...] = (normed * gate).astype(bf16)
        gate_grad_ref[...] = (grad * normed).astype(bf16)
        normed_grad = grad * gate
        moved[...] = (
            inverse
            * (
                normed_grad
                - jnp.mean(normed_grad, axis=1, keepdims=True)
                - normed * jnp.mean(normed_grad * normed, axis=1, keepdims=True)
            )
        ).astype(bf16)
        order = sort_matrix(slot)
        for k in range(head_count):
            cols = pl.ds(pl.multiple_of(peer[k] * size, size), size)
            outs[k][...] = dot(order, moved[:, cols]).astype(bf16)

    out_shape = [shaped((tokens, width), bf16)] * 2 + [shaped((tokens, size), bf16)] * head_count
    outs = pl.pallas_call(
        body,
        grid_spec=pltpu.PrefetchScalarGridSpec(
            num_scalar_prefetch=1,
            grid=(1,),
            in_specs=[vmem_spec(slot_row.shape)]
            + [vmem_spec(gate_values.shape)] * 2
            + [vmem_spec(x.shape) for x in mixed_parts],
            out_specs=[vmem_spec(s.shape) for s in out_shape],
            scratch_shapes=[pltpu.VMEM((tokens, width), f32), pltpu.VMEM((tokens, width), bf16)],
        ),
        out_shape=out_shape,
        compiler_params=params(1),
        name="norm_gate",
    )(peer_head, slot_row, gate_values, fresh_grad, *mixed_parts)
    return outs[0], outs[1], outs[2:]


def attend_backward(
    plan, counts, place, bias, stamps, sorted_query, sorted_pair, grads, window, loaders, buckets
):
    owners, _, spots = place.shape
    head_count = len(grads)
    tokens, size = grads[0].shape
    query_max, key_max = bias.shape[1:]
    query_tile = min(128, query_max)
    scale = size ** (-0.5)
    near = head_count * window
    batch = batch_of(owners)

    def body(plan_ref, count, place_ref, bias_ref, time_ref, qs_ref, kvs_ref, *refs):
        grad_refs = refs[:head_count]
        dq_ref, dkv_ref, sums_ref = refs[head_count : head_count + 3]
        grad_win, grad_rows, dq_acc, dkv_acc, dq_back, dkv_back = refs[head_count + 3 :]

        @pl.when(pl.program_id(0) == 0)
        def _():
            for ref in (dq_ref, dkv_ref, sums_ref):
                ref[...] = jnp.zeros(ref.shape, ref.dtype)

        eye = lax.broadcasted_iota(i32, (query_tile, query_tile), 0) == lax.broadcasted_iota(
            i32, (query_tile, query_tile), 1
        )

        def load_grads(g, qt):
            chosen = gather_matrix(qt * query_tile, query_tile, place_ref[g, :, :near])
            rows = slice(qt * query_tile, (qt + 1) * query_tile)
            grad_rows[g, rows, :] = dot(chosen, grad_win[g]).astype(bf16)

        def attend(g, qt, kt):
            rows = slice(qt * query_tile, (qt + 1) * query_tile)
            cols = slice(kt * key_tile, (kt + 1) * key_tile)
            query = qs_ref[g, rows, :]
            key = kvs_ref[g, cols, :size]
            value = kvs_ref[g, cols, size:]
            grad = grad_rows[g, rows, :]
            score = dot(query, key, ((1,), (1,))) * scale + bias_ref[g, rows, cols]
            product = dot(grad, value, ((1,), (1,)))
            allowed = score > 0.1 * masked_score
            gate = gate_of(score)
            silu = score * gate
            weight = jnp.where(allowed, silu, 0.0).astype(bf16)
            score_grad = jnp.where(allowed, product * (gate + silu * (1.0 - gate)), 0.0)
            rounded = score_grad.astype(bf16)
            dv = dot(weight, grad, ((0,), (0,)))
            dk = dot(rounded, query, ((0,), (0,)))
            dq = dot(rounded, key)
            if qt == 0:
                dkv_acc[g, cols, :size] = dk
                dkv_acc[g, cols, size:] = dv
            else:
                dkv_acc[g, cols, :size] = dkv_acc[g, cols, :size] + dk
                dkv_acc[g, cols, size:] = dkv_acc[g, cols, size:] + dv
            dq_acc[g, rows, :] = dq if kt == 0 else dq_acc[g, rows, :] + dq
            time_col = jnp.sum(jnp.where(eye, time_ref[g, :, rows], 0), axis=1, keepdims=True)
            gap = time_col - time_ref[g, :, cols]
            for level in range(buckets):
                held = score_grad
                if level > 0:
                    held = jnp.where(gap >= 2 ** (level - 1), score_grad, 0.0)
                folded = jnp.sum(held.reshape(query_tile // 8, 8, key_tile), axis=0)
                sums_ref[level] = sums_ref[level] + (folded[:, :128] + folded[:, 128:])

        owner_of = [pl.program_id(0) * batch + g for g in range(batch)]
        plans = [read_plan(plan_ref, owner, owners, loaders) for owner in owner_of]
        for g in range(batch):
            for i in range(head_count):
                grad_win[g, i * window : (i + 1) * window, :] = grad_refs[i][
                    pl.ds(plans[g][0][i], window), :
                ]
        for g in range(batch):
            load_grads(g, 0)
        for g in range(batch):
            attend(g, 0, 0)
        for g in range(batch):
            query_count = count[owner_of[g]]
            key_count = count[owners + owner_of[g]]

            @pl.when((query_count > query_tile) | (key_count > key_tile))
            def _():
                for qt in range(1, query_max // query_tile):
                    pl.when(qt * query_tile < query_count)(lambda: load_grads(g, qt))
                for qt, kt in tiles_of(query_max, key_max, query_tile):
                    if qt == 0 and kt > 0:
                        cols = slice(kt * key_tile, (kt + 1) * key_tile)
                        dkv_acc[g, cols, :] = jnp.zeros((key_tile, 2 * size), f32)
                    pl.when((qt * query_tile < query_count) & (kt * key_tile < key_count))(
                        lambda: attend(g, qt, kt)
                    )

        def halves(g, cols):
            scaled = dkv_acc[g, cols, :size] * scale
            return jnp.concatenate([scaled, dkv_acc[g, cols, size:]], axis=1).astype(bf16)

        for g in range(batch):
            spans = plans[g][1]
            chosen = scatter_matrix(0, query_tile, spans[:head_count], window)
            dq_back[g] = dot(chosen, (dq_acc[g, :query_tile, :] * scale).astype(bf16))
            chosen = scatter_matrix(0, key_tile, spans, window)
            dkv_back[g] = dot(chosen, halves(g, slice(0, key_tile)))
        for g in range(batch):
            spans = plans[g][1]
            for qt in range(1, query_max // query_tile):

                @pl.when(qt * query_tile < count[owner_of[g]])
                def _():
                    chosen = scatter_matrix(qt * query_tile, query_tile, spans[:head_count], window)
                    rows = slice(qt * query_tile, (qt + 1) * query_tile)
                    dq_back[g] = dq_back[g] + dot(chosen, (dq_acc[g, rows, :] * scale).astype(bf16))

            for kt in range(1, key_max // key_tile):

                @pl.when(kt * key_tile < count[owners + owner_of[g]])
                def _():
                    chosen = scatter_matrix(kt * key_tile, key_tile, spans, window)
                    cols = slice(kt * key_tile, (kt + 1) * key_tile)
                    dkv_back[g] = dkv_back[g] + dot(chosen, halves(g, cols))

        for g in range(batch):
            for i in range(loaders):
                spot = pl.ds(plans[g][0][i], window)
                part = slice(i * window, (i + 1) * window)
                if i < head_count:
                    dq_ref[i, spot, :] = dq_ref[i, spot, :] + dq_back[g, part, :].astype(bf16)
                dkv_ref[i, spot, :] = dkv_ref[i, spot, :] + dkv_back[g, part, :].astype(bf16)

    out_shape = [
        shaped((head_count, tokens, size), bf16),
        shaped((loaders, tokens, 2 * size), bf16),
        shaped((buckets, 8, 128), f32),
    ]
    by_owner = lambda o, *_: (o, 0, 0)
    return pl.pallas_call(
        body,
        grid_spec=pltpu.PrefetchScalarGridSpec(
            num_scalar_prefetch=2,
            grid=(owners // batch,),
            in_specs=[
                pl.BlockSpec((batch, 1, spots), by_owner),
                pl.BlockSpec((batch, query_max, key_max), by_owner),
                pl.BlockSpec((batch, 1, key_max), by_owner),
                pl.BlockSpec((batch, query_max, size), by_owner),
                pl.BlockSpec((batch, key_max, 2 * size), by_owner),
            ]
            + [vmem_spec(x.shape) for x in grads],
            out_specs=[vmem_spec(s.shape) for s in out_shape],
            scratch_shapes=[
                pltpu.VMEM((batch, near, size), bf16),
                pltpu.VMEM((batch, query_max, size), bf16),
                pltpu.VMEM((batch, query_max, size), f32),
                pltpu.VMEM((batch, key_max, 2 * size), f32),
                pltpu.VMEM((batch, near, size), f32),
                pltpu.VMEM((batch, loaders * window, 2 * size), f32),
            ],
        ),
        out_shape=out_shape,
        compiler_params=params(1),
        name="attend_backward",
    )(plan, counts, place, bias, stamps, sorted_query, sorted_pair, *grads)


def join_rows(queries, own, arrived):
    head_count, tokens, size = queries.shape

    def body(q_ref, own_ref, *refs):
        for k in range(head_count):
            total = own_ref[k].astype(f32)
            for ref in refs[: len(arrived)]:
                total = total + ref[k].astype(f32)
            out = refs[len(arrived) + k]
            out[:, : 2 * size] = total.astype(bf16)
            out[:, 2 * size :] = q_ref[k]

    pair_shape = (head_count, tokens, 2 * size)
    return pl.pallas_call(
        body,
        grid=(1,),
        in_specs=[vmem_spec(queries.shape)] + [vmem_spec(pair_shape)] * (1 + len(arrived)),
        out_specs=[vmem_spec((tokens, 3 * size))] * head_count,
        out_shape=[shaped((tokens, 3 * size), bf16)] * head_count,
        compiler_params=params(1),
        name="join_rows",
    )(queries, own, *arrived)


def weight_parts(rows_at, fresh_list, grad_list, piece, factor):
    tokens, width = fresh_list[0].shape
    sources = len(fresh_list)
    targets = rows_at.shape[0]

    def body(at, *refs):
        fresh_refs = refs[:sources]
        grad_refs = refs[sources : 2 * sources]
        outs = refs[2 * sources : 2 * sources + targets]
        (total,) = refs[2 * sources + targets :]
        for i in range(sources):
            part = dot(fresh_refs[i][...], grad_refs[i][...], ((0,), (0,)))
            total[...] = part if i == 0 else total[...] + part
        for j in range(targets):
            rows = pl.ds(pl.multiple_of(at[j] * piece, piece), piece)
            outs[j][...] = (total[rows, :] * factor).astype(bf16)

    out_shape = [shaped((piece, width), bf16)] * targets
    return pl.pallas_call(
        body,
        grid_spec=pltpu.PrefetchScalarGridSpec(
            num_scalar_prefetch=1,
            grid=(1,),
            in_specs=[vmem_spec((tokens, width))] * (2 * sources),
            out_specs=[vmem_spec((piece, width))] * targets,
            scratch_shapes=[pltpu.VMEM((width, width), f32)],
        ),
        out_shape=out_shape,
        compiler_params=params(1),
        name="weight_parts",
    )(rows_at, *fresh_list, *grad_list)


def unpack_rows(peer_head, slot_row, packs):
    head_count = len(packs)
    tokens = packs[0].shape[0]
    size = packs[0].shape[1] // 3
    width = head_count * size

    def body(peer, slot_ref, *refs):
        q_out, k_out, v_out = refs[head_count:]
        unsort = unsort_matrix(slot_ref[...])
        for k in range(head_count):
            cols = pl.ds(pl.multiple_of(peer[k] * size, size), size)
            k_out[:, cols] = dot(unsort, refs[k][:, :size]).astype(bf16)
            v_out[:, cols] = dot(unsort, refs[k][:, size : 2 * size]).astype(bf16)
            q_out[:, cols] = dot(unsort, refs[k][:, 2 * size :]).astype(bf16)

    return pl.pallas_call(
        body,
        grid_spec=pltpu.PrefetchScalarGridSpec(
            num_scalar_prefetch=1,
            grid=(1,),
            in_specs=[vmem_spec(slot_row.shape)] + [vmem_spec(x.shape) for x in packs],
            out_specs=[vmem_spec((tokens, width))] * 3,
        ),
        out_shape=[shaped((tokens, width), bf16)] * 3,
        compiler_params=params(1),
        name="unpack_rows",
    )(peer_head, slot_row, *packs)


def on_device(
    query_rows,
    key_rows,
    value_rows,
    gate_values,
    out_grad,
    out_weight,
    time_bias,
    route_slot,
    history_id,
    event_time,
):
    ranks = lax.axis_size("ctx")
    tokens, width = query_rows.shape
    buckets, head_count = time_bias.shape
    slot_count = 2 * tokens
    capacity = slot_count // ranks
    siblings = ranks // head_count
    window = (capacity + 30) // 16 * 16
    query_max = head_count * capacity
    piece = width // ranks
    grad_scale = (tokens * ranks) ** (-0.5)
    me = lax.axis_index("ctx")
    head = me // siblings
    sibling = me % siblings
    peer_head = head ^ jnp.arange(head_count, dtype=i32)
    slot_row = route_slot.reshape(1, tokens)
    far_first = sorted(range(1, head_count), reverse=True)

    def flip(array, mask):
        return lax.ppermute(array, "ctx", [(i, i ^ mask) for i in range(ranks)])

    def exchange(parts):
        got = {k: flip(parts[k], k * siblings) for k in far_first}
        return [parts[0]] + [got[k] for k in range(1, head_count)]

    packs = pack_rows(peer_head, slot_row, query_rows, key_rows, value_rows, head_count)

    taken = route_slot[:, None] == jnp.arange(slot_count, dtype=i32)[None, :]
    slot_meta = jnp.stack(
        [
            jnp.sum(jnp.where(taken, history_id[:, None] + 1, 0), axis=0) - 1,
            jnp.sum(jnp.where(taken, event_time[:, None], 0), axis=0),
        ]
    )[None]
    mask = siblings
    while mask < ranks:
        slot_meta = jnp.concatenate([slot_meta, flip(slot_meta, mask)], axis=0)
        mask *= 2
    mask = 1
    while mask < siblings:
        slot_meta = jnp.concatenate([slot_meta, flip(slot_meta, mask)], axis=0)
        mask *= 2

    packs = exchange(packs)
    mask = 1
    while mask < siblings:
        packs = packs + [flip(x, mask) for x in packs]
        mask *= 2

    def by_owner(table):
        return jnp.transpose(table.reshape(ranks, ranks, capacity), (1, 0, 2))

    hist_slots = by_owner(slot_meta[:, 0])
    time_slots = by_owner(slot_meta[:, 1])
    present = (hist_slots >= 0).astype(i32)
    each = jnp.sum(present, axis=2)
    before = jnp.arange(ranks)[:, None] < jnp.arange(ranks)[None, :]
    first = jnp.sum(jnp.where(before[:, :, None], each[:, None, :], 0), axis=0)
    base = jnp.sum(jnp.where(before[None], each[:, :, None], 0), axis=1)
    start = jnp.minimum(first // 16 * 16, tokens - window)
    offset = first - start
    step = jnp.arange(window, dtype=i32)[None, None]
    inside = (step >= offset[..., None]) & (step < (offset + each)[..., None])
    place = jnp.where(inside, step + (base - offset)[..., None], -1)
    place = place.reshape(ranks, 1, ranks * window)
    earlier = jnp.arange(capacity)[:, None] < jnp.arange(capacity)[None, :]
    within = jnp.sum(jnp.where(earlier[None, None], present[..., None], 0), axis=2)
    compact = jnp.where(present > 0, within + base[..., None], -1).reshape(ranks, slot_count)
    match = compact[:, :, None] == jnp.arange(slot_count, dtype=i32)[None, None, :]
    flat_hist = hist_slots.reshape(ranks, slot_count)[:, :, None]
    flat_time = time_slots.reshape(ranks, slot_count)[:, :, None]
    history = (jnp.sum(jnp.where(match, flat_hist + 1, 0), axis=1) - 1)[:, None, :]
    stamps = jnp.sum(jnp.where(match, flat_time, 0), axis=1)[:, None, :]
    counts = jnp.concatenate([jnp.sum(each[:, :head_count], axis=1), jnp.sum(each, axis=1)])
    plan = jnp.stack([start, offset, offset + each, base - offset]).reshape(-1)

    head_bias = lax.dynamic_index_in_dim(time_bias, head, axis=1, keepdims=False)
    bias = bias_tiles(head_bias, counts, history, stamps, query_max)
    fresh_grad = lax.dot_general(
        out_grad, out_weight, (((1,), (1,)), ((), ())), preferred_element_type=f32
    ).astype(bf16)

    mixed, sorted_query, sorted_pair = attend_forward(
        plan, counts, place, bias, packs, window, head_count
    )
    out_grads = [out_grad] + [flip(out_grad, m) for m in range(1, siblings)]
    fresh, gate_grad, grad_parts = norm_gate(
        peer_head, slot_row, gate_values, fresh_grad, exchange(mixed)
    )
    freshes = [fresh] + [flip(fresh, m) for m in range(1, siblings)]
    grads = exchange(grad_parts)
    layer_out = jnp.dot(fresh, out_weight, preferred_element_type=f32).astype(bf16)
    weight_sent = weight_parts(
        peer_head * siblings + sibling, freshes, out_grads, piece, grad_scale
    )

    query_back, pair_back, sums = attend_backward(
        plan,
        counts,
        place,
        bias,
        stamps,
        sorted_query,
        sorted_pair,
        grads,
        window,
        ranks,
        buckets,
    )
    weight_grad = sum(x.astype(f32) for x in exchange(weight_sent))
    other = [
        flip(pair_back[m * head_count : (m + 1) * head_count], m) for m in range(1, siblings)
    ]
    homes = exchange(join_rows(query_back, pair_back[:head_count], other))
    query_grad, key_grad, value_grad = unpack_rows(peer_head, slot_row, homes)

    above = jnp.sum(sums, axis=(1, 2))
    head_part = above - jnp.concatenate([above[1:], jnp.zeros((1,), f32)])
    bias_grad = jnp.where(
        jnp.arange(head_count)[None, :] == head, head_part[:, None] * grad_scale, 0.0
    )
    mask = 1
    while mask < ranks:
        bias_grad = bias_grad + flip(bias_grad, mask)
        mask *= 2
    return (layer_out, query_grad, key_grad, value_grad, gate_grad, weight_grad, bias_grad)


def solution(mesh):
    rows = P(("groups", "ctx"), None)
    flat = P(("groups", "ctx"))
    in_specs = (rows, rows, rows, rows, rows, P(), P(), flat, flat, flat)
    out_specs = (rows, rows, rows, rows, rows, rows, P("groups", None))
    return jax.shard_map(
        on_device, mesh=mesh, in_specs=in_specs, out_specs=out_specs, check_vma=False
    )
```

time: 290 us -> 251 us (0.87)
  the two profiles are of different devices: /device:TPU:0 before, /device:TPU:10 now
where the time goes in v1:
time: 251 us; the launch traced here: 250 us
  Pallas kernels  73.4 us (29%)
  waiting for transfers between devices  70.1 us (28%)
  starting transfers between devices  59.8 us (24%)
  other arithmetic  23.8 us (9%)
  local copies, waits for them, and re-layouts  18.3 us (7%)
  matrix products  3.04 us (1%)
    ppermute x54, waiting for transfers between devices, flip(): return lax.ppermute(array, 'ctx', [(i, i ^ mask) for i in range(ranks)])  70.1 us
    ppermute x54, starting transfers between devices, flip(): return lax.ppermute(array, 'ctx', [(i, i ^ mask) for i in range(ranks)])  59.8 us
    pallas_call x1, Pallas kernels, attend_backward(): pl.pallas_call(body, grid_spec=pltpu.PrefetchScalarGridSpec(num_scalar_pr...  27.2 us
    pallas_call x1, Pallas kernels, attend_forward(): pl.pallas_call(body, grid_spec=pltpu.PrefetchScalarGridSpec(num_scalar_pr...  16.8 us
    pallas_call x1, Pallas kernels, bias_tiles(): pl.pallas_call(body, grid_spec=pltpu.PrefetchScalarGridSpec(num_scalar_pr...  9.34 us
    reduce_sum x1, other arithmetic, on_device(): stamps = jnp.sum(jnp.where(match, flat_time, 0), axis=1)[:, None, :]  5.66 us
  transfers between devices with their start and end apart: 54, of which 22 were waited for; matrix products, arithmetic and copies ran while one was open for 14% of the time, Pallas kernels for 8%

profile of v1, /device:TPU:10, one launch (start us, length us, event | category | flops | bytes accessed | tf_op | source)
XLA Modules:
  0.0 249.6 jit_solution(12810361338822567049)
XLA Ops:
  4.5 3.8 %pack_rows.1 = (bf16[256,384]{1,0:T(8,128)(2,1)}, bf16[256,384]{1,0:T(8,128)(2,1)}, bf16[256,384]{1,0:T(8,128)(2,1)}, bf16[256,384]{1,0:T(8,128)(2,1)}, bf16[256...) custom-call(s32[8]{0:T(128)} %iota_xor_fusion.peer, ...), custom_call_target="tpu_custom_call" | custom-call | tf_op jit(solution)/shard_map/pack_rows/pallas_call | solution.py:70
  15.6 8.2 %collective-permute-done.1 = s32[2,2,512]{2,0,1:T(2,128)S(1)} collective-permute-done((s32[2,2,512]{2,0,1:T(2,128)S(1)}, s32[2,2,512]{2,0,1:T(2,128)S(1)}, u32[]{:S(2)}, u32[]{:S(2)}) %collective-permute-start.1) | collective-permute-done | bytes 8224 | tf_op jit(solution)/shard_map/ppermute | solution.py:632
  30.5 3.6 %collective-permute-start.8 = (bf16[256,384]{1,0:T(8,128)(2,1)}, bf16[256,384]{1,0:T(8,128)(2,1)S(1)}, u32[]{:S(2)}, u32[]{:S(2)}) collective-permute-start(bf16[256,384]{1,0:T(8,128)(2,1)} %get-tuple-element.62), channel_id=1, source_target_pairs={{0,10},{1,11},{2,8},{3,9},{4,14},{5,15},{6,12},{7,13},{8,2},{9,3},... | collective-permute-start | bytes 589832 | tf_op jit(solution)/shard_map/ppermute | solution.py:632
  38.1 2.8 %select_reduce_fusion.2 = s32[16,16,32]{2,1,0:T(8,128)S(1)} fusion(s32[16,16,32]{2,1,0:T(8,128)S(1)} %get-tuple-element.115, pred[32,32]{1,0:T(8,128)(4,1)} %iota_compare_fusion.2), kind=kLoop, calls=%fused_computation.3 | loop fusion | flops 516096 | bytes 66560 | tf_op jit(solution)/shard_map/reduce_sum | solution.py:679
  45.1 5.7 %select_reduce_fusion = (s32[16,512]{1,0:T(8,128)S(1)}, s32[16,512]{1,0:T(8,128)S(1)}) fusion(s32[16,512]{1,0:T(8,128)S(1)} %broadcast_in_dim.169, s32[16,512]{1,0:T(8,128)} %eq.42, s32[16,512]{1,0:T(8,128)} %add.182), kind=kLoop, calls=%fused_computation | loop fusion | flops 20955136 | bytes 163840 | tf_op jit(solution)/shard_map/reduce_sum | solution.py:685
  62.0 9.3 %bias_tiles.1.bias_ref = f32[16,256,512]{2,1,0:T(8,128)} custom-call(f32[16]{0:T(128)} %dynamic-slice_bitcast_fusion.bias, s32[32]{0:T(128)} %pad_add_fusion.5.count, s32[16,1,512]{2,1,0:T(1,128)} %sub.88.hist_ref, s32[16,1,512]{2,1,0:T(1,128)} %broadcast_in_dim.171.time_ref), custom_call_target="tpu_custom_call" | custom-call | tf_op jit(solution)/shard_map/bias_tiles/pallas_call | solution.py:128
  73.8 3.4 %collective-permute-done.10.refs_7_ = bf16[256,384]{1,0:T(8,128)(2,1)S(1)} collective-permute-done((bf16[256,384]{1,0:T(8,128)(2,1)}, bf16[256,384]{1,0:T(8,128)(2,1)S(1)}, u32[]{:S(2)}, u32[]{:S(2)}) %collective-permute-start.10) | collective-permute-done | bytes 196640 | tf_op jit(solution)/shard_map/ppermute | solution.py:632
  80.6 16.8 %attend_forward.1 = (bf16[256,128]{1,0:T(8,128)(2,1)}, bf16[256,128]{1,0:T(8,128)(2,1)}, bf16[256,128]{1,0:T(8,128)(2,1)}, bf16[256,128]{1,0:T(8,128)(2,1)}, bf1...) custom-call(s32[1024]{0:T(1024)} %reshape.346.plan_ref, ...), custom_call_target="tpu_custom_call" | custom-call | tf_op jit(solution)/shard_map/attend_forward/pallas_call | solution.py:268
  100.9 3.9 %collective-permute-start.23 = (bf16[256,128]{1,0:T(8,128)(2,1)}, bf16[256,128]{1,0:T(8,128)(2,1)S(1)}, u32[]{:S(2)}, u32[]{:S(2)}) collective-permute-start(bf16[256,128]{1,0:T(8,128)(2,1)} %get-tuple-element.70), channel_id=1, source_target_pairs={{0,10},{1,11},{2,8},{3,9},{4,14},{5,15},{6,12},{7,13},{8,2},{9,3},... | collective-permute-start | bytes 196616 | tf_op jit(solution)/shard_map/ppermute | solution.py:632
  109.7 4.1 %collective-permute-done.24.refs_6_ = bf16[256,128]{1,0:T(8,128)(2,1)S(1)} collective-permute-done((bf16[256,128]{1,0:T(8,128)(2,1)}, bf16[256,128]{1,0:T(8,128)(2,1)S(1)}, u32[]{:S(2)}, u32[]{:S(2)}) %collective-permute-start.24) | collective-permute-done | bytes 65568 | tf_op jit(solution)/shard_map/ppermute | solution.py:632
  115.8 4.6 %norm_gate.1 = (bf16[256,1024]{1,0:T(8,128)(2,1)}, bf16[256,1024]{1,0:T(8,128)(2,1)}, bf16[256,128]{1,0:T(8,128)(2,1)}, bf16[256,128]{1,0:T(8,128)(2,1)}, bf16[2...) custom-call(s32[8]{0:T(128)} %iota_xor_fusion.peer, ...), custom_call_target="tpu_custom_call" | custom-call | tf_op jit(solution)/shard_map/norm_gate/pallas_call | solution.py:335
  121.2 2.7 %collective-permute-start.28 = (bf16[256,128]{1,0:T(8,128)(2,1)}, bf16[256,128]{1,0:T(8,128)(2,1)S(1)}, u32[]{:S(2)}, u32[]{:S(2)}) collective-permute-start(bf16[256,128]{1,0:T(8,128)(2,1)} %get-tuple-element.79), channel_id=1, source_target_pairs={{0,6},{1,7},{2,4},{3,5},{4,2},{5,3},{6,0},{7,1},{8,14},{9,15},{10,... | collective-permute-start | bytes 196616 | tf_op jit(solution)/shard_map/ppermute | solution.py:632
  124.0 3.0 %collective-permute-start.30 = (bf16[256,128]{1,0:T(8,128)(2,1)}, bf16[256,128]{1,0:T(8,128)(2,1)S(1)}, u32[]{:S(2)}, u32[]{:S(2)}) collective-permute-start(bf16[256,128]{1,0:T(8,128)(2,1)} %get-tuple-element.81), channel_id=1, source_target_pairs={{0,10},{1,11},{2,8},{3,9},{4,14},{5,15},{6,12},{7,13},{8,2},{9,3},... | collective-permute-start | bytes 196616 | tf_op jit(solution)/shard_map/ppermute | solution.py:632
  132.6 3.3 %collective-permute-done.31.refs_6_ = bf16[256,128]{1,0:T(8,128)(2,1)S(1)} collective-permute-done((bf16[256,128]{1,0:T(8,128)(2,1)}, bf16[256,128]{1,0:T(8,128)(2,1)S(1)}, u32[]{:S(2)}, u32[]{:S(2)}) %collective-permute-start.31) | collective-permute-done | bytes 65568 | tf_op jit(solution)/shard_map/ppermute | solution.py:632
  138.0 27.2 %attend_backward.1 = (bf16[8,256,128]{2,1,0:T(8,128)(2,1)}, bf16[16,256,256]{2,1,0:T(8,128)(2,1)}, f32[16,8,128]{2,1,0:T(8,128)}) custom-call(s32[1024]{0:T(1024)} %reshape.346.plan_ref, s32[32]{0:T(128)} %pad_add_fusion.5.count, s32[16,1,768]{2,1,0:T(1,128)} %and_select_fusion.place_ref, f32[16,256,512]{2,1,0:T(8,128)} %bias_tiles.1.bias_ref, ...), custom_call_target="tpu_custom_call" | custom-call | tf_op jit(solution)/shard_map/attend_backward/pallas_call | solution.py:487
  166.3 3.0 %fusion.15 = (bf16[8,256,256]{2,1,0:T(8,128)(2,1)}, bf16[8,256,256]{2,1,0:T(8,128)(2,1)}) fusion(bf16[16,256,256]{2,1,0:T(8,128)(2,1)} %get-tuple-element.85), kind=kLoop, calls=%fused_computation.65 | loop fusion | bytes 4194304 | tf_op jit(solution)/shard_map/slice | solution.py:724
  176.6 4.4 %weight_parts.1 = (bf16[64,1024]{1,0:T(8,128)(2,1)}, bf16[64,1024]{1,0:T(8,128)(2,1)}, bf16[64,1024]{1,0:T(8,128)(2,1)}, bf16[64,1024]{1,0:T(8,128)(2,1)}, bf16[...) custom-call(s32[8]{0:T(128)} %multiply_add_fusion.at, ...), custom_call_target="tpu_custom_call" | custom-call | tf_op jit(solution)/shard_map/weight_parts/pallas_call | solution.py:558
  184.6 2.7 %collective-permute-start.46 = (bf16[64,1024]{1,0:T(8,128)(2,1)}, bf16[64,1024]{1,0:T(8,128)(2,1)S(1)}, u32[]{:S(2)}, u32[]{:S(2)}) collective-permute-start(bf16[64,1024]{1,0:T(8,128)(2,1)} %get-tuple-element.102), channel_id=1, source_target_pairs={{0,8},{1,9},{2,10},{3,11},{4,12},{5,13},{6,14},{7,15},{8,0},{9,1},... | collective-permute-start | bytes 393224 | tf_op jit(solution)/shard_map/ppermute | solution.py:632
  188.2 2.9 %join_rows.1 = (bf16[256,384]{1,0:T(8,128)(2,1)}, bf16[256,384]{1,0:T(8,128)(2,1)}, bf16[256,384]{1,0:T(8,128)(2,1)}, bf16[256,384]{1,0:T(8,128)(2,1)}, bf16[256...) custom-call(bf16[8,256,128]{2,1,0:T(8,128)(2,1)} %get-tuple-element.84.q_ref, ...), custom_call_target="tpu_custom_call" | custom-call | tf_op jit(solution)/shard_map/join_rows/pallas_call | solution.py:529
  205.7 3.9 %collective-permute-start.36 = (bf16[256,384]{1,0:T(8,128)(2,1)}, bf16[256,384]{1,0:T(8,128)(2,1)S(1)}, u32[]{:S(2)}, u32[]{:S(2)}) collective-permute-start(bf16[256,384]{1,0:T(8,128)(2,1)} %get-tuple-element.89), channel_id=1, source_target_pairs={{0,6},{1,7},{2,4},{3,5},{4,2},{5,3},{6,0},{7,1},{8,14},{9,15},{10,... | collective-permute-start | bytes 589832 | tf_op jit(solution)/shard_map/ppermute | solution.py:632
  210.0 13.8 %collective-permute-done.49 = bf16[64,1024]{1,0:T(8,128)(2,1)S(1)} collective-permute-done((bf16[64,1024]{1,0:T(8,128)(2,1)}, bf16[64,1024]{1,0:T(8,128)(2,1)S(1)}, u32[]{:S(2)}, u32[]{:S(2)}) %collective-permute-start.49) | collective-permute-done | bytes 131104 | tf_op jit(solution)/shard_map/ppermute | solution.py:632
  227.3 9.3 %collective-permute-done.38.refs_5_ = bf16[256,384]{1,0:T(8,128)(2,1)S(1)} collective-permute-done((bf16[256,384]{1,0:T(8,128)(2,1)}, bf16[256,384]{1,0:T(8,128)(2,1)S(1)}, u32[]{:S(2)}, u32[]{:S(2)}) %collective-permute-start.38) | collective-permute-done | bytes 196640 | tf_op jit(solution)/shard_map/ppermute | solution.py:632
  236.6 5.5 %collective-permute-done.39.refs_6_ = bf16[256,384]{1,0:T(8,128)(2,1)S(1)} collective-permute-done((bf16[256,384]{1,0:T(8,128)(2,1)}, bf16[256,384]{1,0:T(8,128)(2,1)S(1)}, u32[]{:S(2)}, u32[]{:S(2)}) %collective-permute-start.39) | collective-permute-done | bytes 196640 | tf_op jit(solution)/shard_map/ppermute | solution.py:632
  245.2 4.3 %unpack_rows.1 = (bf16[256,1024]{1,0:T(8,128)(2,1)}, bf16[256,1024]{1,0:T(8,128)(2,1)}, bf16[256,1024]{1,0:T(8,128)(2,1)}) custom-call(s32[8]{0:T(128)} %iota_xor_fusion.peer, s32[1,256]{1,0:T(1,128)} %bitcast.54, bf16[256,384]{1,0:T(8,128)(2,1)} %get-tuple-element.86.refs_0_, bf16[256,384]{1,0:T(8,128)(2,1)} %copy-done.5, bf16[256,384]{1,0:T(8,128)(2,1)} %copy-done.6, ...), custom_call_target="tpu_custom_call" | custom-call | tf_op jit(solution)/shard_map/unpack_rows/pallas_call | solution.py:588
  (251 shorter events, 96.1 us)
Async XLA Ops:
  8.3 49.0 %collective-permute-start.4 = (bf16[256,384]{1,0:T(8,128)(2,1)}, bf16[256,384]{1,0:T(8,128)(2,1)S(1)}, u32[]{:S(2)}, u32[]{:S(2)}) collective-permute-start(bf16[256,384]{1,0:T(8,128)(2,1)} %get-tuple-element.58), channel_id=1, source_target_pairs={{0,2},{1,3},{2,0},{3,1},{4,6},{5,7},{6,4},{7,5},{8,10},{9,11},{10,... | collective-permute-start | bytes 589832 | tf_op jit(solution)/shard_map/ppermute | solution.py:632
  8.8 48.5 %collective-permute-start.5 = (bf16[256,384]{1,0:T(8,128)(2,1)}, bf16[256,384]{1,0:T(8,128)(2,1)S(1)}, u32[]{:S(2)}, u32[]{:S(2)}) collective-permute-start(bf16[256,384]{1,0:T(8,128)(2,1)} %get-tuple-element.59), channel_id=1, source_target_pairs={{0,4},{1,5},{2,6},{3,7},{4,0},{5,1},{6,2},{7,3},{8,12},{9,13},{10,... | collective-permute-start | bytes 589832 | tf_op jit(solution)/shard_map/ppermute | solution.py:632
  9.3 50.1 %collective-permute-start.6 = (bf16[256,384]{1,0:T(8,128)(2,1)}, bf16[256,384]{1,0:T(8,128)(2,1)S(1)}, u32[]{:S(2)}, u32[]{:S(2)}) collective-permute-start(bf16[256,384]{1,0:T(8,128)(2,1)} %get-tuple-element.60), channel_id=1, source_target_pairs={{0,6},{1,7},{2,4},{3,5},{4,2},{5,3},{6,0},{7,1},{8,14},{9,15},{10,... | collective-permute-start | bytes 589832 | tf_op jit(solution)/shard_map/ppermute | solution.py:632
  11.8 47.6 %collective-permute-start.7 = (bf16[256,384]{1,0:T(8,128)(2,1)}, bf16[256,384]{1,0:T(8,128)(2,1)S(1)}, u32[]{:S(2)}, u32[]{:S(2)}) collective-permute-start(bf16[256,384]{1,0:T(8,128)(2,1)} %get-tuple-element.61), channel_id=1, source_target_pairs={{0,8},{1,9},{2,10},{3,11},{4,12},{5,13},{6,14},{7,15},{8,0},{9,1},... | collective-permute-start | bytes 589832 | tf_op jit(solution)/shard_map/ppermute | solution.py:632
  30.5 29.4 %collective-permute-start.8 = (bf16[256,384]{1,0:T(8,128)(2,1)}, bf16[256,384]{1,0:T(8,128)(2,1)S(1)}, u32[]{:S(2)}, u32[]{:S(2)}) collective-permute-start(bf16[256,384]{1,0:T(8,128)(2,1)} %get-tuple-element.62), channel_id=1, source_target_pairs={{0,10},{1,11},{2,8},{3,9},{4,14},{5,15},{6,12},{7,13},{8,2},{9,3},... | collective-permute-start | bytes 589832 | tf_op jit(solution)/shard_map/ppermute | solution.py:632
  57.4 16.4 %collective-permute-start.9 = (bf16[256,384]{1,0:T(8,128)(2,1)}, bf16[256,384]{1,0:T(8,128)(2,1)S(1)}, u32[]{:S(2)}, u32[]{:S(2)}) collective-permute-start(bf16[256,384]{1,0:T(8,128)(2,1)} %get-tuple-element.63), channel_id=1, source_target_pairs={{0,12},{1,13},{2,14},{3,15},{4,8},{5,9},{6,10},{7,11},{8,4},{9,5},... | collective-permute-start | bytes 589832 | tf_op jit(solution)/shard_map/ppermute | solution.py:632
  57.4 19.8 %collective-permute-start.10 = (bf16[256,384]{1,0:T(8,128)(2,1)}, bf16[256,384]{1,0:T(8,128)(2,1)S(1)}, u32[]{:S(2)}, u32[]{:S(2)}) collective-permute-start(bf16[256,384]{1,0:T(8,128)(2,1)} %get-tuple-element.64), channel_id=1, source_target_pairs={{0,14},{1,15},{2,12},{3,13},{4,10},{5,11},{6,8},{7,9},{8,6},{9,7},... | collective-permute-start | bytes 589832 | tf_op jit(solution)/shard_map/ppermute | solution.py:632
  59.4 17.8 %collective-permute-start.11 = (bf16[256,384]{1,0:T(8,128)(2,1)S(1)}, bf16[256,384]{1,0:T(8,128)(2,1)S(1)}, u32[]{:S(2)}, u32[]{:S(2)}) collective-permute-start(bf16[256,384]{1,0:T(8,128)(2,1)S(1)} %copy-done.12), channel_id=1, source_target_pairs={{0,1},{1,0},{2,3},{3,2},{4,5},{5,4},{6,7},{7,6},{8,9},{9,8},{10,11... | collective-permute-start | bytes 589832 | tf_op jit(solution)/shard_map/ppermute | solution.py:632
  59.5 18.3 %collective-permute-start.12 = (bf16[256,384]{1,0:T(8,128)(2,1)S(1)}, bf16[256,384]{1,0:T(8,128)(2,1)S(1)}, u32[]{:S(2)}, u32[]{:S(2)}) collective-permute-start(bf16[256,384]{1,0:T(8,128)(2,1)S(1)} %collective-permute-done.4.refs_1_), channel_id=1, source_target_pairs={{0,1},{1,0},{2,3},{3,2},{4,5},{5,4},{6,7},{7,6},{8,9},{9,8},{10,11... | collective-permute-start | bytes 589832 | tf_op jit(solution)/shard_map/ppermute | solution.py:632
  59.9 17.9 %collective-permute-start.13 = (bf16[256,384]{1,0:T(8,128)(2,1)S(1)}, bf16[256,384]{1,0:T(8,128)(2,1)S(1)}, u32[]{:S(2)}, u32[]{:S(2)}) collective-permute-start(bf16[256,384]{1,0:T(8,128)(2,1)S(1)} %collective-permute-done.5.refs_2_), channel_id=1, source_target_pairs={{0,1},{1,0},{2,3},{3,2},{4,5},{5,4},{6,7},{7,6},{8,9},{9,8},{10,11... | collective-permute-start | bytes 589832 | tf_op jit(solution)/shard_map/ppermute | solution.py:632
  169.4 17.9 %collective-permute-start.33 = (bf16[8,256,256]{2,1,0:T(8,128)(2,1)}, bf16[8,256,256]{2,1,0:T(8,128)(2,1)S(1)}, u32[]{:S(2)}, u32[]{:S(2)}) collective-permute-start(bf16[8,256,256]{2,1,0:T(8,128)(2,1)} %get-tuple-element.113), channel_id=1, source_target_pairs={{0,1},{1,0},{2,3},{3,2},{4,5},{5,4},{6,7},{7,6},{8,9},{9,8},{10,11... | collective-permute-start | bytes 3145736 | tf_op jit(solution)/shard_map/ppermute | solution.py:632
  181.1 14.8 %collective-permute-start.43 = (bf16[64,1024]{1,0:T(8,128)(2,1)}, bf16[64,1024]{1,0:T(8,128)(2,1)S(1)}, u32[]{:S(2)}, u32[]{:S(2)}) collective-permute-start(bf16[64,1024]{1,0:T(8,128)(2,1)} %get-tuple-element.99), channel_id=1, source_target_pairs={{0,2},{1,3},{2,0},{3,1},{4,6},{5,7},{6,4},{7,5},{8,10},{9,11},{10,... | collective-permute-start | bytes 393224 | tf_op jit(solution)/shard_map/ppermute | solution.py:632
  182.1 14.7 %collective-permute-start.44 = (bf16[64,1024]{1,0:T(8,128)(2,1)}, bf16[64,1024]{1,0:T(8,128)(2,1)S(1)}, u32[]{:S(2)}, u32[]{:S(2)}) collective-permute-start(bf16[64,1024]{1,0:T(8,128)(2,1)} %get-tuple-element.100), channel_id=1, source_target_pairs={{0,4},{1,5},{2,6},{3,7},{4,0},{5,1},{6,2},{7,3},{8,12},{9,13},{10,... | collective-permute-start | bytes 393224 | tf_op jit(solution)/shard_map/ppermute | solution.py:632
  184.1 14.4 %collective-permute-start.45 = (bf16[64,1024]{1,0:T(8,128)(2,1)}, bf16[64,1024]{1,0:T(8,128)(2,1)S(1)}, u32[]{:S(2)}, u32[]{:S(2)}) collective-permute-start(bf16[64,1024]{1,0:T(8,128)(2,1)} %get-tuple-element.101), channel_id=1, source_target_pairs={{0,6},{1,7},{2,4},{3,5},{4,2},{5,3},{6,0},{7,1},{8,14},{9,15},{10,... | collective-permute-start | bytes 393224 | tf_op jit(solution)/shard_map/ppermute | solution.py:632
  184.6 14.8 %collective-permute-start.46 = (bf16[64,1024]{1,0:T(8,128)(2,1)}, bf16[64,1024]{1,0:T(8,128)(2,1)S(1)}, u32[]{:S(2)}, u32[]{:S(2)}) collective-permute-start(bf16[64,1024]{1,0:T(8,128)(2,1)} %get-tuple-element.102), channel_id=1, source_target_pairs={{0,8},{1,9},{2,10},{3,11},{4,12},{5,13},{6,14},{7,15},{8,0},{9,1},... | collective-permute-start | bytes 393224 | tf_op jit(solution)/shard_map/ppermute | solution.py:632
  195.9 14.2 %collective-permute-start.48 = (bf16[64,1024]{1,0:T(8,128)(2,1)}, bf16[64,1024]{1,0:T(8,128)(2,1)S(1)}, u32[]{:S(2)}, u32[]{:S(2)}) collective-permute-start(bf16[64,1024]{1,0:T(8,128)(2,1)} %get-tuple-element.104), channel_id=1, source_target_pairs={{0,12},{1,13},{2,14},{3,15},{4,8},{5,9},{6,10},{7,11},{8,4},{9,5},... | collective-permute-start | bytes 393224 | tf_op jit(solution)/shard_map/ppermute | solution.py:632
  196.8 27.1 %collective-permute-start.49 = (bf16[64,1024]{1,0:T(8,128)(2,1)}, bf16[64,1024]{1,0:T(8,128)(2,1)S(1)}, u32[]{:S(2)}, u32[]{:S(2)}) collective-permute-start(bf16[64,1024]{1,0:T(8,128)(2,1)} %get-tuple-element.105), channel_id=1, source_target_pairs={{0,14},{1,15},{2,12},{3,13},{4,10},{5,11},{6,8},{7,9},{8,6},{9,7},... | collective-permute-start | bytes 393224 | tf_op jit(solution)/shard_map/ppermute | solution.py:632
  198.4 25.4 %collective-permute-start.34 = (bf16[256,384]{1,0:T(8,128)(2,1)}, bf16[256,384]{1,0:T(8,128)(2,1)S(1)}, u32[]{:S(2)}, u32[]{:S(2)}) collective-permute-start(bf16[256,384]{1,0:T(8,128)(2,1)} %get-tuple-element.87), channel_id=1, source_target_pairs={{0,2},{1,3},{2,0},{3,1},{4,6},{5,7},{6,4},{7,5},{8,10},{9,11},{10,... | collective-permute-start | bytes 589832 | tf_op jit(solution)/shard_map/ppermute | solution.py:632
  199.4 25.8 %collective-permute-start.35 = (bf16[256,384]{1,0:T(8,128)(2,1)}, bf16[256,384]{1,0:T(8,128)(2,1)S(1)}, u32[]{:S(2)}, u32[]{:S(2)}) collective-permute-start(bf16[256,384]{1,0:T(8,128)(2,1)} %get-tuple-element.88), channel_id=1, source_target_pairs={{0,4},{1,5},{2,6},{3,7},{4,0},{5,1},{6,2},{7,3},{8,12},{9,13},{10,... | collective-permute-start | bytes 589832 | tf_op jit(solution)/shard_map/ppermute | solution.py:632
  205.7 21.6 %collective-permute-start.36 = (bf16[256,384]{1,0:T(8,128)(2,1)}, bf16[256,384]{1,0:T(8,128)(2,1)S(1)}, u32[]{:S(2)}, u32[]{:S(2)}) collective-permute-start(bf16[256,384]{1,0:T(8,128)(2,1)} %get-tuple-element.89), channel_id=1, source_target_pairs={{0,6},{1,7},{2,4},{3,5},{4,2},{5,3},{6,0},{7,1},{8,14},{9,15},{10,... | collective-permute-start | bytes 589832 | tf_op jit(solution)/shard_map/ppermute | solution.py:632
  210.0 17.2 %collective-permute-start.37 = (bf16[256,384]{1,0:T(8,128)(2,1)}, bf16[256,384]{1,0:T(8,128)(2,1)S(1)}, u32[]{:S(2)}, u32[]{:S(2)}) collective-permute-start(bf16[256,384]{1,0:T(8,128)(2,1)} %get-tuple-element.90), channel_id=1, source_target_pairs={{0,8},{1,9},{2,10},{3,11},{4,12},{5,13},{6,14},{7,15},{8,0},{9,1},... | collective-permute-start | bytes 589832 | tf_op jit(solution)/shard_map/ppermute | solution.py:632
  223.9 12.7 %collective-permute-start.38 = (bf16[256,384]{1,0:T(8,128)(2,1)}, bf16[256,384]{1,0:T(8,128)(2,1)S(1)}, u32[]{:S(2)}, u32[]{:S(2)}) collective-permute-start(bf16[256,384]{1,0:T(8,128)(2,1)} %get-tuple-element.91), channel_id=1, source_target_pairs={{0,10},{1,11},{2,8},{3,9},{4,14},{5,15},{6,12},{7,13},{8,2},{9,3},... | collective-permute-start | bytes 589832 | tf_op jit(solution)/shard_map/ppermute | solution.py:632
  223.9 18.2 %collective-permute-start.39 = (bf16[256,384]{1,0:T(8,128)(2,1)}, bf16[256,384]{1,0:T(8,128)(2,1)S(1)}, u32[]{:S(2)}, u32[]{:S(2)}) collective-permute-start(bf16[256,384]{1,0:T(8,128)(2,1)} %get-tuple-element.92), channel_id=1, source_target_pairs={{0,12},{1,13},{2,14},{3,15},{4,8},{5,9},{6,10},{7,11},{8,4},{9,5},... | collective-permute-start | bytes 589832 | tf_op jit(solution)/shard_map/ppermute | solution.py:632
  225.1 19.4 %collective-permute-start.40 = (bf16[256,384]{1,0:T(8,128)(2,1)}, bf16[256,384]{1,0:T(8,128)(2,1)S(1)}, u32[]{:S(2)}, u32[]{:S(2)}) collective-permute-start(bf16[256,384]{1,0:T(8,128)(2,1)} %get-tuple-element.93), channel_id=1, source_target_pairs={{0,14},{1,15},{2,12},{3,13},{4,10},{5,11},{6,8},{7,9},{8,6},{9,7},... | collective-permute-start | bytes 589832 | tf_op jit(solution)/shard_map/ppermute | solution.py:632
  (75 other events, 761.6 us)

commit v2 on v1

v2 whole, which is shorter than its diff:
```python
import jax
import jax.numpy as jnp
from jax import lax
from jax.experimental import pallas as pl
from jax.experimental.pallas import tpu as pltpu
from jax.sharding import PartitionSpec as P

norm_epsilon = 1e-05
masked_score = -1e30
key_tile = 256
bf16 = jnp.bfloat16
f32 = jnp.float32
i32 = jnp.int32


def whole(ndim):
    return lambda *_: (0,) * ndim


def vmem_spec(shape):
    return pl.BlockSpec(tuple(shape), whole(len(shape)))


def shaped(shape, dtype):
    return jax.ShapeDtypeStruct(tuple(shape), dtype)


def dot(a, b, dims=((1,), (0,))):
    return lax.dot_general(a, b, (dims, ((), ())), preferred_element_type=f32)


def params(steps=0):
    semantics = ("arbitrary",) * steps if steps else None
    return pltpu.CompilerParams(dimension_semantics=semantics, vmem_limit_bytes=56 << 20)


def slot_ranks(slot_row):
    count = slot_row.shape[1]
    down = lax.broadcasted_iota(i32, (count, count), 0)
    across = lax.broadcasted_iota(i32, (count, count), 1)
    slot_col = jnp.sum(jnp.where(down == across, slot_row, 0), axis=1, keepdims=True)
    return slot_col, down, across


def sort_matrix(slot_row):
    slot_col, down, _ = slot_ranks(slot_row)
    rank_row = jnp.sum((slot_col < slot_row).astype(i32), axis=0, keepdims=True)
    return jnp.where(down == rank_row, 1.0, 0.0).astype(bf16)


def unsort_matrix(slot_row):
    slot_col, _, across = slot_ranks(slot_row)
    rank_col = jnp.sum((slot_row < slot_col).astype(i32), axis=1, keepdims=True)
    return jnp.where(across == rank_col, 1.0, 0.0).astype(bf16)


def pack_rows(slot_row, query_rows, key_rows, value_rows, head_count):
    tokens, width = query_rows.shape
    size = width // head_count

    def body(slot_ref, q_ref, k_ref, v_ref, out_ref):
        order = sort_matrix(slot_ref[...])
        for h in range(head_count):
            cols = slice(h * size, (h + 1) * size)
            out_ref[h, :, :size] = dot(order, k_ref[:, cols]).astype(bf16)
            out_ref[h, :, size : 2 * size] = dot(order, v_ref[:, cols]).astype(bf16)
            out_ref[h, :, 2 * size :] = dot(order, q_ref[:, cols]).astype(bf16)

    return pl.pallas_call(
        body,
        out_shape=shaped((head_count, tokens, 3 * size), bf16),
        compiler_params=params(),
        name="pack_rows",
    )(slot_row, query_rows, key_rows, value_rows)


def batch_of(owners):
    return 4 if owners % 4 == 0 else 1


def tiles_of(query_max, key_max, query_tile):
    return [
        (qt, kt) for qt in range(query_max // query_tile) for kt in range(key_max // key_tile)
    ][1:]


def make_plan(head_bias, slot_meta, capacity, window, near_loaders):
    loaders, _, slot_count = slot_meta.shape
    owners = slot_count // capacity
    tokens = slot_count // 2
    buckets = head_bias.shape[0]
    query_max = near_loaders * capacity
    key_max = slot_count
    query_tile = min(128, query_max)
    spots = loaders * window
    batch = batch_of(owners)
    stamp_span = 2 ** (buckets - 1)
    nobody = 2**20 * stamp_span // 2**15
    shift = capacity.bit_length() - 1

    def owner_mask(shape, row_owner, test):
        column = lax.shift_right_logical(lax.broadcasted_iota(i32, shape, 1), shift)
        row = lax.broadcasted_iota(i32, shape, 0)
        if not row_owner:
            row = lax.shift_right_logical(row, shift)
        return test(row, column)

    def ones(mask):
        return jnp.where(mask, 1.0, 0.0).astype(bf16)

    def body(bias, meta_ref, plan_ref, place_ref, code_ref, out_ref, spot_col, code_col):
        @pl.when(pl.program_id(0) == 0)
        def _():
            hist = meta_ref[:, 0, :]
            here = ones(hist >= 0)
            shape = (owners, slot_count)
            last = ((1,), (1,))
            each = dot(ones(owner_mask(shape, True, lambda r, c: r == c)), here, last)
            first = dot(ones(owner_mask(shape, True, lambda r, c: c < r)), here, last)
            down = lax.broadcasted_iota(i32, (loaders, loaders), 0)
            across = lax.broadcasted_iota(i32, (loaders, loaders), 1)
            base = dot(each.astype(bf16), ones(down < across))
            each, first, base = each.astype(i32), first.astype(i32), base.astype(i32)
            start = jnp.minimum(first // 16 * 16, tokens - window)
            low = first - start
            near = lax.broadcasted_iota(i32, (owners, loaders), 1) < near_loaders
            totals = [
                jnp.sum(jnp.where(near, each, 0), axis=1, keepdims=True),
                jnp.sum(each, axis=1, keepdims=True),
            ]
            fields = [start, low, low + each, base - low]
            fields += [jnp.broadcast_to(x, (owners, loaders)) for x in totals]
            for i, field in enumerate(fields):
                plan_ref[i * owners : (i + 1) * owners, :] = field
            spot = lax.broadcasted_iota(i32, (loaders, spots), 1)
            step = spot - window * lax.broadcasted_iota(i32, (loaders, spots), 0)
            spread = (step >= 0) & (step < window)
            step_row = jnp.sum(jnp.where(spread, step, 0), axis=0, keepdims=True)
            wide = jnp.where(spread, 1.0, 0.0)
            low_at, high_at, shift_at = [
                lax.dot_general(
                    x.astype(f32), wide, (((1,), (0,)), ((), ())), precision=lax.Precision.HIGHEST
                ).astype(i32)
                for x in fields[1:4]
            ]
            place = jnp.where(
                (step_row >= low_at) & (step_row < high_at), step_row + shift_at, -1
            )
            for owner in range(owners):
                place_ref[owner] = place[owner : owner + 1, :]
            square = (slot_count, slot_count)
            same = owner_mask(square, False, lambda r, c: r == c)
            sooner = lax.broadcasted_iota(i32, square, 0) < lax.broadcasted_iota(i32, square, 1)
            above = dot(ones(across < down), here).astype(bf16)
            spot_of = dot(above, ones(same)) + dot(here, ones(same & sooner))
            spot_of = jnp.where(hist >= 0, spot_of.astype(i32), -1)
            spot_col[...] = jnp.transpose(spot_of)
            code_col[...] = jnp.transpose(hist * stamp_span + meta_ref[:, 1, :] - nobody)

        eye = lax.broadcasted_iota(i32, (query_tile, query_tile), 0) == lax.broadcasted_iota(
            i32, (query_tile, query_tile), 1
        )

        def fill(g, qt, kt):
            rows = slice(qt * query_tile, (qt + 1) * query_tile)
            cols = slice(kt * key_tile, (kt + 1) * key_tile)
            column = jnp.sum(jnp.where(eye, code_ref[g, :, rows], 0), axis=1, keepdims=True)
            gap = column - code_ref[g, :, cols]
            level = jnp.full(gap.shape, bias[0], f32)
            for e in range(buckets - 1):
                level = jnp.where(gap >= 2**e, bias[e + 1], level)
            allowed = (gap >= 0) & ((column ^ code_ref[g, :, cols]) < stamp_span)
            out_ref[g, rows, cols] = jnp.where(allowed, level, masked_score)

        ids = lax.broadcasted_iota(i32, (capacity, key_max), 1)
        totals = []
        for g in range(batch):
            owner = pl.program_id(0) * batch + g
            rows = pl.ds(pl.multiple_of(owner * capacity, 8), capacity)
            spot = spot_col[rows, :]
            code = code_col[rows, :]
            found = jnp.zeros((capacity, key_max), i32)
            for i in range(loaders):
                found = found + jnp.where(spot[:, i : i + 1] == ids, code[:, i : i + 1], 0)
            held = (spot >= 0).astype(f32)
            totals.append((jnp.sum(held[:, :near_loaders]), jnp.sum(held)))
            code_ref[g] = jnp.sum(found, axis=0, keepdims=True) + nobody
        for g in range(batch):
            fill(g, 0, 0)
        for g in range(batch):
            query_count, key_count = totals[g]
            for qt, kt in tiles_of(query_max, key_max, query_tile):

                @pl.when((query_count > qt * query_tile) & (key_count > kt * key_tile))
                def _():
                    fill(g, qt, kt)

    by_owner = lambda o, *_: (o, 0, 0)
    return pl.pallas_call(
        body,
        grid_spec=pltpu.PrefetchScalarGridSpec(
            num_scalar_prefetch=1,
            grid=(owners // batch,),
            in_specs=[vmem_spec(slot_meta.shape)],
            out_specs=[
                vmem_spec((6 * owners, loaders)),
                vmem_spec((owners, 1, spots)),
                pl.BlockSpec((batch, 1, key_max), by_owner),
                pl.BlockSpec((batch, query_max, key_max), by_owner),
            ],
            scratch_shapes=[
                pltpu.VMEM((slot_count, loaders), i32),
                pltpu.VMEM((slot_count, loaders), i32),
            ],
        ),
        out_shape=[
            shaped((6 * owners, loaders), i32),
            shaped((owners, 1, spots), i32),
            shaped((owners, 1, key_max), i32),
            shaped((owners, query_max, key_max), f32),
        ],
        compiler_params=params(1),
        name="make_plan",
    )(head_bias, slot_meta)


def gather_matrix(first, count, place):
    ids = lax.broadcasted_iota(i32, (count, place.shape[1]), 0) + first
    return jnp.where(ids == place, 1.0, 0.0).astype(bf16)


def scatter_matrix(first, count, spans, window):
    step = lax.broadcasted_iota(i32, (window, 128), 0)
    reach = lax.broadcasted_iota(i32, (window, 128), 1) - step + first
    stack = []
    for low, high, shift in spans:
        inside = (step >= low) & (step < high)
        lanes = [
            jnp.where(inside & (reach == shift - lane), 1.0, 0.0) for lane in range(0, count, 128)
        ]
        stack.append(jnp.concatenate(lanes, axis=1)[:, :count])
    return jnp.concatenate(stack, axis=0).astype(bf16)


def gate_of(score):
    return 1.0 / (1.0 + jnp.exp(-jnp.maximum(score, -87.0)))


def read_plan(plan, owner, owners, loaders):
    at = lambda field, i: plan[field * owners + owner, i]
    begin = [pl.multiple_of(at(0, i), 16) for i in range(loaders)]
    spans = [(at(1, i), at(2, i), at(3, i)) for i in range(loaders)]
    return begin, spans


def attend_forward(plan, place, bias, packs, window, head_count):
    owners, _, spots = place.shape
    loaders = len(packs) * head_count
    tokens = packs[0].shape[1]
    size = packs[0].shape[2] // 3
    query_max, key_max = bias.shape[1:]
    query_tile = min(128, query_max)
    scale = size ** (-0.5)
    near = head_count * window
    batch = batch_of(owners)

    def body(plan_ref, place_ref, bias_ref, *refs):
        pack_refs = refs[: len(packs)]
        mixed_ref, qs_ref, kvs_ref, q_win, kv_win, acc, back = refs[len(packs) :]

        @pl.when(pl.program_id(0) == 0)
        def _():
            mixed_ref[...] = jnp.zeros(mixed_ref.shape, mixed_ref.dtype)

        def attend(g, qt, kt):
            rows = slice(qt * query_tile, (qt + 1) * query_tile)
            cols = slice(kt * key_tile, (kt + 1) * key_tile)
            score = (
                dot(qs_ref[g, rows, :], kvs_ref[g, cols, :size], ((1,), (1,))) * scale
                + bias_ref[g, rows, cols]
            )
            weight = jnp.where(
                score > 0.1 * masked_score, score * gate_of(score), 0.0
            ).astype(bf16)
            part = dot(weight, kvs_ref[g, cols, size:])
            acc[g, rows, :] = part if kt == 0 else acc[g, rows, :] + part

        def load_keys(g, kt):
            chosen = gather_matrix(kt * key_tile, key_tile, place_ref[g])
            kvs_ref[g, kt * key_tile : (kt + 1) * key_tile, :] = dot(chosen, kv_win[g]).astype(bf16)

        def load_queries(g, qt):
            chosen = gather_matrix(qt * query_tile, query_tile, place_ref[g, :, :near])
            qs_ref[g, qt * query_tile : (qt + 1) * query_tile, :] = dot(chosen, q_win[g]).astype(bf16)

        owner_of = [pl.program_id(0) * batch + g for g in range(batch)]
        plans = [read_plan(plan_ref, owner, owners, loaders) for owner in owner_of]
        for g in range(batch):
            begin = plans[g][0]
            for i in range(loaders):
                spot = slice(i * window, (i + 1) * window)
                source, h = pack_refs[i // head_count], i % head_count
                kv_win[g, spot, :] = source[h, pl.ds(begin[i], window), : 2 * size]
                if i < head_count:
                    q_win[g, spot, :] = source[h, pl.ds(begin[i], window), 2 * size :]
        for g in range(batch):
            load_keys(g, 0)
            load_queries(g, 0)
        for g in range(batch):
            attend(g, 0, 0)
        for g in range(batch):
            query_count = plan_ref[4 * owners + owner_of[g], 0]
            key_count = plan_ref[5 * owners + owner_of[g], 0]

            @pl.when((query_count > query_tile) | (key_count > key_tile))
            def _():
                for kt in range(1, key_max // key_tile):
                    pl.when(kt * key_tile < key_count)(lambda: load_keys(g, kt))
                for qt in range(1, query_max // query_tile):
                    pl.when(qt * query_tile < query_count)(lambda: load_queries(g, qt))
                for qt, kt in tiles_of(query_max, key_max, query_tile):
                    pl.when((qt * query_tile < query_count) & (kt * key_tile < key_count))(
                        lambda: attend(g, qt, kt)
                    )

        for g in range(batch):
            chosen = scatter_matrix(0, query_tile, plans[g][1][:head_count], window)
            back[g] = dot(chosen, acc[g, :query_tile, :].astype(bf16))
        for g in range(batch):
            for qt in range(1, query_max // query_tile):

                @pl.when(qt * query_tile < plan_ref[4 * owners + owner_of[g], 0])
                def _():
                    chosen = scatter_matrix(
                        qt * query_tile, query_tile, plans[g][1][:head_count], window
                    )
                    rows = slice(qt * query_tile, (qt + 1) * query_tile)
                    back[g] = back[g] + dot(chosen, acc[g, rows, :].astype(bf16))

        for g in range(batch):
            for i in range(head_count):
                spot = pl.ds(plans[g][0][i], window)
                mixed_ref[i, spot, :] = mixed_ref[i, spot, :] + back[
                    g, i * window : (i + 1) * window, :
                ].astype(bf16)

    out_shape = [
        shaped((head_count, tokens, size), bf16),
        shaped((owners, query_max, size), bf16),
        shaped((owners, key_max, 2 * size), bf16),
    ]
    by_owner = lambda o, *_: (o, 0, 0)
    return pl.pallas_call(
        body,
        grid_spec=pltpu.PrefetchScalarGridSpec(
            num_scalar_prefetch=1,
            grid=(owners // batch,),
            in_specs=[
                pl.BlockSpec((batch, 1, spots), by_owner),
                pl.BlockSpec((batch, query_max, key_max), by_owner),
            ]
            + [vmem_spec(x.shape) for x in packs],
            out_specs=[
                vmem_spec((head_count, tokens, size)),
                pl.BlockSpec((batch, query_max, size), by_owner),
                pl.BlockSpec((batch, key_max, 2 * size), by_owner),
            ],
            scratch_shapes=[
                pltpu.VMEM((batch, near, size), bf16),
                pltpu.VMEM((batch, loaders * window, 2 * size), bf16),
                pltpu.VMEM((batch, query_max, size), f32),
                pltpu.VMEM((batch, near, size), f32),
            ],
        ),
        out_shape=out_shape,
        compiler_params=params(1),
        name="attend_forward",
    )(plan, place, bias, *packs)


def norm_gate(slot_row, gate_values, fresh_grad, mixed_parts):
    tokens, width = gate_values.shape
    head_count = mixed_parts.shape[0]
    size = width // head_count

    def body(slot_ref, gate_ref, grad_ref, parts, fresh_ref, gate_grad_ref, outs, joined, moved):
        slot = slot_ref[...]
        unsort = unsort_matrix(slot)
        for k in range(head_count):
            joined[:, k * size : (k + 1) * size] = dot(unsort, parts[k])
        mixed = joined[...]
        centered = mixed - jnp.mean(mixed, axis=1, keepdims=True)
        inverse = lax.rsqrt(jnp.mean(centered * centered, axis=1, keepdims=True) + norm_epsilon)
        normed = centered * inverse
        gate = gate_ref[...].astype(f32)
        grad = grad_ref[...].astype(f32)
        fresh_ref[...] = (normed * gate).astype(bf16)
        gate_grad_ref[...] = (grad * normed).astype(bf16)
        normed_grad = grad * gate
        moved[...] = (
            inverse
            * (
                normed_grad
                - jnp.mean(normed_grad, axis=1, keepdims=True)
                - normed * jnp.mean(normed_grad * normed, axis=1, keepdims=True)
            )
        ).astype(bf16)
        order = sort_matrix(slot)
        for k in range(head_count):
            outs[k] = dot(order, moved[:, k * size : (k + 1) * size]).astype(bf16)

    return pl.pallas_call(
        body,
        out_shape=[
            shaped((tokens, width), bf16),
            shaped((tokens, width), bf16),
            shaped((head_count, tokens, size), bf16),
        ],
        scratch_shapes=[pltpu.VMEM((tokens, width), f32), pltpu.VMEM((tokens, width), bf16)],
        compiler_params=params(),
        name="norm_gate",
    )(slot_row, gate_values, fresh_grad, mixed_parts)


def attend_backward(
    plan, place, bias, codes, sorted_query, sorted_pair, grads, window, loaders, buckets
):
    owners, _, spots = place.shape
    head_count, tokens, size = grads.shape
    query_max, key_max = bias.shape[1:]
    query_tile = min(128, query_max)
    scale = size ** (-0.5)
    near = head_count * window
    batch = batch_of(owners)

    def body(plan_ref, place_ref, bias_ref, code_ref, qs_ref, kvs_ref, grad_ref, *refs):
        dq_ref, dkv_ref, sums_ref = refs[:3]
        grad_win, grad_rows, dq_acc, dkv_acc, dq_back, dkv_back = refs[3:]

        @pl.when(pl.program_id(0) == 0)
        def _():
            for ref in (dq_ref, dkv_ref, sums_ref):
                ref[...] = jnp.zeros(ref.shape, ref.dtype)

        eye = lax.broadcasted_iota(i32, (query_tile, query_tile), 0) == lax.broadcasted_iota(
            i32, (query_tile, query_tile), 1
        )

        def load_grads(g, qt):
            chosen = gather_matrix(qt * query_tile, query_tile, place_ref[g, :, :near])
            rows = slice(qt * query_tile, (qt + 1) * query_tile)
            grad_rows[g, rows, :] = dot(chosen, grad_win[g]).astype(bf16)

        def attend(g, qt, kt):
            rows = slice(qt * query_tile, (qt + 1) * query_tile)
            cols = slice(kt * key_tile, (kt + 1) * key_tile)
            query = qs_ref[g, rows, :]
            key = kvs_ref[g, cols, :size]
            value = kvs_ref[g, cols, size:]
            grad = grad_rows[g, rows, :]
            score = dot(query, key, ((1,), (1,))) * scale + bias_ref[g, rows, cols]
            product = dot(grad, value, ((1,), (1,)))
            allowed = score > 0.1 * masked_score
            gate = gate_of(score)
            silu = score * gate
            weight = jnp.where(allowed, silu, 0.0).astype(bf16)
            score_grad = jnp.where(allowed, product * (gate + silu * (1.0 - gate)), 0.0)
            rounded = score_grad.astype(bf16)
            dv = dot(weight, grad, ((0,), (0,)))
            dk = dot(rounded, query, ((0,), (0,)))
            dq = dot(rounded, key)
            if qt == 0:
                dkv_acc[g, cols, :size] = dk
                dkv_acc[g, cols, size:] = dv
            else:
                dkv_acc[g, cols, :size] = dkv_acc[g, cols, :size] + dk
                dkv_acc[g, cols, size:] = dkv_acc[g, cols, size:] + dv
            dq_acc[g, rows, :] = dq if kt == 0 else dq_acc[g, rows, :] + dq
            time_col = jnp.sum(jnp.where(eye, code_ref[g, :, rows], 0), axis=1, keepdims=True)
            gap = time_col - code_ref[g, :, cols]
            for level in range(buckets):
                held = score_grad
                if level > 0:
                    held = jnp.where(gap >= 2 ** (level - 1), score_grad, 0.0)
                folded = jnp.sum(held.reshape(query_tile // 8, 8, key_tile), axis=0)
                sums_ref[level] = sums_ref[level] + (folded[:, :128] + folded[:, 128:])

        owner_of = [pl.program_id(0) * batch + g for g in range(batch)]
        plans = [read_plan(plan_ref, owner, owners, loaders) for owner in owner_of]
        for g in range(batch):
            for i in range(head_count):
                grad_win[g, i * window : (i + 1) * window, :] = grad_ref[
                    i, pl.ds(plans[g][0][i], window), :
                ]
        for g in range(batch):
            load_grads(g, 0)
        for g in range(batch):
            attend(g, 0, 0)
        for g in range(batch):
            query_count = plan_ref[4 * owners + owner_of[g], 0]
            key_count = plan_ref[5 * owners + owner_of[g], 0]

            @pl.when((query_count > query_tile) | (key_count > key_tile))
            def _():
                for qt in range(1, query_max // query_tile):
                    pl.when(qt * query_tile < query_count)(lambda: load_grads(g, qt))
                for qt, kt in tiles_of(query_max, key_max, query_tile):
                    if qt == 0 and kt > 0:
                        cols = slice(kt * key_tile, (kt + 1) * key_tile)
                        dkv_acc[g, cols, :] = jnp.zeros((key_tile, 2 * size), f32)
                    pl.when((qt * query_tile < query_count) & (kt * key_tile < key_count))(
                        lambda: attend(g, qt, kt)
                    )

        def halves(g, cols):
            scaled = dkv_acc[g, cols, :size] * scale
            return jnp.concatenate([scaled, dkv_acc[g, cols, size:]], axis=1).astype(bf16)

        for g in range(batch):
            spans = plans[g][1]
            chosen = scatter_matrix(0, query_tile, spans[:head_count], window)
            dq_back[g] = dot(chosen, (dq_acc[g, :query_tile, :] * scale).astype(bf16))
            chosen = scatter_matrix(0, key_tile, spans, window)
            dkv_back[g] = dot(chosen, halves(g, slice(0, key_tile)))
        for g in range(batch):
            spans = plans[g][1]
            for qt in range(1, query_max // query_tile):

                @pl.when(qt * query_tile < plan_ref[4 * owners + owner_of[g], 0])
                def _():
                    chosen = scatter_matrix(qt * query_tile, query_tile, spans[:head_count], window)
                    rows = slice(qt * query_tile, (qt + 1) * query_tile)
                    dq_back[g] = dq_back[g] + dot(chosen, (dq_acc[g, rows, :] * scale).astype(bf16))

            for kt in range(1, key_max // key_tile):

                @pl.when(kt * key_tile < plan_ref[5 * owners + owner_of[g], 0])
                def _():
                    chosen = scatter_matrix(kt * key_tile, key_tile, spans, window)
                    cols = slice(kt * key_tile, (kt + 1) * key_tile)
                    dkv_back[g] = dkv_back[g] + dot(chosen, halves(g, cols))

        for g in range(batch):
            for i in range(loaders):
                spot = pl.ds(plans[g][0][i], window)
                part = slice(i * window, (i + 1) * window)
                if i < head_count:
                    dq_ref[i, spot, :] = dq_ref[i, spot, :] + dq_back[g, part, :].astype(bf16)
                dkv_ref[i, spot, :] = dkv_ref[i, spot, :] + dkv_back[g, part, :].astype(bf16)

    out_shape = [
        shaped((head_count, tokens, size), bf16),
        shaped((loaders, tokens, 2 * size), bf16),
        shaped((buckets, 8, 128), f32),
    ]
    by_owner = lambda o, *_: (o, 0, 0)
    return pl.pallas_call(
        body,
        grid_spec=pltpu.PrefetchScalarGridSpec(
            num_scalar_prefetch=1,
            grid=(owners // batch,),
            in_specs=[
                pl.BlockSpec((batch, 1, spots), by_owner),
                pl.BlockSpec((batch, query_max, key_max), by_owner),
                pl.BlockSpec((batch, 1, key_max), by_owner),
                pl.BlockSpec((batch, query_max, size), by_owner),
                pl.BlockSpec((batch, key_max, 2 * size), by_owner),
                vmem_spec(grads.shape),
            ],
            out_specs=[vmem_spec(s.shape) for s in out_shape],
            scratch_shapes=[
                pltpu.VMEM((batch, near, size), bf16),
                pltpu.VMEM((batch, query_max, size), bf16),
                pltpu.VMEM((batch, query_max, size), f32),
                pltpu.VMEM((batch, key_max, 2 * size), f32),
                pltpu.VMEM((batch, near, size), f32),
                pltpu.VMEM((batch, loaders * window, 2 * size), f32),
            ],
        ),
        out_shape=out_shape,
        compiler_params=params(1),
        name="attend_backward",
    )(plan, place, bias, codes, sorted_query, sorted_pair, grads)


def join_rows(queries, own, arrived, head_sums):
    head_count, tokens, size = queries.shape
    pair = 2 * size

    def body(q_ref, own_ref, sum_ref, *refs):
        out_ref = refs[-1]
        rest = sum_ref[...]
        row = lax.broadcasted_iota(i32, (8, 3 * size), 0)
        extra = jnp.zeros((8, 3 * size), f32)
        for digit in range(3):
            rounded = rest.astype(bf16).astype(f32)
            rest = rest - rounded
            extra = jnp.where(row == digit, rounded, extra)
        for h in range(head_count):
            total = own_ref[h].astype(f32)
            for ref in refs[:-1]:
                total = total + ref[h].astype(f32)
            out_ref[h, :tokens, :pair] = total.astype(bf16)
            out_ref[h, :tokens, pair:] = q_ref[h]
            out_ref[h, tokens:, :] = extra.astype(bf16)

    pair_spec = vmem_spec((head_count, tokens, pair))
    return pl.pallas_call(
        body,
        grid=(1,),
        in_specs=[vmem_spec(queries.shape), pair_spec, vmem_spec(head_sums.shape)]
        + [pair_spec] * len(arrived),
        out_specs=vmem_spec((head_count, tokens + 8, 3 * size)),
        out_shape=shaped((head_count, tokens + 8, 3 * size), bf16),
        compiler_params=params(1),
        name="join_rows",
    )(queries, own, head_sums, *arrived)


def weight_parts(sibling, fresh_list, grad_list, piece, head_count, factor):
    tokens, width = fresh_list[0].shape
    sources = len(fresh_list)
    size = width // head_count

    def body(at, *refs):
        fresh_refs = refs[:sources]
        grad_refs = refs[sources : 2 * sources]
        out_ref, total = refs[2 * sources :]
        rows = pl.ds(pl.multiple_of(at[0] * piece, piece), piece)
        for h in range(head_count):
            cols = slice(h * size, (h + 1) * size)
            part = dot(fresh_refs[0][:, cols], grad_refs[0][...], ((0,), (0,)))
            for i in range(1, sources):
                part = part + dot(fresh_refs[i][:, cols], grad_refs[i][...], ((0,), (0,)))
            total[h] = part * factor
            out_ref[h] = total[h, rows, :].astype(bf16)

    return pl.pallas_call(
        body,
        grid_spec=pltpu.PrefetchScalarGridSpec(
            num_scalar_prefetch=1,
            grid=(1,),
            in_specs=[vmem_spec((tokens, width))] * (2 * sources),
            out_specs=vmem_spec((head_count, piece, width)),
            scratch_shapes=[pltpu.VMEM((head_count, size, width), f32)],
        ),
        out_shape=shaped((head_count, piece, width), bf16),
        compiler_params=params(1),
        name="weight_parts",
    )(sibling, *fresh_list, *grad_list)


def unpack_rows(slot_row, packs, buckets):
    head_count, rows, triple = packs.shape
    tokens = slot_row.shape[1]
    size = triple // 3
    width = head_count * size

    def body(slot_ref, pack_ref, q_out, k_out, v_out, bias_out):
        unsort = unsort_matrix(slot_ref[...])
        for h in range(head_count):
            cols = slice(h * size, (h + 1) * size)
            k_out[:, cols] = dot(unsort, pack_ref[h, :tokens, :size]).astype(bf16)
            v_out[:, cols] = dot(unsort, pack_ref[h, :tokens, size : 2 * size]).astype(bf16)
            q_out[:, cols] = dot(unsort, pack_ref[h, :tokens, 2 * size :]).astype(bf16)
            digits = pack_ref[h, tokens:, :128].astype(f32)
            bias_out[h : h + 1, :] = digits[0:1] + digits[1:2] + digits[2:3]

    return pl.pallas_call(
        body,
        out_shape=[shaped((tokens, width), bf16)] * 3 + [shaped((head_count, 128), f32)],
        compiler_params=params(),
        name="unpack_rows",
    )(slot_row, packs)


def on_device(
    query_rows,
    key_rows,
    value_rows,
    gate_values,
    out_grad,
    out_weight,
    time_bias,
    route_slot,
    history_id,
    event_time,
):
    ranks = lax.axis_size("ctx")
    tokens, width = query_rows.shape
    buckets, head_count = time_bias.shape
    slot_count = 2 * tokens
    capacity = slot_count // ranks
    siblings = ranks // head_count
    window = (capacity + 30) // 16 * 16
    query_max = head_count * capacity
    piece = width // ranks
    grad_scale = (tokens * ranks) ** (-0.5)
    me = lax.axis_index("ctx")
    head = me // siblings
    sibling = me % siblings
    peer_head = head ^ jnp.arange(head_count, dtype=i32)
    slot_row = route_slot.reshape(1, tokens)
    teams = [[h * siblings + b for h in range(head_count)] for b in range(siblings)]

    def flip(array, mask):
        return lax.ppermute(array, "ctx", [(i, i ^ mask) for i in range(ranks)])

    def exchange(parts):
        return lax.all_to_all(parts, "ctx", 0, 0, axis_index_groups=teams, tiled=True)

    sent = pack_rows(slot_row, query_rows, key_rows, value_rows, head_count)
    taken = route_slot[:, None] == jnp.arange(slot_count, dtype=i32)[None, :]
    slot_meta = jnp.stack(
        [
            jnp.sum(jnp.where(taken, history_id[:, None] + 1, 0), axis=0) - 1,
            jnp.sum(jnp.where(taken, event_time[:, None], 0), axis=0),
        ]
    )[None]
    mask = siblings
    while mask < ranks:
        slot_meta = jnp.concatenate([slot_meta, flip(slot_meta, mask)], axis=0)
        mask *= 2
    sent, slot_meta = lax.optimization_barrier((sent, slot_meta))
    arrived = exchange(sent)
    slot_meta = slot_meta[peer_head]
    mask = 1
    while mask < siblings:
        slot_meta = jnp.concatenate([slot_meta, flip(slot_meta, mask)], axis=0)
        mask *= 2

    head_bias = lax.dynamic_index_in_dim(time_bias, head, axis=1, keepdims=False)
    plan, place, codes, bias = make_plan(head_bias, slot_meta, capacity, window, head_count)
    arrived, plan = lax.optimization_barrier((arrived, plan))
    packs = [arrived]
    mask = 1
    while mask < siblings:
        packs = packs + [flip(x, mask) for x in packs]
        mask *= 2
    fresh_grad = lax.dot_general(
        out_grad, out_weight, (((1,), (1,)), ((), ())), preferred_element_type=f32
    ).astype(bf16)

    mixed, sorted_query, sorted_pair = attend_forward(
        plan, place, bias, packs, window, head_count
    )
    out_grads = [out_grad] + [flip(out_grad, m) for m in range(1, siblings)]
    fresh, gate_grad, grad_parts = norm_gate(slot_row, gate_values, fresh_grad, exchange(mixed))
    freshes = [fresh] + [flip(fresh, m) for m in range(1, siblings)]
    grads = exchange(grad_parts)
    layer_out = jnp.dot(fresh, out_weight, preferred_element_type=f32).astype(bf16)
    weight_sent = weight_parts(sibling[None], freshes, out_grads, piece, head_count, grad_scale)
    grads, weight_sent = lax.optimization_barrier((grads, weight_sent))
    weight_grad = jnp.sum(exchange(weight_sent).astype(f32), axis=0)

    query_back, pair_back, sums = attend_backward(
        plan, place, bias, codes, sorted_query, sorted_pair, grads, window, ranks, buckets
    )
    other = [
        flip(pair_back[m * head_count : (m + 1) * head_count], m) for m in range(1, siblings)
    ]
    above = jnp.sum(sums, axis=(1, 2))
    head_sums = (above - jnp.concatenate([above[1:], jnp.zeros((1,), f32)])) * grad_scale
    head_sums = jnp.pad(head_sums, (0, width * 3 // head_count - buckets))[None]
    mask = 1
    while mask < siblings:
        head_sums = head_sums + flip(head_sums, mask)
        mask *= 2
    joined = join_rows(query_back, pair_back[:head_count], other, head_sums)
    query_grad, key_grad, value_grad, bias_rows = unpack_rows(slot_row, exchange(joined), buckets)
    bias_grad = jnp.transpose(bias_rows[:, :buckets])
    return (layer_out, query_grad, key_grad, value_grad, gate_grad, weight_grad, bias_grad)


def solution(mesh):
    rows = P(("groups", "ctx"), None)
    flat = P(("groups", "ctx"))
    in_specs = (rows, rows, rows, rows, rows, P(), P(), flat, flat, flat)
    out_specs = (rows, rows, rows, rows, rows, rows, P("groups", None))
    return jax.shard_map(
        on_device, mesh=mesh, in_specs=in_specs, out_specs=out_specs, check_vma=False
    )
```

time: 251 us -> 211 us (0.84)
  the two profiles are of different devices: /device:TPU:10 before, /device:TPU:0 now
where the time goes in v2:
time: 211 us; the launch traced here: 212 us
  waiting for transfers between devices  85.7 us (41%)
  Pallas kernels  77.6 us (37%)
  starting transfers between devices  30.6 us (15%)
  local copies, waits for them, and re-layouts  9.02 us (4%)
  other arithmetic  4.09 us (2%)
  matrix products  4.08 us (2%)
    all_to_all x5, waiting for transfers between devices, exchange(): lax.all_to_all(parts, 'ctx', 0, 0, axis_index_groups=teams, tiled=True)  74.6 us
    pallas_call x1, Pallas kernels, attend_backward(): pl.pallas_call(body, grid_spec=pltpu.PrefetchScalarGridSpec(num_scalar_pr...  28.4 us
    all_to_all x5, starting transfers between devices, exchange(): lax.all_to_all(parts, 'ctx', 0, 0, axis_index_groups=teams, tiled=True)  21.3 us
    pallas_call x1, Pallas kernels, attend_forward(): pl.pallas_call(body, grid_spec=pltpu.PrefetchScalarGridSpec(num_scalar_pr...  17.9 us
    pallas_call x1, Pallas kernels, make_plan(): pl.pallas_call(body, grid_spec=pltpu.PrefetchScalarGridSpec(num_scalar_pr...  13 us
    ppermute x9, waiting for transfers between devices, flip(): return lax.ppermute(array, 'ctx', [(i, i ^ mask) for i in range(ranks)])  11.1 us
    ppermute x9, starting transfers between devices, flip(): return lax.ppermute(array, 'ctx', [(i, i ^ mask) for i in range(ranks)])  9.28 us
  transfers between devices with their start and end apart: 14, of which 10 were waited for; matrix products, arithmetic and copies ran while one was open for 5% of the time, Pallas kernels for 25%

profile of v2, /device:TPU:0, one launch (start us, length us, event | category | flops | bytes accessed | tf_op | source)
XLA Modules:
  0.0 211.8 jit_solution(3532768847125286756)
XLA Ops:
  2.4 3.0 %collective-permute-start = (s32[1,2,512]{2,1,0:T(2,128)S(1)}, s32[1,2,512]{2,1,0:T(2,128)S(1)}, u32[]{:S(2)}, u32[]{:S(2)}) collective-permute-start(s32[1,2,512]{2,1,0:T(2,128)S(1)} %add_bitcast_fusion), channel_id=1, source_target_pairs={{0,2},{1,3},{2,0},{3,1},{4,6},{5,7},{6,4},{7,5},{8,10},{9,11},{10,... | collective-permute-start | bytes 12296 | tf_op jit(solution)/shard_map/ppermute | solution.py:707
  7.0 2.1 collective-permute-start.1
  10.7 3.0 %collective-permute-start.2 = (s32[4,2,512]{2,1,0:T(2,128)S(1)}, s32[4,2,512]{2,1,0:T(2,128)S(1)}, u32[]{:S(2)}, u32[]{:S(2)}) collective-permute-start(s32[4,2,512]{2,1,0:T(2,128)S(1)} %pad_add_fusion.2), channel_id=1, source_target_pairs={{0,8},{1,9},{2,10},{3,11},{4,12},{5,13},{6,14},{7,15},{8,0},{9,1},... | collective-permute-start | bytes 49160 | tf_op jit(solution)/shard_map/ppermute | solution.py:707
  13.8 3.7 %pack_rows.1 = bf16[8,256,384]{2,1,0:T(8,128)(2,1)} custom-call(s32[1,256]{1,0:T(1,128)} %bitcast.16, bf16[256,1024]{1,0:T(8,128)(2,1)} %q_ref.1, bf16[256,1024]{1,0:T(8,128)(2,1)} %k_ref.1, bf16[256,1024]{1,0:T(8,128)(2,1)} %v_ref.1), custom_call_target="tpu_custom_call" | custom-call | tf_op jit(solution)/shard_map/pack_rows/pallas_call | solution.py:69
  17.5 4.3 %all-to-all-start = ((bf16[8,256,384]{2,1,0:T(8,128)(2,1)}), bf16[8,256,384]{2,1,0:T(8,128)(2,1)}, u32[]{:S(2)}, u32[]{:S(2)}) async-start(bf16[8,256,384]{2,1,0:T(8,128)(2,1)} %pack_rows.1), calls=%async_computation | async-start | bytes 3145728 | tf_op jit(solution)/shard_map/all_to_all | solution.py:710
  24.4 13.0 %make_plan.1 = (s32[96,16]{1,0:T(8,128)}, s32[16,1,768]{2,1,0:T(1,128)}, s32[16,1,512]{2,1,0:T(1,128)}, f32[16,256,512]{2,1,0:T(8,128)}) custom-call(f32[16]{0:T(128)} %dynamic-slice_bitcast_fusion.bias, s32[16,2,512]{2,1,0:T(2,128)} %pad_add_fusion.meta_ref), custom_call_target="tpu_custom_call" | custom-call | tf_op jit(solution)/shard_map/make_plan/pallas_call | solution.py:199
  37.4 19.3 %all-to-all-done.refs_0_ = bf16[8,256,384]{2,1,0:T(8,128)(2,1)} async-done(((bf16[8,256,384]{2,1,0:T(8,128)(2,1)}), bf16[8,256,384]{2,1,0:T(8,128)(2,1)}, u32[]{:S(2)}, u32[]{:S(2)}) %all-to-all-start) | async-done | bytes 1572896 | tf_op jit(solution)/shard_map/all_to_all | solution.py:710
  56.7 3.6 %collective-permute-done.4.refs_1_ = bf16[8,256,384]{2,1,0:T(8,128)(2,1)S(1)} collective-permute-done((bf16[8,256,384]{2,1,0:T(8,128)(2,1)}, bf16[8,256,384]{2,1,0:T(8,128)(2,1)S(1)}, u32[]{:S(2)}, u32[]{:S(2)}) %collective-permute-start.4) | collective-permute-done | bytes 1572896 | tf_op jit(solution)/shard_map/ppermute | solution.py:707
  61.5 17.9 %attend_forward.1 = (bf16[8,256,128]{2,1,0:T(8,128)(2,1)}, bf16[16,256,128]{2,1,0:T(8,128)(2,1)}, bf16[16,512,256]{2,1,0:T(8,128)(2,1)}) custom-call(s32[96,16]{1,0:T(8,128)} %get-tuple-element.33.plan_ref, s32[16,1,768]{2,1,0:T(1,128)} %get-tuple-element.34.place_ref, f32[16,256,512]{2,1,0:T(8,128)} %get-tuple-element.35.bias_ref, ...), custom_call_target="tpu_custom_call" | custom-call | tf_op jit(solution)/shard_map/attend_forward/pallas_call | solution.py:353
  79.4 3.7 %all-to-all-start.1 = ((bf16[8,256,128]{2,1,0:T(8,128)(2,1)}), bf16[8,256,128]{2,1,0:T(8,128)(2,1)S(1)}, u32[]{:S(2)}, u32[]{:S(2)}) async-start(bf16[8,256,128]{2,1,0:T(8,128)(2,1)} %get-tuple-element.37), calls=%async_computation.1 | async-start | bytes 1048576 | tf_op jit(solution)/shard_map/all_to_all | solution.py:710
  84.6 12.5 %all-to-all-done.1.parts = bf16[8,256,128]{2,1,0:T(8,128)(2,1)S(1)} async-done(((bf16[8,256,128]{2,1,0:T(8,128)(2,1)}), bf16[8,256,128]{2,1,0:T(8,128)(2,1)S(1)}, u32[]{:S(2)}, u32[]{:S(2)}) %all-to-all-start.1) | async-done | bytes 524320 | tf_op jit(solution)/shard_map/all_to_all | solution.py:710
  98.0 3.9 %norm_gate.1 = (bf16[256,1024]{1,0:T(8,128)(2,1)}, bf16[256,1024]{1,0:T(8,128)(2,1)}, bf16[8,256,128]{2,1,0:T(8,128)(2,1)}) custom-call(s32[1,256]{1,0:T(1,128)} %bitcast.17, bf16[256,1024]{1,0:T(8,128)(2,1)} %gate_ref.1, bf16[256,1024]{1,0:T(8,128)(2,1)} %convolution_convert_fusion.1.grad_ref, bf16[8,256,128]{2,1,0:T(8,128)(2,1)} %copy-done.2), custom_call_target="tpu_custom_call" | custom-call | tf_op jit(solution)/shard_map/norm_gate/pallas_call | solution.py:412
  101.8 3.6 %all-to-all-start.2 = ((bf16[8,256,128]{2,1,0:T(8,128)(2,1)}), bf16[8,256,128]{2,1,0:T(8,128)(2,1)S(1)}, u32[]{:S(2)}, u32[]{:S(2)}) async-start(bf16[8,256,128]{2,1,0:T(8,128)(2,1)} %get-tuple-element.42), calls=%async_computation.2 | async-start | bytes 1048576 | tf_op jit(solution)/shard_map/all_to_all | solution.py:710
  108.5 3.8 %weight_parts.1 = bf16[8,64,1024]{2,1,0:T(8,128)(2,1)} custom-call(s32[1]{0:T(128)} %bitcast.6.at, bf16[256,1024]{1,0:T(8,128)(2,1)} %get-tuple-element.38.refs_0_, bf16[256,1024]{1,0:T(8,128)(2,1)} %collective-permute-done.5.refs_1_, bf16[256,1024]{1,0:T(8,128)(2,1)} %refs_2_.1, bf16[256,1024]{1,0:T(8,128)(2,1)} %collective-permute-done.6.refs_3_), custom_call_target="tpu_custom_call" | custom-call | tf_op jit(solution)/shard_map/weight_parts/pallas_call | solution.py:638
  112.3 7.8 %all-to-all-done.2.grad_ref = bf16[8,256,128]{2,1,0:T(8,128)(2,1)S(1)} async-done(((bf16[8,256,128]{2,1,0:T(8,128)(2,1)}), bf16[8,256,128]{2,1,0:T(8,128)(2,1)S(1)}, u32[]{:S(2)}, u32[]{:S(2)}) %all-to-all-start.2) | async-done | bytes 524320 | tf_op jit(solution)/shard_map/all_to_all | solution.py:710
  120.9 3.6 %all-to-all-start.4 = ((bf16[8,64,1024]{2,1,0:T(8,128)(2,1)}), bf16[8,64,1024]{2,1,0:T(8,128)(2,1)S(1)}, u32[]{:S(2)}, u32[]{:S(2)}) async-start(bf16[8,64,1024]{2,1,0:T(8,128)(2,1)} %weight_parts.1), calls=%async_computation.4 | async-start | bytes 2097152 | tf_op jit(solution)/shard_map/all_to_all | solution.py:710
  124.5 28.4 %attend_backward.1 = (bf16[8,256,128]{2,1,0:T(8,128)(2,1)}, bf16[16,256,256]{2,1,0:T(8,128)(2,1)}, f32[16,8,128]{2,1,0:T(8,128)}) custom-call(s32[96,16]{1,0:T(8,128)} %get-tuple-element.33.plan_ref, s32[16,1,768]{2,1,0:T(1,128)} %get-tuple-element.34.place_ref, f32[16,256,512]{2,1,0:T(8,128)} %get-tuple-element.35.bias_ref, ...), custom_call_target="tpu_custom_call" | custom-call | tf_op jit(solution)/shard_map/attend_backward/pallas_call | solution.py:557
  152.9 3.1 %fusion.2 = (bf16[8,256,256]{2,1,0:T(8,128)(2,1)}, bf16[8,256,256]{2,1,0:T(8,128)(2,1)}) fusion(bf16[16,256,256]{2,1,0:T(8,128)(2,1)} %get-tuple-element.45), kind=kLoop, calls=%fused_computation.21 | loop fusion | bytes 4194304 | tf_op jit(solution)/shard_map/slice | solution.py:760
  156.9 1.7 collective-permute-done.7
  159.2 3.1 %join_rows.1 = bf16[8,264,384]{2,1,0:T(8,128)(2,1)} custom-call(bf16[8,256,128]{2,1,0:T(8,128)(2,1)} %get-tuple-element.44.q_ref, bf16[8,256,256]{2,1,0:T(8,128)(2,1)} %get-tuple-element.56.own_ref, f32[1,384]{1,0:T(1,128)} %reshape_add_fusion.sum_ref, bf16[8,256,256]{2,1,0:T(8,128)(2,1)} %collective-permute-done.8.refs_0_), custom_call_target="tpu_custom_call" | custom-call | tf_op jit(solution)/shard_map/join_rows/pallas_call | solution.py:608
  162.3 6.0 %all-to-all-start.3 = ((bf16[8,264,384]{2,1,0:T(8,128)(2,1)}), bf16[8,264,384]{2,1,0:T(8,128)(2,1)}, u32[]{:S(2)}, u32[]{:S(2)}) async-start(bf16[8,264,384]{2,1,0:T(8,128)(2,1)} %join_rows.1), calls=%async_computation.3 | async-start | bytes 3244032 | tf_op jit(solution)/shard_map/all_to_all | solution.py:710
  168.3 2.5 %convolution_convert_fusion = bf16[256,1024]{1,0:T(8,128)(2,1)} fusion(bf16[256,1024]{1,0:T(8,128)(2,1)} %get-tuple-element.38.refs_0_, bf16[1024,1024]{1,0:T(8,128)(2,1)S(1)} %copy-done), kind=kOutput, calls=%fused_computation.2 | convolution fusion | flops 537133056 | bytes 3145728 | tf_op jit(solution)/shard_map/dot_general | solution.py:751
  171.8 35.1 %all-to-all-done.3.pack_ref = bf16[8,264,384]{2,1,0:T(8,128)(2,1)} async-done(((bf16[8,264,384]{2,1,0:T(8,128)(2,1)}), bf16[8,264,384]{2,1,0:T(8,128)(2,1)}, u32[]{:S(2)}, u32[]{:S(2)}) %all-to-all-start.3) | async-done | bytes 1622048 | tf_op jit(solution)/shard_map/all_to_all | solution.py:710
  206.8 3.7 %unpack_rows.1 = (bf16[256,1024]{1,0:T(8,128)(2,1)}, bf16[256,1024]{1,0:T(8,128)(2,1)}, bf16[256,1024]{1,0:T(8,128)(2,1)}, f32[8,128]{1,0:T(8,128)}) custom-call(s32[1,256]{1,0:T(1,128)} %bitcast.18, bf16[8,264,384]{2,1,0:T(8,128)(2,1)} %all-to-all-done.3.pack_ref), custom_call_target="tpu_custom_call" | custom-call | tf_op jit(solution)/shard_map/unpack_rows/pallas_call | solution.py:669
  (47 shorter events, 18.4 us)
Async XLA Ops:
  0.6 82.4 %copy-start = (bf16[1024,1024]{1,0:T(8,128)(2,1)S(1)}, bf16[1024,1024]{1,0:T(8,128)(2,1)}, u32[]{:S(2)}) copy-start(bf16[1024,1024]{1,0:T(8,128)(2,1)} %param.15) | copy-start | bytes 6291460
  2.4 4.6 %collective-permute-start = (s32[1,2,512]{2,1,0:T(2,128)S(1)}, s32[1,2,512]{2,1,0:T(2,128)S(1)}, u32[]{:S(2)}, u32[]{:S(2)}) collective-permute-start(s32[1,2,512]{2,1,0:T(2,128)S(1)} %add_bitcast_fusion), channel_id=1, source_target_pairs={{0,2},{1,3},{2,0},{3,1},{4,6},{5,7},{6,4},{7,5},{8,10},{9,11},{10,... | collective-permute-start | bytes 12296 | tf_op jit(solution)/shard_map/ppermute | solution.py:707
  7.0 3.7 %collective-permute-start.1 = (s32[2,2,512]{2,1,0:T(2,128)S(1)}, s32[2,2,512]{2,1,0:T(2,128)S(1)}, u32[]{:S(2)}, u32[]{:S(2)}) collective-permute-start(s32[2,2,512]{2,1,0:T(2,128)S(1)} %pad_add_fusion.3), channel_id=1, source_target_pairs={{0,4},{1,5},{2,6},{3,7},{4,0},{5,1},{6,2},{7,3},{8,12},{9,13},{10,... | collective-permute-start | bytes 24584 | tf_op jit(solution)/shard_map/ppermute | solution.py:707
  10.7 6.7 %collective-permute-start.2 = (s32[4,2,512]{2,1,0:T(2,128)S(1)}, s32[4,2,512]{2,1,0:T(2,128)S(1)}, u32[]{:S(2)}, u32[]{:S(2)}) collective-permute-start(s32[4,2,512]{2,1,0:T(2,128)S(1)} %pad_add_fusion.2), channel_id=1, source_target_pairs={{0,8},{1,9},{2,10},{3,11},{4,12},{5,13},{6,14},{7,15},{8,0},{9,1},... | collective-permute-start | bytes 49160 | tf_op jit(solution)/shard_map/ppermute | solution.py:707
  17.5 39.2 %all-to-all-start = ((bf16[8,256,384]{2,1,0:T(8,128)(2,1)}), bf16[8,256,384]{2,1,0:T(8,128)(2,1)}, u32[]{:S(2)}, u32[]{:S(2)}) async-start(bf16[8,256,384]{2,1,0:T(8,128)(2,1)} %pack_rows.1), calls=%async_computation | async-start | bytes 3145728 | tf_op jit(solution)/shard_map/all_to_all | solution.py:710
  22.4 1.3 collective-permute-start.3
  56.7 3.6 %collective-permute-start.4 = (bf16[8,256,384]{2,1,0:T(8,128)(2,1)}, bf16[8,256,384]{2,1,0:T(8,128)(2,1)S(1)}, u32[]{:S(2)}, u32[]{:S(2)}) collective-permute-start(bf16[8,256,384]{2,1,0:T(8,128)(2,1)} %all-to-all-done.refs_0_), channel_id=1, source_target_pairs={{0,1},{1,0},{2,3},{3,2},{4,5},{5,4},{6,7},{7,6},{8,9},{9,8},{10,11... | collective-permute-start | bytes 4718600 | tf_op jit(solution)/shard_map/ppermute | solution.py:707
  60.3 1.2 copy-start.3
  61.5 21.6 %copy-start.4 = (bf16[256,1024]{1,0:T(8,128)(2,1)S(1)}, bf16[256,1024]{1,0:T(8,128)(2,1)}, u32[]{:S(2)}) copy-start(bf16[256,1024]{1,0:T(8,128)(2,1)} %refs_2_.1) | copy-start | bytes 1572868
  79.4 17.8 %all-to-all-start.1 = ((bf16[8,256,128]{2,1,0:T(8,128)(2,1)}), bf16[8,256,128]{2,1,0:T(8,128)(2,1)S(1)}, u32[]{:S(2)}, u32[]{:S(2)}) async-start(bf16[8,256,128]{2,1,0:T(8,128)(2,1)} %get-tuple-element.37), calls=%async_computation.1 | async-start | bytes 1048576 | tf_op jit(solution)/shard_map/all_to_all | solution.py:710
  97.2 0.8 copy-start.2
  101.8 18.2 %all-to-all-start.2 = ((bf16[8,256,128]{2,1,0:T(8,128)(2,1)}), bf16[8,256,128]{2,1,0:T(8,128)(2,1)S(1)}, u32[]{:S(2)}, u32[]{:S(2)}) async-start(bf16[8,256,128]{2,1,0:T(8,128)(2,1)} %get-tuple-element.42), calls=%async_computation.2 | async-start | bytes 1048576 | tf_op jit(solution)/shard_map/all_to_all | solution.py:710
  105.5 2.0 collective-permute-start.6
  105.5 3.0 %collective-permute-start.5 = (bf16[256,1024]{1,0:T(8,128)(2,1)}, bf16[256,1024]{1,0:T(8,128)(2,1)}, u32[]{:S(2)}, u32[]{:S(2)}) collective-permute-start(bf16[256,1024]{1,0:T(8,128)(2,1)} %get-tuple-element.38.refs_0_), channel_id=1, source_target_pairs={{0,1},{1,0},{2,3},{3,2},{4,5},{5,4},{6,7},{7,6},{8,9},{9,8},{10,11... | collective-permute-start | bytes 1572872 | tf_op jit(solution)/shard_map/ppermute | solution.py:707
  120.1 0.8 copy-start.1
  120.9 41.5 %all-to-all-start.4 = ((bf16[8,64,1024]{2,1,0:T(8,128)(2,1)}), bf16[8,64,1024]{2,1,0:T(8,128)(2,1)S(1)}, u32[]{:S(2)}, u32[]{:S(2)}) async-start(bf16[8,64,1024]{2,1,0:T(8,128)(2,1)} %weight_parts.1), calls=%async_computation.4 | async-start | bytes 2097152 | tf_op jit(solution)/shard_map/all_to_all | solution.py:710
  152.9 3.1 %copy-start.5 = (f32[16,8,128]{2,1,0:T(8,128)S(1)}, f32[16,8,128]{2,1,0:T(8,128)}, u32[]{:S(2)}) copy-start(f32[16,8,128]{2,1,0:T(8,128)} %get-tuple-element.46) | copy-start | bytes 196612
  156.0 3.2 %collective-permute-start.8 = (bf16[8,256,256]{2,1,0:T(8,128)(2,1)}, bf16[8,256,256]{2,1,0:T(8,128)(2,1)}, u32[]{:S(2)}, u32[]{:S(2)}) collective-permute-start(bf16[8,256,256]{2,1,0:T(8,128)(2,1)} %get-tuple-element.55), channel_id=1, source_target_pairs={{0,1},{1,0},{2,3},{3,2},{4,5},{5,4},{6,7},{7,6},{8,9},{9,8},{10,11... | collective-permute-start | bytes 3145736 | tf_op jit(solution)/shard_map/ppermute | solution.py:707
  156.4 2.3 %collective-permute-start.7 = (f32[1,384]{1,0:T(1,128)S(1)}, f32[1,384]{1,0:T(1,128)S(1)}, u32[]{:S(2)}, u32[]{:S(2)}) collective-permute-start(f32[1,384]{1,0:T(1,128)S(1)} %broadcast_in_dim.37), channel_id=1, source_target_pairs={{0,1},{1,0},{2,3},{3,2},{4,5},{5,4},{6,7},{7,6},{8,9},{9,8},{10,11... | collective-permute-start | bytes 4616 | tf_op jit(solution)/shard_map/ppermute | solution.py:707
  162.3 44.5 %all-to-all-start.3 = ((bf16[8,264,384]{2,1,0:T(8,128)(2,1)}), bf16[8,264,384]{2,1,0:T(8,128)(2,1)}, u32[]{:S(2)}, u32[]{:S(2)}) async-start(bf16[8,264,384]{2,1,0:T(8,128)(2,1)} %join_rows.1), calls=%async_computation.3 | async-start | bytes 3244032 | tf_op jit(solution)/shard_map/all_to_all | solution.py:710

commit v3 on v2

--- a/solution.py
+++ b/solution.py
@@ -31,7 +31,9 @@
 
 def params(steps=0):
     semantics = ("arbitrary",) * steps if steps else None
-    return pltpu.CompilerParams(dimension_semantics=semantics, vmem_limit_bytes=56 << 20)
+    return pltpu.CompilerParams(
+        dimension_semantics=semantics, vmem_limit_bytes=62 << 20
+    )
 
 
 def slot_ranks(slot_row):
@@ -78,10 +80,33 @@
     return 4 if owners % 4 == 0 else 1
 
 
-def tiles_of(query_max, key_max, query_tile):
-    return [
-        (qt, kt) for qt in range(query_max // query_tile) for kt in range(key_max // key_tile)
-    ][1:]
+def query_cuts(query_max):
+    main = query_max * 9 // 16 if query_max % 256 == 0 else query_max
+    return [slice(0, main)] + ([slice(main, query_max)] if main < query_max else [])
+
+
+def tiles_of(cuts, key_max):
+    return [(qt, kt) for qt in range(len(cuts)) for kt in range(key_max // key_tile)][1:]
+
+
+def column_of(ref, g, rows):
+    first, count = rows.start, rows.stop - rows.start
+    low = first // 128 * 128
+    row = ref[g, :, low : -(-rows.stop // 128) * 128]
+    eye = lax.broadcasted_iota(i32, (count, row.shape[1]), 0) + (first - low)
+    eye = eye == lax.broadcasted_iota(i32, (count, row.shape[1]), 1)
+    return jnp.sum(jnp.where(eye, row, 0), axis=1, keepdims=True)
+
+
+def bias_tile(levels, buckets, ref, g, rows, cols):
+    column = column_of(ref, g, rows)
+    key_codes = ref[g, :, cols]
+    gap = column - key_codes
+    level = jnp.full(gap.shape, levels[0], f32)
+    for e in range(buckets - 1):
+        level = jnp.where(gap >= 2**e, levels[e + 1], level)
+    allowed = (gap >= 0) & ((column ^ key_codes) < 2 ** (buckets - 1))
+    return jnp.where(allowed, level, masked_score)
 
 
 def make_plan(head_bias, slot_meta, capacity, window, near_loaders):
@@ -91,7 +116,8 @@
     buckets = head_bias.shape[0]
     query_max = near_loaders * capacity
     key_max = slot_count
-    query_tile = min(128, query_max)
+    cuts = query_cuts(query_max)
+    query_tile = cuts[0].stop
     spots = loaders * window
     batch = batch_of(owners)
     stamp_span = 2 ** (buckets - 1)
@@ -157,23 +183,7 @@
             spot_col[...] = jnp.transpose(spot_of)
             code_col[...] = jnp.transpose(hist * stamp_span + meta_ref[:, 1, :] - nobody)
 
-        eye = lax.broadcasted_iota(i32, (query_tile, query_tile), 0) == lax.broadcasted_iota(
-            i32, (query_tile, query_tile), 1
-        )
-
-        def fill(g, qt, kt):
-            rows = slice(qt * query_tile, (qt + 1) * query_tile)
-            cols = slice(kt * key_tile, (kt + 1) * key_tile)
-            column = jnp.sum(jnp.where(eye, code_ref[g, :, rows], 0), axis=1, keepdims=True)
-            gap = column - code_ref[g, :, cols]
-            level = jnp.full(gap.shape, bias[0], f32)
-            for e in range(buckets - 1):
-                level = jnp.where(gap >= 2**e, bias[e + 1], level)
-            allowed = (gap >= 0) & ((column ^ code_ref[g, :, cols]) < stamp_span)
-            out_ref[g, rows, cols] = jnp.where(allowed, level, masked_score)
-
         ids = lax.broadcasted_iota(i32, (capacity, key_max), 1)
-        totals = []
         for g in range(batch):
             owner = pl.program_id(0) * batch + g
             rows = pl.ds(pl.multiple_of(owner * capacity, 8), capacity)
@@ -182,18 +192,9 @@
             found = jnp.zeros((capacity, key_max), i32)
             for i in range(loaders):
                 found = found + jnp.where(spot[:, i : i + 1] == ids, code[:, i : i + 1], 0)
-            held = (spot >= 0).astype(f32)
-            totals.append((jnp.sum(held[:, :near_loaders]), jnp.sum(held)))
             code_ref[g] = jnp.sum(found, axis=0, keepdims=True) + nobody
         for g in range(batch):
-            fill(g, 0, 0)
-        for g in range(batch):
-            query_count, key_count = totals[g]
-            for qt, kt in tiles_of(query_max, key_max, query_tile):
-
-                @pl.when((query_count > qt * query_tile) & (key_count > kt * key_tile))
-                def _():
-                    fill(g, qt, kt)
+            out_ref[g] = bias_tile(bias, buckets, code_ref, g, cuts[0], slice(0, key_tile))
 
     by_owner = lambda o, *_: (o, 0, 0)
     return pl.pallas_call(
@@ -206,7 +207,7 @@
                 vmem_spec((6 * owners, loaders)),
                 vmem_spec((owners, 1, spots)),
                 pl.BlockSpec((batch, 1, key_max), by_owner),
-                pl.BlockSpec((batch, query_max, key_max), by_owner),
+                pl.BlockSpec((batch, query_tile, key_tile), by_owner),
             ],
             scratch_shapes=[
                 pltpu.VMEM((slot_count, loaders), i32),
@@ -217,7 +218,7 @@
             shaped((6 * owners, loaders), i32),
             shaped((owners, 1, spots), i32),
             shaped((owners, 1, key_max), i32),
-            shaped((owners, query_max, key_max), f32),
+            shaped((owners, query_tile, key_tile), f32),
         ],
         compiler_params=params(1),
         name="make_plan",
@@ -253,18 +254,21 @@
     return begin, spans
 
 
-def attend_forward(plan, place, bias, packs, window, head_count):
+def attend_forward(plan, head_bias, place, bias, codes, packs, window, head_count):
     owners, _, spots = place.shape
     loaders = len(packs) * head_count
     tokens = packs[0].shape[1]
     size = packs[0].shape[2] // 3
-    query_max, key_max = bias.shape[1:]
-    query_tile = min(128, query_max)
+    key_max = codes.shape[2]
+    query_max = head_count * key_max // loaders
+    buckets = head_bias.shape[0]
+    cuts = query_cuts(query_max)
+    query_tile = cuts[0].stop
     scale = size ** (-0.5)
     near = head_count * window
     batch = batch_of(owners)
 
-    def body(plan_ref, place_ref, bias_ref, *refs):
+    def body(plan_ref, levels, place_ref, bias_ref, code_ref, *refs):
         pack_refs = refs[: len(packs)]
         mixed_ref, qs_ref, kvs_ref, q_win, kv_win, acc, back = refs[len(packs) :]
 
@@ -273,12 +277,13 @@
             mixed_ref[...] = jnp.zeros(mixed_ref.shape, mixed_ref.dtype)
 
         def attend(g, qt, kt):
-            rows = slice(qt * query_tile, (qt + 1) * query_tile)
+            rows = cuts[qt]
             cols = slice(kt * key_tile, (kt + 1) * key_tile)
-            score = (
-                dot(qs_ref[g, rows, :], kvs_ref[g, cols, :size], ((1,), (1,))) * scale
-                + bias_ref[g, rows, cols]
-            )
+            if (qt, kt) == (0, 0):
+                level = bias_ref[g]
+            else:
+                level = bias_tile(levels, buckets, code_ref, g, rows, cols)
+            score = dot(qs_ref[g, rows, :], kvs_ref[g, cols, :size], ((1,), (1,))) * scale + level
             weight = jnp.where(
                 score > 0.1 * masked_score, score * gate_of(score), 0.0
             ).astype(bf16)
@@ -290,8 +295,8 @@
             kvs_ref[g, kt * key_tile : (kt + 1) * key_tile, :] = dot(chosen, kv_win[g]).astype(bf16)
 
         def load_queries(g, qt):
-            chosen = gather_matrix(qt * query_tile, query_tile, place_ref[g, :, :near])
-            qs_ref[g, qt * query_tile : (qt + 1) * query_tile, :] = dot(chosen, q_win[g]).astype(bf16)
+            chosen = gather_matrix(cuts[qt].start, cuts[qt].stop - cuts[qt].start, place_ref[g, :, :near])
+            qs_ref[g, cuts[qt], :] = dot(chosen, q_win[g]).astype(bf16)
 
         owner_of = [pl.program_id(0) * batch + g for g in range(batch)]
         plans = [read_plan(plan_ref, owner, owners, loaders) for owner in owner_of]
@@ -316,33 +321,36 @@
             def _():
                 for kt in range(1, key_max // key_tile):
                     pl.when(kt * key_tile < key_count)(lambda: load_keys(g, kt))
-                for qt in range(1, query_max // query_tile):
-                    pl.when(qt * query_tile < query_count)(lambda: load_queries(g, qt))
-                for qt, kt in tiles_of(query_max, key_max, query_tile):
-                    pl.when((qt * query_tile < query_count) & (kt * key_tile < key_count))(
+                for qt in range(1, len(cuts)):
+                    pl.when(cuts[qt].start < query_count)(lambda: load_queries(g, qt))
+                for qt, kt in tiles_of(cuts, key_max):
+                    pl.when((cuts[qt].start < query_count) & (kt * key_tile < key_count))(
                         lambda: attend(g, qt, kt)
                     )
 
         for g in range(batch):
             chosen = scatter_matrix(0, query_tile, plans[g][1][:head_count], window)
-            back[g] = dot(chosen, acc[g, :query_tile, :].astype(bf16))
-        for g in range(batch):
-            for qt in range(1, query_max // query_tile):
-
-                @pl.when(qt * query_tile < plan_ref[4 * owners + owner_of[g], 0])
+            back[g] = dot(chosen, acc[g, :query_tile, :].astype(bf16)).astype(bf16)
+        for g in range(batch):
+            for qt in range(1, len(cuts)):
+
+                @pl.when(cuts[qt].start < plan_ref[4 * owners + owner_of[g], 0])
                 def _():
                     chosen = scatter_matrix(
-                        qt * query_tile, query_tile, plans[g][1][:head_count], window
+                        cuts[qt].start,
+                        cuts[qt].stop - cuts[qt].start,
+                        plans[g][1][:head_count],
+                        window,
                     )
-                    rows = slice(qt * query_tile, (qt + 1) * query_tile)
-                    back[g] = back[g] + dot(chosen, acc[g, rows, :].astype(bf16))
+                    rows = cuts[qt]
+                    back[g] = back[g] + dot(chosen, acc[g, rows, :].astype(bf16)).astype(bf16)
 
         for g in range(batch):
             for i in range(head_count):
                 spot = pl.ds(plans[g][0][i], window)
                 mixed_ref[i, spot, :] = mixed_ref[i, spot, :] + back[
                     g, i * window : (i + 1) * window, :
-                ].astype(bf16)
+                ]
 
     out_shape = [
         shaped((head_count, tokens, size), bf16),
@@ -353,11 +361,12 @@
     return pl.pallas_call(
         body,
         grid_spec=pltpu.PrefetchScalarGridSpec(
-            num_scalar_prefetch=1,
+            num_scalar_prefetch=2,
             grid=(owners // batch,),
             in_specs=[
                 pl.BlockSpec((batch, 1, spots), by_owner),
-                pl.BlockSpec((batch, query_max, key_max), by_owner),
+                pl.BlockSpec((batch, query_tile, key_tile), by_owner),
+                pl.BlockSpec((batch, 1, key_max), by_owner),
             ]
             + [vmem_spec(x.shape) for x in packs],
             out_specs=[
@@ -369,13 +378,13 @@
                 pltpu.VMEM((batch, near, size), bf16),
                 pltpu.VMEM((batch, loaders * window, 2 * size), bf16),
                 pltpu.VMEM((batch, query_max, size), f32),
-                pltpu.VMEM((batch, near, size), f32),
+                pltpu.VMEM((batch, near, size), bf16),
             ],
         ),
         out_shape=out_shape,
         compiler_params=params(1),
         name="attend_forward",
-    )(plan, place, bias, *packs)
+    )(plan, head_bias, place, bias, codes, *packs)
 
 
 def norm_gate(slot_row, gate_values, fresh_grad, mixed_parts):
@@ -423,42 +432,47 @@
 
 
 def attend_backward(
-    plan, place, bias, codes, sorted_query, sorted_pair, grads, window, loaders, buckets
+    plan, head_bias, place, bias, codes, sorted_query, sorted_pair, grads, window, loaders, factor
 ):
     owners, _, spots = place.shape
     head_count, tokens, size = grads.shape
-    query_max, key_max = bias.shape[1:]
-    query_tile = min(128, query_max)
+    key_max = codes.shape[2]
+    query_max = head_count * key_max // loaders
+    buckets = head_bias.shape[0]
+    cuts = query_cuts(query_max)
+    query_tile = cuts[0].stop
     scale = size ** (-0.5)
     near = head_count * window
     batch = batch_of(owners)
-
-    def body(plan_ref, place_ref, bias_ref, code_ref, qs_ref, kvs_ref, grad_ref, *refs):
-        dq_ref, dkv_ref, sums_ref = refs[:3]
-        grad_win, grad_rows, dq_acc, dkv_acc, dq_back, dkv_back = refs[3:]
+    groups = loaders // head_count
+
+    def body(plan_ref, levels, place_ref, bias_ref, code_ref, qs_ref, kvs_ref, grad_ref, *refs):
+        dq_ref, bias_ref_out = refs[:2]
+        dkv_refs = refs[2 : 2 + groups]
+        grad_win, grad_rows, dq_acc, dkv_acc, dq_back, dkv_back, sums_ref = refs[2 + groups :]
 
         @pl.when(pl.program_id(0) == 0)
         def _():
-            for ref in (dq_ref, dkv_ref, sums_ref):
+            for ref in (dq_ref, sums_ref) + tuple(dkv_refs):
                 ref[...] = jnp.zeros(ref.shape, ref.dtype)
 
-        eye = lax.broadcasted_iota(i32, (query_tile, query_tile), 0) == lax.broadcasted_iota(
-            i32, (query_tile, query_tile), 1
-        )
-
         def load_grads(g, qt):
-            chosen = gather_matrix(qt * query_tile, query_tile, place_ref[g, :, :near])
-            rows = slice(qt * query_tile, (qt + 1) * query_tile)
+            chosen = gather_matrix(cuts[qt].start, cuts[qt].stop - cuts[qt].start, place_ref[g, :, :near])
+            rows = cuts[qt]
             grad_rows[g, rows, :] = dot(chosen, grad_win[g]).astype(bf16)
 
         def attend(g, qt, kt):
-            rows = slice(qt * query_tile, (qt + 1) * query_tile)
+            rows = cuts[qt]
             cols = slice(kt * key_tile, (kt + 1) * key_tile)
             query = qs_ref[g, rows, :]
             key = kvs_ref[g, cols, :size]
             value = kvs_ref[g, cols, size:]
             grad = grad_rows[g, rows, :]
-            score = dot(query, key, ((1,), (1,))) * scale + bias_ref[g, rows, cols]
+            if (qt, kt) == (0, 0):
+                level = bias_ref[g]
+            else:
+                level = bias_tile(levels, buckets, code_ref, g, rows, cols)
+            score = dot(query, key, ((1,), (1,))) * scale + level
             product = dot(grad, value, ((1,), (1,)))
             allowed = score > 0.1 * masked_score
             gate = gate_of(score)
@@ -476,13 +490,12 @@
                 dkv_acc[g, cols, :size] = dkv_acc[g, cols, :size] + dk
                 dkv_acc[g, cols, size:] = dkv_acc[g, cols, size:] + dv
             dq_acc[g, rows, :] = dq if kt == 0 else dq_acc[g, rows, :] + dq
-            time_col = jnp.sum(jnp.where(eye, code_ref[g, :, rows], 0), axis=1, keepdims=True)
-            gap = time_col - code_ref[g, :, cols]
+            gap = column_of(code_ref, g, rows) - code_ref[g, :, cols]
             for level in range(buckets):
                 held = score_grad
                 if level > 0:
                     held = jnp.where(gap >= 2 ** (level - 1), score_grad, 0.0)
-                folded = jnp.sum(held.reshape(query_tile // 8, 8, key_tile), axis=0)
+                folded = jnp.sum(held.reshape(held.shape[0] // 8, 8, key_tile), axis=0)
                 sums_ref[level] = sums_ref[level] + (folded[:, :128] + folded[:, 128:])
 
         owner_of = [pl.program_id(0) * batch + g for g in range(batch)]
@@ -502,13 +515,13 @@
 
             @pl.when((query_count > query_tile) | (key_count > key_tile))
             def _():
-                for qt in range(1, query_max // query_tile):
-                    pl.when(qt * query_tile < query_count)(lambda: load_grads(g, qt))
-                for qt, kt in tiles_of(query_max, key_max, query_tile):
+                for qt in range(1, len(cuts)):
+                    pl.when(cuts[qt].start < query_count)(lambda: load_grads(g, qt))
+                for qt, kt in tiles_of(cuts, key_max):
                     if qt == 0 and kt > 0:
                         cols = slice(kt * key_tile, (kt + 1) * key_tile)
                         dkv_acc[g, cols, :] = jnp.zeros((key_tile, 2 * size), f32)
-                    pl.when((qt * query_tile < query_count) & (kt * key_tile < key_count))(
+                    pl.when((cuts[qt].start < query_count) & (kt * key_tile < key_count))(
                         lambda: attend(g, qt, kt)
                     )
 
@@ -519,18 +532,21 @@
         for g in range(batch):
             spans = plans[g][1]
             chosen = scatter_matrix(0, query_tile, spans[:head_count], window)
-            dq_back[g] = dot(chosen, (dq_acc[g, :query_tile, :] * scale).astype(bf16))
+            dq_back[g] = dot(chosen, (dq_acc[g, :query_tile, :] * scale).astype(bf16)).astype(bf16)
             chosen = scatter_matrix(0, key_tile, spans, window)
-            dkv_back[g] = dot(chosen, halves(g, slice(0, key_tile)))
+            dkv_back[g] = dot(chosen, halves(g, slice(0, key_tile))).astype(bf16)
         for g in range(batch):
             spans = plans[g][1]
-            for qt in range(1, query_max // query_tile):
-
-                @pl.when(qt * query_tile < plan_ref[4 * owners + owner_of[g], 0])
+            for qt in range(1, len(cuts)):
+
+                @pl.when(cuts[qt].start < plan_ref[4 * owners + owner_of[g], 0])
                 def _():
-                    chosen = scatter_matrix(qt * query_tile, query_tile, spans[:head_count], window)
-                    rows = slice(qt * query_tile, (qt + 1) * query_tile)
-                    dq_back[g] = dq_back[g] + dot(chosen, (dq_acc[g, rows, :] * scale).astype(bf16))
+                    chosen = scatter_matrix(
+                        cuts[qt].start, cuts[qt].stop - cuts[qt].start, spans[:head_count], window
+                    )
+                    rows = cuts[qt]
+                    moved = dot(chosen, (dq_acc[g, rows, :] * scale).astype(bf16))
+                    dq_back[g] = dq_back[g] + moved.astype(bf16)
 
             for kt in range(1, key_max // key_tile):
 
@@ -538,30 +554,39 @@
                 def _():
                     chosen = scatter_matrix(kt * key_tile, key_tile, spans, window)
                     cols = slice(kt * key_tile, (kt + 1) * key_tile)
-                    dkv_back[g] = dkv_back[g] + dot(chosen, halves(g, cols))
+                    dkv_back[g] = dkv_back[g] + dot(chosen, halves(g, cols)).astype(bf16)
 
         for g in range(batch):
             for i in range(loaders):
                 spot = pl.ds(plans[g][0][i], window)
                 part = slice(i * window, (i + 1) * window)
                 if i < head_count:
-                    dq_ref[i, spot, :] = dq_ref[i, spot, :] + dq_back[g, part, :].astype(bf16)
-                dkv_ref[i, spot, :] = dkv_ref[i, spot, :] + dkv_back[g, part, :].astype(bf16)
+                    dq_ref[i, spot, :] = dq_ref[i, spot, :] + dq_back[g, part, :]
+                target, h = dkv_refs[i // head_count], i % head_count
+                target[h, spot, :] = target[h, spot, :] + dkv_back[g, part, :]
+
+        @pl.when(pl.program_id(0) == owners // batch - 1)
+        def _():
+            above = jnp.sum(jnp.sum(sums_ref[...], axis=1), axis=1, keepdims=True)
+            part = above - jnp.concatenate([above[1:], jnp.zeros((1, 1), f32)], axis=0)
+            spot = lax.broadcasted_iota(i32, (buckets, 128), 0) == lax.broadcasted_iota(
+                i32, (buckets, 128), 1
+            )
+            bias_ref_out[...] = jnp.sum(jnp.where(spot, part * factor, 0.0), axis=0, keepdims=True)
 
     out_shape = [
         shaped((head_count, tokens, size), bf16),
-        shaped((loaders, tokens, 2 * size), bf16),
-        shaped((buckets, 8, 128), f32),
-    ]
+        shaped((1, 128), f32),
+    ] + [shaped((head_count, tokens, 2 * size), bf16)] * groups
     by_owner = lambda o, *_: (o, 0, 0)
     return pl.pallas_call(
         body,
         grid_spec=pltpu.PrefetchScalarGridSpec(
-            num_scalar_prefetch=1,
+            num_scalar_prefetch=2,
             grid=(owners // batch,),
             in_specs=[
                 pl.BlockSpec((batch, 1, spots), by_owner),
-                pl.BlockSpec((batch, query_max, key_max), by_owner),
+                pl.BlockSpec((batch, query_tile, key_tile), by_owner),
                 pl.BlockSpec((batch, 1, key_max), by_owner),
                 pl.BlockSpec((batch, query_max, size), by_owner),
                 pl.BlockSpec((batch, key_max, 2 * size), by_owner),
@@ -573,14 +598,15 @@
                 pltpu.VMEM((batch, query_max, size), bf16),
                 pltpu.VMEM((batch, query_max, size), f32),
                 pltpu.VMEM((batch, key_max, 2 * size), f32),
-                pltpu.VMEM((batch, near, size), f32),
-                pltpu.VMEM((batch, loaders * window, 2 * size), f32),
+                pltpu.VMEM((batch, near, size), bf16),
+                pltpu.VMEM((batch, loaders * window, 2 * size), bf16),
+                pltpu.VMEM((buckets, 8, 128), f32),
             ],
         ),
         out_shape=out_shape,
         compiler_params=params(1),
         name="attend_backward",
-    )(plan, place, bias, codes, sorted_query, sorted_pair, grads)
+    )(plan, head_bias, place, bias, codes, sorted_query, sorted_pair, grads)
 
 
 def join_rows(queries, own, arrived, head_sums):
@@ -590,8 +616,8 @@
     def body(q_ref, own_ref, sum_ref, *refs):
         out_ref = refs[-1]
         rest = sum_ref[...]
-        row = lax.broadcasted_iota(i32, (8, 3 * size), 0)
-        extra = jnp.zeros((8, 3 * size), f32)
+        row = lax.broadcasted_iota(i32, (8, 128), 0)
+        extra = jnp.zeros((8, 128), f32)
         for digit in range(3):
             rounded = rest.astype(bf16).astype(f32)
             rest = rest - rounded
@@ -602,7 +628,7 @@
                 total = total + ref[h].astype(f32)
             out_ref[h, :tokens, :pair] = total.astype(bf16)
             out_ref[h, :tokens, pair:] = q_ref[h]
-            out_ref[h, tokens:, :] = extra.astype(bf16)
+            out_ref[h, tokens:, :] = jnp.concatenate([extra] * (3 * size // 128), axis=1).astype(bf16)
 
     pair_spec = vmem_spec((head_count, tokens, pair))
     return pl.pallas_call(
@@ -658,17 +684,19 @@
 
     def body(slot_ref, pack_ref, q_out, k_out, v_out, bias_out):
         unsort = unsort_matrix(slot_ref[...])
+        gathered = []
         for h in range(head_count):
             cols = slice(h * size, (h + 1) * size)
             k_out[:, cols] = dot(unsort, pack_ref[h, :tokens, :size]).astype(bf16)
             v_out[:, cols] = dot(unsort, pack_ref[h, :tokens, size : 2 * size]).astype(bf16)
             q_out[:, cols] = dot(unsort, pack_ref[h, :tokens, 2 * size :]).astype(bf16)
             digits = pack_ref[h, tokens:, :128].astype(f32)
-            bias_out[h : h + 1, :] = digits[0:1] + digits[1:2] + digits[2:3]
+            gathered.append(digits[0:1] + digits[1:2] + digits[2:3])
+        bias_out[...] = jnp.transpose(jnp.concatenate(gathered, axis=0))[:buckets, :]
 
     return pl.pallas_call(
         body,
-        out_shape=[shaped((tokens, width), bf16)] * 3 + [shaped((head_count, 128), f32)],
+        out_shape=[shaped((tokens, width), bf16)] * 3 + [shaped((buckets, head_count), f32)],
         compiler_params=params(),
         name="unpack_rows",
     )(slot_row, packs)
@@ -742,7 +770,7 @@
     ).astype(bf16)
 
     mixed, sorted_query, sorted_pair = attend_forward(
-        plan, place, bias, packs, window, head_count
+        plan, head_bias, place, bias, codes, packs, window, head_count
     )
     out_grads = [out_grad] + [flip(out_grad, m) for m in range(1, siblings)]
     fresh, gate_grad, grad_parts = norm_gate(slot_row, gate_values, fresh_grad, exchange(mixed))
@@ -753,22 +781,16 @@
     grads, weight_sent = lax.optimization_barrier((grads, weight_sent))
     weight_grad = jnp.sum(exchange(weight_sent).astype(f32), axis=0)
 
-    query_back, pair_back, sums = attend_backward(
-        plan, place, bias, codes, sorted_query, sorted_pair, grads, window, ranks, buckets
+    query_back, head_sums, *pair_back = attend_backward(
+        plan, head_bias, place, bias, codes, sorted_query, sorted_pair, grads, window, ranks, grad_scale
     )
-    other = [
-        flip(pair_back[m * head_count : (m + 1) * head_count], m) for m in range(1, siblings)
-    ]
-    above = jnp.sum(sums, axis=(1, 2))
-    head_sums = (above - jnp.concatenate([above[1:], jnp.zeros((1,), f32)])) * grad_scale
-    head_sums = jnp.pad(head_sums, (0, width * 3 // head_count - buckets))[None]
+    other = [flip(pair_back[m], m) for m in range(1, siblings)]
     mask = 1
     while mask < siblings:
         head_sums = head_sums + flip(head_sums, mask)
         mask *= 2
-    joined = join_rows(query_back, pair_back[:head_count], other, head_sums)
-    query_grad, key_grad, value_grad, bias_rows = unpack_rows(slot_row, exchange(joined), buckets)
-    bias_grad = jnp.transpose(bias_rows[:, :buckets])
+    joined = join_rows(query_back, pair_back[0], other, head_sums)
+    query_grad, key_grad, value_grad, bias_grad = unpack_rows(slot_row, exchange(joined), buckets)
     return (layer_out, query_grad, key_grad, value_grad, gate_grad, weight_grad, bias_grad)
 
 

time: 211 us -> 207 us (0.981)
  Pallas kernels: 77.6 us -> 70.6 us
  matrix products: 4.08 us -> 6.52 us
  local copies, waits for them, and re-layouts: 9.02 us -> 6.68 us
    pallas_call x1, Pallas kernels: 13 us -> 9.77 us  [make_plan(): pl.pallas_call(body, grid_spec=pltpu.PrefetchScalarGridSpec(num_scalar_pr...]
    slice x2 -> x0, local copies, waits for them, and re-layouts: 3.18 us -> none  [the longest x1 3.1 us: on_device(): pair_back[m * head_count:(m + 1) * head_count]]
    unnamed x12 -> x23, local copies, waits for them, and re-layouts: 2.76 us -> 5.57 us
  transfers between devices with their start and end apart: 14 -> 14, of which waited for: 10 -> 11; matrix products, arithmetic and copies ran while one was open for 5% -> 5% of each run, Pallas kernels for 25% -> 23%
where the time goes in v3:
time: 207 us
  waiting for transfers between devices  87.3 us (42%)
  Pallas kernels  70.6 us (34%)
  starting transfers between devices  30.5 us (15%)
  local copies, waits for them, and re-layouts  6.68 us (3%)
  matrix products  6.52 us (3%)
  other arithmetic  4.27 us (2%)
    all_to_all x5, waiting for transfers between devices, exchange(): lax.all_to_all(parts, 'ctx', 0, 0, axis_index_groups=teams, tiled=True)  75.6 us
    pallas_call x1, Pallas kernels, attend_backward(): pl.pallas_call(body, grid_spec=pltpu.PrefetchScalarGridSpec(num_scalar_pr...  26.5 us
    all_to_all x5, starting transfers between devices, exchange(): lax.all_to_all(parts, 'ctx', 0, 0, axis_index_groups=teams, tiled=True)  21.2 us
    pallas_call x1, Pallas kernels, attend_forward(): pl.pallas_call(body, grid_spec=pltpu.PrefetchScalarGridSpec(num_scalar_pr...  16.1 us
    ppermute x9, waiting for transfers between devices, flip(): return lax.ppermute(array, 'ctx', [(i, i ^ mask) for i in range(ranks)])  11.7 us
    pallas_call x1, Pallas kernels, make_plan(): pl.pallas_call(body, grid_spec=pltpu.PrefetchScalarGridSpec(num_scalar_pr...  9.77 us
    ppermute x9, starting transfers between devices, flip(): return lax.ppermute(array, 'ctx', [(i, i ^ mask) for i in range(ranks)])  9.3 us
    unnamed x23, local copies, waits for them, and re-layouts  5.57 us
  transfers between devices with their start and end apart: 14, of which 11 were waited for; matrix products, arithmetic and copies ran while one was open for 5% of the time, Pallas kernels for 23%

profile of v3, /device:TPU:0, one launch (start us, length us, event | category | flops | bytes accessed | tf_op | source)
XLA Modules:
  0.0 206.6 jit_solution(7621372945977585134)
XLA Ops:
  2.2 3.0 %collective-permute-start = (s32[1,2,512]{2,1,0:T(2,128)S(1)}, s32[1,2,512]{2,1,0:T(2,128)S(1)}, u32[]{:S(2)}, u32[]{:S(2)}) collective-permute-start(s32[1,2,512]{2,1,0:T(2,128)S(1)} %add_bitcast_fusion), channel_id=1, source_target_pairs={{0,2},{1,3},{2,0},{3,1},{4,6},{5,7},{6,4},{7,5},{8,10},{9,11},{10,... | collective-permute-start | bytes 12296 | tf_op jit(solution)/shard_map/ppermute | solution.py:735
  6.9 2.1 %collective-permute-start.1 = (s32[2,2,512]{2,1,0:T(2,128)S(1)}, s32[2,2,512]{2,1,0:T(2,128)S(1)}, u32[]{:S(2)}, u32[]{:S(2)}) collective-permute-start(s32[2,2,512]{2,1,0:T(2,128)S(1)} %pad_add_fusion.3), channel_id=1, source_target_pairs={{0,4},{1,5},{2,6},{3,7},{4,0},{5,1},{6,2},{7,3},{8,12},{9,13},{10,... | collective-permute-start | bytes 24584 | tf_op jit(solution)/shard_map/ppermute | solution.py:735
  10.6 3.0 %collective-permute-start.2 = (s32[4,2,512]{2,1,0:T(2,128)S(1)}, s32[4,2,512]{2,1,0:T(2,128)S(1)}, u32[]{:S(2)}, u32[]{:S(2)}) collective-permute-start(s32[4,2,512]{2,1,0:T(2,128)S(1)} %pad_add_fusion.2), channel_id=1, source_target_pairs={{0,8},{1,9},{2,10},{3,11},{4,12},{5,13},{6,14},{7,15},{8,0},{9,1},... | collective-permute-start | bytes 49160 | tf_op jit(solution)/shard_map/ppermute | solution.py:735
  13.6 3.7 %pack_rows.1 = bf16[8,256,384]{2,1,0:T(8,128)(2,1)} custom-call(s32[1,256]{1,0:T(1,128)} %bitcast.14, bf16[256,1024]{1,0:T(8,128)(2,1)} %q_ref.1, bf16[256,1024]{1,0:T(8,128)(2,1)} %k_ref.1, bf16[256,1024]{1,0:T(8,128)(2,1)} %v_ref.1), custom_call_target="tpu_custom_call" | custom-call | tf_op jit(solution)/shard_map/pack_rows/pallas_call | solution.py:71
  17.3 4.3 %all-to-all-start = ((bf16[8,256,384]{2,1,0:T(8,128)(2,1)}), bf16[8,256,384]{2,1,0:T(8,128)(2,1)S(1)}, u32[]{:S(2)}, u32[]{:S(2)}) async-start(bf16[8,256,384]{2,1,0:T(8,128)(2,1)} %pack_rows.1), calls=%async_computation | async-start | bytes 3145728 | tf_op jit(solution)/shard_map/all_to_all | solution.py:738
  24.1 9.8 %make_plan.1 = (s32[96,16]{1,0:T(8,128)}, s32[16,1,768]{2,1,0:T(1,128)}, s32[16,1,512]{2,1,0:T(1,128)}, f32[16,144,256]{2,1,0:T(8,128)}) custom-call(f32[16]{0:T(128)} %dynamic-slice_bitcast_fusion.bias.levels, s32[16,2,512]{2,1,0:T(2,128)} %pad_add_fusion.meta_ref), custom_call_target="tpu_custom_call" | custom-call | tf_op jit(solution)/shard_map/make_plan/pallas_call | solution.py:200
  33.9 21.9 %all-to-all-done.refs_0_ = bf16[8,256,384]{2,1,0:T(8,128)(2,1)S(1)} async-done(((bf16[8,256,384]{2,1,0:T(8,128)(2,1)}), bf16[8,256,384]{2,1,0:T(8,128)(2,1)S(1)}, u32[]{:S(2)}, u32[]{:S(2)}) %all-to-all-start) | async-done | bytes 1572896 | tf_op jit(solution)/shard_map/all_to_all | solution.py:738
  55.8 3.4 %collective-permute-done.4.refs_1_ = bf16[8,256,384]{2,1,0:T(8,128)(2,1)S(1)} collective-permute-done((bf16[8,256,384]{2,1,0:T(8,128)(2,1)S(1)}, bf16[8,256,384]{2,1,0:T(8,128)(2,1)S(1)}, u32[]{:S(2)}, u32[]{:S(2)}) %collective-permute-start.4) | collective-permute-done | bytes 1572896 | tf_op jit(solution)/shard_map/ppermute | solution.py:735
  60.4 16.1 %attend_forward.1 = (bf16[8,256,128]{2,1,0:T(8,128)(2,1)}, bf16[16,256,128]{2,1,0:T(8,128)(2,1)}, bf16[16,512,256]{2,1,0:T(8,128)(2,1)}) custom-call(s32[96,16]{1,0:T(8,128)} %get-tuple-element.34.plan_ref, f32[16]{0:T(128)} %dynamic-slice_bitcast_fusion.bias.levels, s32[16,1,768]{2,1,0:T(1,128)} %get-tuple-element.35.place_ref, ...), custom_call_target="tpu_custom_call" | custom-call | tf_op jit(solution)/shard_map/attend_forward/pallas_call | solution.py:361
  76.4 3.7 %all-to-all-start.1 = ((bf16[8,256,128]{2,1,0:T(8,128)(2,1)}), bf16[8,256,128]{2,1,0:T(8,128)(2,1)S(1)}, u32[]{:S(2)}, u32[]{:S(2)}) async-start(bf16[8,256,128]{2,1,0:T(8,128)(2,1)} %get-tuple-element.39), calls=%async_computation.1 | async-start | bytes 1048576 | tf_op jit(solution)/shard_map/all_to_all | solution.py:738
  80.1 3.3 %convolution_convert_fusion.1.grad_ref = bf16[256,1024]{1,0:T(8,128)(2,1)} fusion(bf16[256,1024]{1,0:T(8,128)(2,1)} %refs_2_.1, bf16[1024,1024]{1,0:T(8,128)(2,1)} %param.15), kind=kOutput, calls=%fused_computation.3 | convolution fusion | flops 537133056 | bytes 3145728 | tf_op jit(solution)/shard_map/dot_general | solution.py:768
  83.4 11.5 %all-to-all-done.1.parts = bf16[8,256,128]{2,1,0:T(8,128)(2,1)S(1)} async-done(((bf16[8,256,128]{2,1,0:T(8,128)(2,1)}), bf16[8,256,128]{2,1,0:T(8,128)(2,1)S(1)}, u32[]{:S(2)}, u32[]{:S(2)}) %all-to-all-start.1) | async-done | bytes 524320 | tf_op jit(solution)/shard_map/all_to_all | solution.py:738
  95.7 3.9 %norm_gate.1 = (bf16[256,1024]{1,0:T(8,128)(2,1)}, bf16[256,1024]{1,0:T(8,128)(2,1)}, bf16[8,256,128]{2,1,0:T(8,128)(2,1)}) custom-call(s32[1,256]{1,0:T(1,128)} %bitcast.15, bf16[256,1024]{1,0:T(8,128)(2,1)} %gate_ref.1, bf16[256,1024]{1,0:T(8,128)(2,1)} %convolution_convert_fusion.1.grad_ref, bf16[8,256,128]{2,1,0:T(8,128)(2,1)} %copy-done.6), custom_call_target="tpu_custom_call" | custom-call | tf_op jit(solution)/shard_map/norm_gate/pallas_call | solution.py:421
  99.6 3.6 %all-to-all-start.2 = ((bf16[8,256,128]{2,1,0:T(8,128)(2,1)}), bf16[8,256,128]{2,1,0:T(8,128)(2,1)S(1)}, u32[]{:S(2)}, u32[]{:S(2)}) async-start(bf16[8,256,128]{2,1,0:T(8,128)(2,1)} %get-tuple-element.43), calls=%async_computation.2 | async-start | bytes 1048576 | tf_op jit(solution)/shard_map/all_to_all | solution.py:738
  106.3 3.8 %weight_parts.1 = bf16[8,64,1024]{2,1,0:T(8,128)(2,1)} custom-call(s32[1]{0:T(128)} %bitcast.6.at, bf16[256,1024]{1,0:T(8,128)(2,1)} %get-tuple-element.40.refs_0_, bf16[256,1024]{1,0:T(8,128)(2,1)} %collective-permute-done.5.refs_1_, bf16[256,1024]{1,0:T(8,128)(2,1)} %refs_2_.1, bf16[256,1024]{1,0:T(8,128)(2,1)} %copy-done.10), custom_call_target="tpu_custom_call" | custom-call | tf_op jit(solution)/shard_map/weight_parts/pallas_call | solution.py:664
  110.1 7.8 %all-to-all-done.2.grad_ref = bf16[8,256,128]{2,1,0:T(8,128)(2,1)S(1)} async-done(((bf16[8,256,128]{2,1,0:T(8,128)(2,1)}), bf16[8,256,128]{2,1,0:T(8,128)(2,1)S(1)}, u32[]{:S(2)}, u32[]{:S(2)}) %all-to-all-start.2) | async-done | bytes 524320 | tf_op jit(solution)/shard_map/all_to_all | solution.py:738
  117.9 3.6 %all-to-all-start.4 = ((bf16[8,64,1024]{2,1,0:T(8,128)(2,1)}), bf16[8,64,1024]{2,1,0:T(8,128)(2,1)S(1)}, u32[]{:S(2)}, u32[]{:S(2)}) async-start(bf16[8,64,1024]{2,1,0:T(8,128)(2,1)} %weight_parts.1), calls=%async_computation.4 | async-start | bytes 2097152 | tf_op jit(solution)/shard_map/all_to_all | solution.py:738
  121.6 26.5 %attend_backward.1 = (bf16[8,256,128]{2,1,0:T(8,128)(2,1)}, f32[1,128]{1,0:T(1,128)}, bf16[8,256,256]{2,1,0:T(8,128)(2,1)}, bf16[8,256,256]{2,1,0:T(8,128)(2,1)}) custom-call(s32[96,16]{1,0:T(8,128)} %get-tuple-element.34.plan_ref, f32[16]{0:T(128)} %dynamic-slice_bitcast_fusion.bias.levels, s32[16,1,768]{2,1,0:T(1,128)} %get-tuple-element.35.place_ref, ...), custom_call_target="tpu_custom_call" | custom-call | tf_op jit(solution)/shard_map/attend_backward/pallas_call | solution.py:582
  148.6 1.9 collective-permute-done.7
  151.7 3.2 %join_rows.1 = bf16[8,264,384]{2,1,0:T(8,128)(2,1)} custom-call(bf16[8,256,128]{2,1,0:T(8,128)(2,1)} %get-tuple-element.45.q_ref, bf16[8,256,256]{2,1,0:T(8,128)(2,1)} %get-tuple-element.46.own_ref, f32[1,128]{1,0:T(1,128)} %add.43.sum_ref, bf16[8,256,256]{2,1,0:T(8,128)(2,1)} %collective-permute-done.8.refs_0_), custom_call_target="tpu_custom_call" | custom-call | tf_op jit(solution)/shard_map/join_rows/pallas_call | solution.py:634
  155.8 6.0 %all-to-all-start.3 = ((bf16[8,264,384]{2,1,0:T(8,128)(2,1)}), bf16[8,264,384]{2,1,0:T(8,128)(2,1)S(1)}, u32[]{:S(2)}, u32[]{:S(2)}) async-start(bf16[8,264,384]{2,1,0:T(8,128)(2,1)} %join_rows.1), calls=%async_computation.3 | async-start | bytes 3244032 | tf_op jit(solution)/shard_map/all_to_all | solution.py:738
  161.8 3.2 %convolution_convert_fusion = bf16[256,1024]{1,0:T(8,128)(2,1)} fusion(bf16[256,1024]{1,0:T(8,128)(2,1)S(1)} %copy-done.9, bf16[1024,1024]{1,0:T(8,128)(2,1)} %param.15), kind=kOutput, calls=%fused_computation.2 | convolution fusion | flops 537133056 | bytes 3145728 | tf_op jit(solution)/shard_map/dot_general | solution.py:779
  165.9 34.4 %all-to-all-done.3.pack_ref = bf16[8,264,384]{2,1,0:T(8,128)(2,1)S(1)} async-done(((bf16[8,264,384]{2,1,0:T(8,128)(2,1)}), bf16[8,264,384]{2,1,0:T(8,128)(2,1)S(1)}, u32[]{:S(2)}, u32[]{:S(2)}) %all-to-all-start.3) | async-done | bytes 1622048 | tf_op jit(solution)/shard_map/all_to_all | solution.py:738
  201.6 3.6 %unpack_rows.1 = (bf16[256,1024]{1,0:T(8,128)(2,1)}, bf16[256,1024]{1,0:T(8,128)(2,1)}, bf16[256,1024]{1,0:T(8,128)(2,1)}, f32[16,8]{1,0:T(8,128)}) custom-call(s32[1,256]{1,0:T(1,128)} %bitcast.16, bf16[8,264,384]{2,1,0:T(8,128)(2,1)} %copy-done.1), custom_call_target="tpu_custom_call" | custom-call | tf_op jit(solution)/shard_map/unpack_rows/pallas_call | solution.py:697
  (51 shorter events, 18.5 us)
Async XLA Ops:
  0.6 21.6 %copy-start = (f32[16,8]{0,1:T(8,128)S(1)}, f32[16,8]{0,1:T(8,128)}, u32[]{:S(2)}) copy-start(f32[16,8]{0,1:T(8,128)} %param.16) | copy-start | bytes 1540
  2.2 4.6 %collective-permute-start = (s32[1,2,512]{2,1,0:T(2,128)S(1)}, s32[1,2,512]{2,1,0:T(2,128)S(1)}, u32[]{:S(2)}, u32[]{:S(2)}) collective-permute-start(s32[1,2,512]{2,1,0:T(2,128)S(1)} %add_bitcast_fusion), channel_id=1, source_target_pairs={{0,2},{1,3},{2,0},{3,1},{4,6},{5,7},{6,4},{7,5},{8,10},{9,11},{10,... | collective-permute-start | bytes 12296 | tf_op jit(solution)/shard_map/ppermute | solution.py:735
  6.9 3.7 %collective-permute-start.1 = (s32[2,2,512]{2,1,0:T(2,128)S(1)}, s32[2,2,512]{2,1,0:T(2,128)S(1)}, u32[]{:S(2)}, u32[]{:S(2)}) collective-permute-start(s32[2,2,512]{2,1,0:T(2,128)S(1)} %pad_add_fusion.3), channel_id=1, source_target_pairs={{0,4},{1,5},{2,6},{3,7},{4,0},{5,1},{6,2},{7,3},{8,12},{9,13},{10,... | collective-permute-start | bytes 24584 | tf_op jit(solution)/shard_map/ppermute | solution.py:735
  10.6 6.7 %collective-permute-start.2 = (s32[4,2,512]{2,1,0:T(2,128)S(1)}, s32[4,2,512]{2,1,0:T(2,128)S(1)}, u32[]{:S(2)}, u32[]{:S(2)}) collective-permute-start(s32[4,2,512]{2,1,0:T(2,128)S(1)} %pad_add_fusion.2), channel_id=1, source_target_pairs={{0,8},{1,9},{2,10},{3,11},{4,12},{5,13},{6,14},{7,15},{8,0},{9,1},... | collective-permute-start | bytes 49160 | tf_op jit(solution)/shard_map/ppermute | solution.py:735
  17.3 38.5 %all-to-all-start = ((bf16[8,256,384]{2,1,0:T(8,128)(2,1)}), bf16[8,256,384]{2,1,0:T(8,128)(2,1)S(1)}, u32[]{:S(2)}, u32[]{:S(2)}) async-start(bf16[8,256,384]{2,1,0:T(8,128)(2,1)} %pack_rows.1), calls=%async_computation | async-start | bytes 3145728 | tf_op jit(solution)/shard_map/all_to_all | solution.py:738
  22.2 1.3 collective-permute-start.3
  55.7 4.6 %copy-start.2 = (bf16[8,256,384]{2,1,0:T(8,128)(2,1)}, bf16[8,256,384]{2,1,0:T(8,128)(2,1)S(1)}, u32[]{:S(2)}) copy-start(bf16[8,256,384]{2,1,0:T(8,128)(2,1)S(1)} %all-to-all-done.refs_0_) | copy-start | bytes 4718596
  55.7 3.4 %collective-permute-start.4 = (bf16[8,256,384]{2,1,0:T(8,128)(2,1)S(1)}, bf16[8,256,384]{2,1,0:T(8,128)(2,1)S(1)}, u32[]{:S(2)}, u32[]{:S(2)}) collective-permute-start(bf16[8,256,384]{2,1,0:T(8,128)(2,1)S(1)} %all-to-all-done.refs_0_), channel_id=1, source_target_pairs={{0,1},{1,0},{2,3},{3,2},{4,5},{5,4},{6,7},{7,6},{8,9},{9,8},{10,11... | collective-permute-start | bytes 4718600 | tf_op jit(solution)/shard_map/ppermute | solution.py:735
  59.2 1.2 copy-start.7
  76.4 18.5 %all-to-all-start.1 = ((bf16[8,256,128]{2,1,0:T(8,128)(2,1)}), bf16[8,256,128]{2,1,0:T(8,128)(2,1)S(1)}, u32[]{:S(2)}, u32[]{:S(2)}) async-start(bf16[8,256,128]{2,1,0:T(8,128)(2,1)} %get-tuple-element.39), calls=%async_computation.1 | async-start | bytes 1048576 | tf_op jit(solution)/shard_map/all_to_all | solution.py:738
  83.4 19.8 %copy-start.8 = (bf16[256,1024]{1,0:T(8,128)(2,1)S(1)}, bf16[256,1024]{1,0:T(8,128)(2,1)}, u32[]{:S(2)}) copy-start(bf16[256,1024]{1,0:T(8,128)(2,1)} %refs_2_.1) | copy-start | bytes 1572868
  99.6 18.3 %all-to-all-start.2 = ((bf16[8,256,128]{2,1,0:T(8,128)(2,1)}), bf16[8,256,128]{2,1,0:T(8,128)(2,1)S(1)}, u32[]{:S(2)}, u32[]{:S(2)}) async-start(bf16[8,256,128]{2,1,0:T(8,128)(2,1)} %get-tuple-element.43), calls=%async_computation.2 | async-start | bytes 1048576 | tf_op jit(solution)/shard_map/all_to_all | solution.py:738
  103.2 2.0 collective-permute-start.6
  103.3 3.0 %collective-permute-start.5 = (bf16[256,1024]{1,0:T(8,128)(2,1)}, bf16[256,1024]{1,0:T(8,128)(2,1)}, u32[]{:S(2)}, u32[]{:S(2)}) collective-permute-start(bf16[256,1024]{1,0:T(8,128)(2,1)} %get-tuple-element.40.refs_0_), channel_id=1, source_target_pairs={{0,1},{1,0},{2,3},{3,2},{4,5},{5,4},{6,7},{7,6},{8,9},{9,8},{10,11... | collective-permute-start | bytes 1572872 | tf_op jit(solution)/shard_map/ppermute | solution.py:735
  105.2 1.1 copy-start.10
  117.9 3.6 %copy-start.5 = (bf16[8,256,128]{2,1,0:T(8,128)(2,1)}, bf16[8,256,128]{2,1,0:T(8,128)(2,1)S(1)}, u32[]{:S(2)}) copy-start(bf16[8,256,128]{2,1,0:T(8,128)(2,1)S(1)} %all-to-all-done.2.grad_ref) | copy-start | bytes 1572868
  117.9 36.9 %all-to-all-start.4 = ((bf16[8,64,1024]{2,1,0:T(8,128)(2,1)}), bf16[8,64,1024]{2,1,0:T(8,128)(2,1)S(1)}, u32[]{:S(2)}, u32[]{:S(2)}) async-start(bf16[8,64,1024]{2,1,0:T(8,128)(2,1)} %weight_parts.1), calls=%async_computation.4 | async-start | bytes 2097152 | tf_op jit(solution)/shard_map/all_to_all | solution.py:738
  148.1 3.6 %collective-permute-start.8 = (bf16[8,256,256]{2,1,0:T(8,128)(2,1)}, bf16[8,256,256]{2,1,0:T(8,128)(2,1)}, u32[]{:S(2)}, u32[]{:S(2)}) collective-permute-start(bf16[8,256,256]{2,1,0:T(8,128)(2,1)} %get-tuple-element.48), channel_id=1, source_target_pairs={{0,1},{1,0},{2,3},{3,2},{4,5},{5,4},{6,7},{7,6},{8,9},{9,8},{10,11... | collective-permute-start | bytes 3145736 | tf_op jit(solution)/shard_map/ppermute | solution.py:735
  148.1 2.4 %collective-permute-start.7 = (f32[1,128]{1,0:T(1,128)}, f32[1,128]{1,0:T(1,128)S(1)}, u32[]{:S(2)}, u32[]{:S(2)}) collective-permute-start(f32[1,128]{1,0:T(1,128)} %get-tuple-element.47), channel_id=1, source_target_pairs={{0,1},{1,0},{2,3},{3,2},{4,5},{5,4},{6,7},{7,6},{8,9},{9,8},{10,11... | collective-permute-start | bytes 1544 | tf_op jit(solution)/shard_map/ppermute | solution.py:735
  154.8 7.0 %copy-start.9 = (bf16[256,1024]{1,0:T(8,128)(2,1)S(1)}, bf16[256,1024]{1,0:T(8,128)(2,1)}, u32[]{:S(2)}) copy-start(bf16[256,1024]{1,0:T(8,128)(2,1)} %get-tuple-element.40.refs_0_) | copy-start | bytes 1572868
  154.8 1.0 copy-start.3
  155.8 44.6 %all-to-all-start.3 = ((bf16[8,264,384]{2,1,0:T(8,128)(2,1)}), bf16[8,264,384]{2,1,0:T(8,128)(2,1)S(1)}, u32[]{:S(2)}, u32[]{:S(2)}) async-start(bf16[8,264,384]{2,1,0:T(8,128)(2,1)} %join_rows.1), calls=%async_computation.3 | async-start | bytes 3244032 | tf_op jit(solution)/shard_map/all_to_all | solution.py:738
  161.8 3.2 %copy-start.4 = (bf16[8,64,1024]{2,1,0:T(8,128)(2,1)S(1)}, bf16[8,64,1024]{2,1,0:T(8,128)(2,1)}, u32[]{:S(2)}) copy-start(bf16[8,64,1024]{2,1,0:T(8,128)(2,1)} %copy-done.3) | copy-start | bytes 3145732
  200.4 1.2 copy-start.1
  (1 other events, 0.8 us)

commit v4 on v3

--- a/solution.py
+++ b/solution.py
@@ -32,7 +32,7 @@
 def params(steps=0):
     semantics = ("arbitrary",) * steps if steps else None
     return pltpu.CompilerParams(
-        dimension_semantics=semantics, vmem_limit_bytes=62 << 20
+        dimension_semantics=semantics, vmem_limit_bytes=63 << 20
     )
 
 
@@ -613,9 +613,11 @@
     head_count, tokens, size = queries.shape
     pair = 2 * size
 
-    def body(q_ref, own_ref, sum_ref, *refs):
+    def body(q_ref, own_ref, *refs):
         out_ref = refs[-1]
-        rest = sum_ref[...]
+        rest = refs[0][...]
+        for ref in refs[1 : len(head_sums)]:
+            rest = rest + ref[...]
         row = lax.broadcasted_iota(i32, (8, 128), 0)
         extra = jnp.zeros((8, 128), f32)
         for digit in range(3):
@@ -624,7 +626,7 @@
             extra = jnp.where(row == digit, rounded, extra)
         for h in range(head_count):
             total = own_ref[h].astype(f32)
-            for ref in refs[:-1]:
+            for ref in refs[len(head_sums) : -1]:
                 total = total + ref[h].astype(f32)
             out_ref[h, :tokens, :pair] = total.astype(bf16)
             out_ref[h, :tokens, pair:] = q_ref[h]
@@ -634,13 +636,14 @@
     return pl.pallas_call(
         body,
         grid=(1,),
-        in_specs=[vmem_spec(queries.shape), pair_spec, vmem_spec(head_sums.shape)]
+        in_specs=[vmem_spec(queries.shape), pair_spec]
+        + [vmem_spec(x.shape) for x in head_sums]
         + [pair_spec] * len(arrived),
         out_specs=vmem_spec((head_count, tokens + 8, 3 * size)),
         out_shape=shaped((head_count, tokens + 8, 3 * size), bf16),
         compiler_params=params(1),
         name="join_rows",
-    )(queries, own, head_sums, *arrived)
+    )(queries, own, *head_sums, *arrived)
 
 
 def weight_parts(sibling, fresh_list, grad_list, piece, head_count, factor):
@@ -692,11 +695,11 @@
             q_out[:, cols] = dot(unsort, pack_ref[h, :tokens, 2 * size :]).astype(bf16)
             digits = pack_ref[h, tokens:, :128].astype(f32)
             gathered.append(digits[0:1] + digits[1:2] + digits[2:3])
-        bias_out[...] = jnp.transpose(jnp.concatenate(gathered, axis=0))[:buckets, :]
+        bias_out[...] = jnp.concatenate(gathered, axis=0)[:, :buckets]
 
     return pl.pallas_call(
         body,
-        out_shape=[shaped((tokens, width), bf16)] * 3 + [shaped((buckets, head_count), f32)],
+        out_shape=[shaped((tokens, width), bf16)] * 3 + [shaped((head_count, buckets), f32)],
         compiler_params=params(),
         name="unpack_rows",
     )(slot_row, packs)
@@ -785,12 +788,15 @@
         plan, head_bias, place, bias, codes, sorted_query, sorted_pair, grads, window, ranks, grad_scale
     )
     other = [flip(pair_back[m], m) for m in range(1, siblings)]
+    head_sums = [head_sums]
     mask = 1
     while mask < siblings:
-        head_sums = head_sums + flip(head_sums, mask)
+        head_sums = [sum(head_sums)]
+        head_sums.append(flip(head_sums[0], mask))
         mask *= 2
     joined = join_rows(query_back, pair_back[0], other, head_sums)
-    query_grad, key_grad, value_grad, bias_grad = unpack_rows(slot_row, exchange(joined), buckets)
+    query_grad, key_grad, value_grad, bias_rows = unpack_rows(slot_row, exchange(joined), buckets)
+    bias_grad = jnp.transpose(bias_rows)
     return (layer_out, query_grad, key_grad, value_grad, gate_grad, weight_grad, bias_grad)
 
 

time: 207 us -> 202 us (0.976)
  local copies, waits for them, and re-layouts: 6.68 us -> 1.93 us
  waiting for transfers between devices: 87.3 us -> 89.5 us
    unnamed x23 -> x12, local copies, waits for them, and re-layouts: 5.57 us -> 0.82 us
  transfers between devices with their start and end apart: 14 -> 14, of which waited for: 11 -> 12; matrix products, arithmetic and copies ran while one was open for 5% -> 4% of each run, Pallas kernels for 23% -> 23%
where the time goes in v4:
time: 202 us; the launch traced here: 203 us
  waiting for transfers between devices  89.5 us (44%)
  Pallas kernels  70.6 us (35%)
  starting transfers between devices  31.1 us (15%)
  matrix products  4.82 us (2%)
  other arithmetic  4.35 us (2%)
    all_to_all x5, waiting for transfers between devices, exchange(): lax.all_to_all(parts, 'ctx', 0, 0, axis_index_groups=teams, tiled=True)  76.8 us
    pallas_call x1, Pallas kernels, attend_backward(): pl.pallas_call(body, grid_spec=pltpu.PrefetchScalarGridSpec(num_scalar_pr...  26.5 us
    all_to_all x5, starting transfers between devices, exchange(): lax.all_to_all(parts, 'ctx', 0, 0, axis_index_groups=teams, tiled=True)  21.9 us
    pallas_call x1, Pallas kernels, attend_forward(): pl.pallas_call(body, grid_spec=pltpu.PrefetchScalarGridSpec(num_scalar_pr...  16.1 us
    ppermute x9, waiting for transfers between devices, flip(): return lax.ppermute(array, 'ctx', [(i, i ^ mask) for i in range(ranks)])  12.6 us
    pallas_call x1, Pallas kernels, make_plan(): pl.pallas_call(body, grid_spec=pltpu.PrefetchScalarGridSpec(num_scalar_pr...  9.77 us
    ppermute x9, starting transfers between devices, flip(): return lax.ppermute(array, 'ctx', [(i, i ^ mask) for i in range(ranks)])  9.24 us
  transfers between devices with their start and end apart: 14, of which 12 were waited for; matrix products, arithmetic and copies ran while one was open for 4% of the time, Pallas kernels for 23%

profile of v4, /device:TPU:0, one launch (start us, length us, event | category | flops | bytes accessed | tf_op | source)
XLA Modules:
  0.0 203.0 jit_solution(7342855500072163003)
XLA Ops:
  2.2 3.0 %collective-permute-start = (s32[1,2,512]{2,1,0:T(2,128)S(1)}, s32[1,2,512]{2,1,0:T(2,128)S(1)}, u32[]{:S(2)}, u32[]{:S(2)}) collective-permute-start(s32[1,2,512]{2,1,0:T(2,128)S(1)} %add_bitcast_fusion), channel_id=1, source_target_pairs={{0,2},{1,3},{2,0},{3,1},{4,6},{5,7},{6,4},{7,5},{8,10},{9,11},{10,... | collective-permute-start | bytes 12296 | tf_op jit(solution)/shard_map/ppermute | solution.py:738
  6.9 2.1 %collective-permute-start.1 = (s32[2,2,512]{2,1,0:T(2,128)S(1)}, s32[2,2,512]{2,1,0:T(2,128)S(1)}, u32[]{:S(2)}, u32[]{:S(2)}) collective-permute-start(s32[2,2,512]{2,1,0:T(2,128)S(1)} %pad_add_fusion.3), channel_id=1, source_target_pairs={{0,4},{1,5},{2,6},{3,7},{4,0},{5,1},{6,2},{7,3},{8,12},{9,13},{10,... | collective-permute-start | bytes 24584 | tf_op jit(solution)/shard_map/ppermute | solution.py:738
  10.6 3.0 %collective-permute-start.2 = (s32[4,2,512]{2,1,0:T(2,128)S(1)}, s32[4,2,512]{2,1,0:T(2,128)S(1)}, u32[]{:S(2)}, u32[]{:S(2)}) collective-permute-start(s32[4,2,512]{2,1,0:T(2,128)S(1)} %pad_add_fusion.2), channel_id=1, source_target_pairs={{0,8},{1,9},{2,10},{3,11},{4,12},{5,13},{6,14},{7,15},{8,0},{9,1},... | collective-permute-start | bytes 49160 | tf_op jit(solution)/shard_map/ppermute | solution.py:738
  13.6 3.7 %pack_rows.1 = bf16[8,256,384]{2,1,0:T(8,128)(2,1)} custom-call(s32[1,256]{1,0:T(1,128)} %bitcast.15, bf16[256,1024]{1,0:T(8,128)(2,1)} %q_ref.1, bf16[256,1024]{1,0:T(8,128)(2,1)} %k_ref.1, bf16[256,1024]{1,0:T(8,128)(2,1)} %v_ref.1), custom_call_target="tpu_custom_call" | custom-call | tf_op jit(solution)/shard_map/pack_rows/pallas_call | solution.py:71
  17.3 4.3 %all-to-all-start = ((bf16[8,256,384]{2,1,0:T(8,128)(2,1)}), bf16[8,256,384]{2,1,0:T(8,128)(2,1)}, u32[]{:S(2)}, u32[]{:S(2)}) async-start(bf16[8,256,384]{2,1,0:T(8,128)(2,1)} %pack_rows.1), calls=%async_computation | async-start | bytes 3145728 | tf_op jit(solution)/shard_map/all_to_all | solution.py:741
  24.1 9.8 %make_plan.1 = (s32[96,16]{1,0:T(8,128)}, s32[16,1,768]{2,1,0:T(1,128)}, s32[16,1,512]{2,1,0:T(1,128)}, f32[16,144,256]{2,1,0:T(8,128)}) custom-call(f32[16]{0:T(128)} %dynamic-slice_bitcast_fusion.bias.levels, s32[16,2,512]{2,1,0:T(2,128)} %pad_add_fusion.meta_ref), custom_call_target="tpu_custom_call" | custom-call | tf_op jit(solution)/shard_map/make_plan/pallas_call | solution.py:200
  33.9 22.6 %all-to-all-done.refs_0_ = bf16[8,256,384]{2,1,0:T(8,128)(2,1)} async-done(((bf16[8,256,384]{2,1,0:T(8,128)(2,1)}), bf16[8,256,384]{2,1,0:T(8,128)(2,1)}, u32[]{:S(2)}, u32[]{:S(2)}) %all-to-all-start) | async-done | bytes 1572896 | tf_op jit(solution)/shard_map/all_to_all | solution.py:741
  56.5 3.7 %collective-permute-done.4.refs_1_ = bf16[8,256,384]{2,1,0:T(8,128)(2,1)} collective-permute-done((bf16[8,256,384]{2,1,0:T(8,128)(2,1)}, bf16[8,256,384]{2,1,0:T(8,128)(2,1)}, u32[]{:S(2)}, u32[]{:S(2)}) %collective-permute-start.4) | collective-permute-done | bytes 1572896 | tf_op jit(solution)/shard_map/ppermute | solution.py:738
  60.2 16.1 %attend_forward.1 = (bf16[8,256,128]{2,1,0:T(8,128)(2,1)}, bf16[16,256,128]{2,1,0:T(8,128)(2,1)}, bf16[16,512,256]{2,1,0:T(8,128)(2,1)}) custom-call(s32[96,16]{1,0:T(8,128)} %get-tuple-element.34.plan_ref, f32[16]{0:T(128)} %dynamic-slice_bitcast_fusion.bias.levels, s32[16,1,768]{2,1,0:T(1,128)} %get-tuple-element.35.place_ref, ...), custom_call_target="tpu_custom_call" | custom-call | tf_op jit(solution)/shard_map/attend_forward/pallas_call | solution.py:361
  76.3 3.7 %all-to-all-start.1 = ((bf16[8,256,128]{2,1,0:T(8,128)(2,1)}), bf16[8,256,128]{2,1,0:T(8,128)(2,1)S(1)}, u32[]{:S(2)}, u32[]{:S(2)}) async-start(bf16[8,256,128]{2,1,0:T(8,128)(2,1)} %get-tuple-element.39), calls=%async_computation.1 | async-start | bytes 1048576 | tf_op jit(solution)/shard_map/all_to_all | solution.py:741
  80.0 3.3 %convolution_convert_fusion.1.grad_ref = bf16[256,1024]{1,0:T(8,128)(2,1)} fusion(bf16[256,1024]{1,0:T(8,128)(2,1)} %refs_2_.1, bf16[1024,1024]{1,0:T(8,128)(2,1)} %param.15), kind=kOutput, calls=%fused_computation.3 | convolution fusion | flops 537133056 | bytes 3145728 | tf_op jit(solution)/shard_map/dot_general | solution.py:771
  83.3 11.5 %all-to-all-done.1.parts = bf16[8,256,128]{2,1,0:T(8,128)(2,1)S(1)} async-done(((bf16[8,256,128]{2,1,0:T(8,128)(2,1)}), bf16[8,256,128]{2,1,0:T(8,128)(2,1)S(1)}, u32[]{:S(2)}, u32[]{:S(2)}) %all-to-all-start.1) | async-done | bytes 524320 | tf_op jit(solution)/shard_map/all_to_all | solution.py:741
  95.6 3.9 %norm_gate.1 = (bf16[256,1024]{1,0:T(8,128)(2,1)}, bf16[256,1024]{1,0:T(8,128)(2,1)}, bf16[8,256,128]{2,1,0:T(8,128)(2,1)}) custom-call(s32[1,256]{1,0:T(1,128)} %bitcast.16, bf16[256,1024]{1,0:T(8,128)(2,1)} %gate_ref.1, bf16[256,1024]{1,0:T(8,128)(2,1)} %convolution_convert_fusion.1.grad_ref, bf16[8,256,128]{2,1,0:T(8,128)(2,1)} %copy-done.2), custom_call_target="tpu_custom_call" | custom-call | tf_op jit(solution)/shard_map/norm_gate/pallas_call | solution.py:421
  99.5 3.6 %all-to-all-start.2 = ((bf16[8,256,128]{2,1,0:T(8,128)(2,1)}), bf16[8,256,128]{2,1,0:T(8,128)(2,1)S(1)}, u32[]{:S(2)}, u32[]{:S(2)}) async-start(bf16[8,256,128]{2,1,0:T(8,128)(2,1)} %get-tuple-element.43), calls=%async_computation.2 | async-start | bytes 1048576 | tf_op jit(solution)/shard_map/all_to_all | solution.py:741
  106.1 3.8 %weight_parts.1 = bf16[8,64,1024]{2,1,0:T(8,128)(2,1)} custom-call(s32[1]{0:T(128)} %bitcast.6.at, bf16[256,1024]{1,0:T(8,128)(2,1)} %get-tuple-element.40.refs_0_, bf16[256,1024]{1,0:T(8,128)(2,1)} %collective-permute-done.5.refs_1_, bf16[256,1024]{1,0:T(8,128)(2,1)} %refs_2_.1, bf16[256,1024]{1,0:T(8,128)(2,1)} %collective-permute-done.6.refs_3_), custom_call_target="tpu_custom_call" | custom-call | tf_op jit(solution)/shard_map/weight_parts/pallas_call | solution.py:667
  109.9 7.9 %all-to-all-done.2.grad_ref = bf16[8,256,128]{2,1,0:T(8,128)(2,1)S(1)} async-done(((bf16[8,256,128]{2,1,0:T(8,128)(2,1)}), bf16[8,256,128]{2,1,0:T(8,128)(2,1)S(1)}, u32[]{:S(2)}, u32[]{:S(2)}) %all-to-all-start.2) | async-done | bytes 524320 | tf_op jit(solution)/shard_map/all_to_all | solution.py:741
  117.8 4.3 %all-to-all-start.4 = ((bf16[8,64,1024]{2,1,0:T(8,128)(2,1)}), bf16[8,64,1024]{2,1,0:T(8,128)(2,1)}, u32[]{:S(2)}, u32[]{:S(2)}) async-start(bf16[8,64,1024]{2,1,0:T(8,128)(2,1)} %weight_parts.1), calls=%async_computation.4 | async-start | bytes 2097152 | tf_op jit(solution)/shard_map/all_to_all | solution.py:741
  122.1 26.5 %attend_backward.1 = (bf16[8,256,128]{2,1,0:T(8,128)(2,1)}, f32[1,128]{1,0:T(1,128)}, bf16[8,256,256]{2,1,0:T(8,128)(2,1)}, bf16[8,256,256]{2,1,0:T(8,128)(2,1)}) custom-call(s32[96,16]{1,0:T(8,128)} %get-tuple-element.34.plan_ref, f32[16]{0:T(128)} %dynamic-slice_bitcast_fusion.bias.levels, s32[16,1,768]{2,1,0:T(1,128)} %get-tuple-element.35.place_ref, ...), custom_call_target="tpu_custom_call" | custom-call | tf_op jit(solution)/shard_map/attend_backward/pallas_call | solution.py:582
  149.1 1.9 collective-permute-done.7.refs_1_
  151.6 3.2 %join_rows.1 = bf16[8,264,384]{2,1,0:T(8,128)(2,1)} custom-call(bf16[8,256,128]{2,1,0:T(8,128)(2,1)} %get-tuple-element.45.q_ref, bf16[8,256,256]{2,1,0:T(8,128)(2,1)} %get-tuple-element.46.own_ref, f32[1,128]{1,0:T(1,128)} %get-tuple-element.47.refs_0_, f32[1,128]{1,0:T(1,128)} %copy-done.4, bf16[8,256,256]{2,1,0:T(8,128)(2,1)} %collective-permute-done.8.refs_2_), custom_call_target="tpu_custom_call" | custom-call | tf_op jit(solution)/shard_map/join_rows/pallas_call | solution.py:636
  154.7 6.0 %all-to-all-start.3 = ((bf16[8,264,384]{2,1,0:T(8,128)(2,1)}), bf16[8,264,384]{2,1,0:T(8,128)(2,1)}, u32[]{:S(2)}, u32[]{:S(2)}) async-start(bf16[8,264,384]{2,1,0:T(8,128)(2,1)} %join_rows.1), calls=%async_computation.3 | async-start | bytes 3244032 | tf_op jit(solution)/shard_map/all_to_all | solution.py:741
  162.3 2.1 %convert_reduce_fusion = f32[64,1024]{1,0:T(8,128)} fusion(bf16[8,64,1024]{2,1,0:T(8,128)(2,1)} %all-to-all-done.4), kind=kLoop, calls=%fused_computation.1 | loop fusion | flops 983040 | bytes 1310720 | tf_op jit(solution)/shard_map/reduce_sum | solution.py:785
  164.4 34.9 %all-to-all-done.3.pack_ref = bf16[8,264,384]{2,1,0:T(8,128)(2,1)} async-done(((bf16[8,264,384]{2,1,0:T(8,128)(2,1)}), bf16[8,264,384]{2,1,0:T(8,128)(2,1)}, u32[]{:S(2)}, u32[]{:S(2)}) %all-to-all-start.3) | async-done | bytes 1622048 | tf_op jit(solution)/shard_map/all_to_all | solution.py:741
  199.4 3.7 %unpack_rows.1 = (bf16[256,1024]{1,0:T(8,128)(2,1)}, bf16[256,1024]{1,0:T(8,128)(2,1)}, bf16[256,1024]{1,0:T(8,128)(2,1)}, f32[8,16]{1,0:T(8,128)}) custom-call(s32[1,256]{1,0:T(1,128)} %bitcast.17, bf16[8,264,384]{2,1,0:T(8,128)(2,1)} %all-to-all-done.3.pack_ref), custom_call_target="tpu_custom_call" | custom-call | tf_op jit(solution)/shard_map/unpack_rows/pallas_call | solution.py:700
  (39 shorter events, 13.7 us)
Async XLA Ops:
  0.6 21.7 %copy-start = (f32[16,8]{0,1:T(8,128)S(1)}, f32[16,8]{0,1:T(8,128)}, u32[]{:S(2)}) copy-start(f32[16,8]{0,1:T(8,128)} %param.16) | copy-start | bytes 1540
  2.2 4.6 %collective-permute-start = (s32[1,2,512]{2,1,0:T(2,128)S(1)}, s32[1,2,512]{2,1,0:T(2,128)S(1)}, u32[]{:S(2)}, u32[]{:S(2)}) collective-permute-start(s32[1,2,512]{2,1,0:T(2,128)S(1)} %add_bitcast_fusion), channel_id=1, source_target_pairs={{0,2},{1,3},{2,0},{3,1},{4,6},{5,7},{6,4},{7,5},{8,10},{9,11},{10,... | collective-permute-start | bytes 12296 | tf_op jit(solution)/shard_map/ppermute | solution.py:738
  6.9 3.7 %collective-permute-start.1 = (s32[2,2,512]{2,1,0:T(2,128)S(1)}, s32[2,2,512]{2,1,0:T(2,128)S(1)}, u32[]{:S(2)}, u32[]{:S(2)}) collective-permute-start(s32[2,2,512]{2,1,0:T(2,128)S(1)} %pad_add_fusion.3), channel_id=1, source_target_pairs={{0,4},{1,5},{2,6},{3,7},{4,0},{5,1},{6,2},{7,3},{8,12},{9,13},{10,... | collective-permute-start | bytes 24584 | tf_op jit(solution)/shard_map/ppermute | solution.py:738
  10.6 6.7 %collective-permute-start.2 = (s32[4,2,512]{2,1,0:T(2,128)S(1)}, s32[4,2,512]{2,1,0:T(2,128)S(1)}, u32[]{:S(2)}, u32[]{:S(2)}) collective-permute-start(s32[4,2,512]{2,1,0:T(2,128)S(1)} %pad_add_fusion.2), channel_id=1, source_target_pairs={{0,8},{1,9},{2,10},{3,11},{4,12},{5,13},{6,14},{7,15},{8,0},{9,1},... | collective-permute-start | bytes 49160 | tf_op jit(solution)/shard_map/ppermute | solution.py:738
  17.3 39.2 %all-to-all-start = ((bf16[8,256,384]{2,1,0:T(8,128)(2,1)}), bf16[8,256,384]{2,1,0:T(8,128)(2,1)}, u32[]{:S(2)}, u32[]{:S(2)}) async-start(bf16[8,256,384]{2,1,0:T(8,128)(2,1)} %pack_rows.1), calls=%async_computation | async-start | bytes 3145728 | tf_op jit(solution)/shard_map/all_to_all | solution.py:741
  22.2 1.3 collective-permute-start.3
  56.5 3.8 %collective-permute-start.4 = (bf16[8,256,384]{2,1,0:T(8,128)(2,1)}, bf16[8,256,384]{2,1,0:T(8,128)(2,1)}, u32[]{:S(2)}, u32[]{:S(2)}) collective-permute-start(bf16[8,256,384]{2,1,0:T(8,128)(2,1)} %all-to-all-done.refs_0_), channel_id=1, source_target_pairs={{0,1},{1,0},{2,3},{3,2},{4,5},{5,4},{6,7},{7,6},{8,9},{9,8},{10,11... | collective-permute-start | bytes 4718600 | tf_op jit(solution)/shard_map/ppermute | solution.py:738
  76.3 18.5 %all-to-all-start.1 = ((bf16[8,256,128]{2,1,0:T(8,128)(2,1)}), bf16[8,256,128]{2,1,0:T(8,128)(2,1)S(1)}, u32[]{:S(2)}, u32[]{:S(2)}) async-start(bf16[8,256,128]{2,1,0:T(8,128)(2,1)} %get-tuple-element.39), calls=%async_computation.1 | async-start | bytes 1048576 | tf_op jit(solution)/shard_map/all_to_all | solution.py:741
  94.8 0.8 copy-start.2
  99.5 18.3 %all-to-all-start.2 = ((bf16[8,256,128]{2,1,0:T(8,128)(2,1)}), bf16[8,256,128]{2,1,0:T(8,128)(2,1)S(1)}, u32[]{:S(2)}, u32[]{:S(2)}) async-start(bf16[8,256,128]{2,1,0:T(8,128)(2,1)} %get-tuple-element.43), calls=%async_computation.2 | async-start | bytes 1048576 | tf_op jit(solution)/shard_map/all_to_all | solution.py:741
  103.1 2.3 %collective-permute-start.6 = (bf16[256,1024]{1,0:T(8,128)(2,1)}, bf16[256,1024]{1,0:T(8,128)(2,1)}, u32[]{:S(2)}, u32[]{:S(2)}) collective-permute-start(bf16[256,1024]{1,0:T(8,128)(2,1)} %refs_2_.1), channel_id=1, source_target_pairs={{0,1},{1,0},{2,3},{3,2},{4,5},{5,4},{6,7},{7,6},{8,9},{9,8},{10,11... | collective-permute-start | bytes 1572872 | tf_op jit(solution)/shard_map/ppermute | solution.py:738
  103.1 3.0 %collective-permute-start.5 = (bf16[256,1024]{1,0:T(8,128)(2,1)}, bf16[256,1024]{1,0:T(8,128)(2,1)}, u32[]{:S(2)}, u32[]{:S(2)}) collective-permute-start(bf16[256,1024]{1,0:T(8,128)(2,1)} %get-tuple-element.40.refs_0_), channel_id=1, source_target_pairs={{0,1},{1,0},{2,3},{3,2},{4,5},{5,4},{6,7},{7,6},{8,9},{9,8},{10,11... | collective-permute-start | bytes 1572872 | tf_op jit(solution)/shard_map/ppermute | solution.py:738
  117.8 4.3 %copy-start.1 = (bf16[8,256,128]{2,1,0:T(8,128)(2,1)}, bf16[8,256,128]{2,1,0:T(8,128)(2,1)S(1)}, u32[]{:S(2)}) copy-start(bf16[8,256,128]{2,1,0:T(8,128)(2,1)S(1)} %all-to-all-done.2.grad_ref) | copy-start | bytes 1572868
  117.8 37.0 %all-to-all-start.4 = ((bf16[8,64,1024]{2,1,0:T(8,128)(2,1)}), bf16[8,64,1024]{2,1,0:T(8,128)(2,1)}, u32[]{:S(2)}, u32[]{:S(2)}) async-start(bf16[8,64,1024]{2,1,0:T(8,128)(2,1)} %weight_parts.1), calls=%async_computation.4 | async-start | bytes 2097152 | tf_op jit(solution)/shard_map/all_to_all | solution.py:741
  148.6 3.0 %collective-permute-start.8 = (bf16[8,256,256]{2,1,0:T(8,128)(2,1)}, bf16[8,256,256]{2,1,0:T(8,128)(2,1)}, u32[]{:S(2)}, u32[]{:S(2)}) collective-permute-start(bf16[8,256,256]{2,1,0:T(8,128)(2,1)} %get-tuple-element.48), channel_id=1, source_target_pairs={{0,1},{1,0},{2,3},{3,2},{4,5},{5,4},{6,7},{7,6},{8,9},{9,8},{10,11... | collective-permute-start | bytes 3145736 | tf_op jit(solution)/shard_map/ppermute | solution.py:738
  148.6 2.4 %collective-permute-start.7 = (f32[1,128]{1,0:T(1,128)}, f32[1,128]{1,0:T(1,128)S(1)}, u32[]{:S(2)}, u32[]{:S(2)}) collective-permute-start(f32[1,128]{1,0:T(1,128)} %get-tuple-element.47.refs_0_), channel_id=1, source_target_pairs={{0,1},{1,0},{2,3},{3,2},{4,5},{5,4},{6,7},{7,6},{8,9},{9,8},{10,11... | collective-permute-start | bytes 1544 | tf_op jit(solution)/shard_map/ppermute | solution.py:738
  151.0 0.6 copy-start.4
  154.7 6.0 %copy-start.3 = (bf16[256,1024]{1,0:T(8,128)(2,1)S(1)}, bf16[256,1024]{1,0:T(8,128)(2,1)}, u32[]{:S(2)}) copy-start(bf16[256,1024]{1,0:T(8,128)(2,1)} %get-tuple-element.40.refs_0_) | copy-start | bytes 1572868
  154.7 6.0 %copy-start.5 = (bf16[1024,1024]{1,0:T(8,128)(2,1)S(1)}, bf16[1024,1024]{1,0:T(8,128)(2,1)}, u32[]{:S(2)}) copy-start(bf16[1024,1024]{1,0:T(8,128)(2,1)} %param.15) | copy-start | bytes 6291460
  154.7 44.6 %all-to-all-start.3 = ((bf16[8,264,384]{2,1,0:T(8,128)(2,1)}), bf16[8,264,384]{2,1,0:T(8,128)(2,1)}, u32[]{:S(2)}, u32[]{:S(2)}) async-start(bf16[8,264,384]{2,1,0:T(8,128)(2,1)} %join_rows.1), calls=%async_computation.3 | async-start | bytes 3244032 | tf_op jit(solution)/shard_map/all_to_all | solution.py:741

commit v5 on v4

--- a/solution.py
+++ b/solution.py
@@ -443,7 +443,7 @@
     query_tile = cuts[0].stop
     scale = size ** (-0.5)
     near = head_count * window
-    batch = batch_of(owners)
+    batch = 2 if owners % 2 == 0 else 1
     groups = loaders // head_count
 
     def body(plan_ref, levels, place_ref, bias_ref, code_ref, qs_ref, kvs_ref, grad_ref, *refs):

time: 202 us -> 203 us (level); the launches traced: 203 us -> 200 us
  Pallas kernels: 70.6 us -> 67.7 us
where the time goes in v5:
time: 203 us; the launch traced here: 200 us
  waiting for transfers between devices  89.5 us (44%)
  Pallas kernels  67.7 us (33%)
  starting transfers between devices  31.1 us (15%)
  matrix products  4.82 us (2%)
  other arithmetic  4.35 us (2%)
    all_to_all x5, waiting for transfers between devices, exchange(): lax.all_to_all(parts, 'ctx', 0, 0, axis_index_groups=teams, tiled=True)  76.9 us
    pallas_call x1, Pallas kernels, attend_backward(): pl.pallas_call(body, grid_spec=pltpu.PrefetchScalarGridSpec(num_scalar_pr...  25.2 us
    all_to_all x5, starting transfers between devices, exchange(): lax.all_to_all(parts, 'ctx', 0, 0, axis_index_groups=teams, tiled=True)  21.9 us
    pallas_call x1, Pallas kernels, attend_forward(): pl.pallas_call(body, grid_spec=pltpu.PrefetchScalarGridSpec(num_scalar_pr...  14.6 us
    ppermute x9, waiting for transfers between devices, flip(): return lax.ppermute(array, 'ctx', [(i, i ^ mask) for i in range(ranks)])  12.6 us
    pallas_call x1, Pallas kernels, make_plan(): pl.pallas_call(body, grid_spec=pltpu.PrefetchScalarGridSpec(num_scalar_pr...  9.77 us
    ppermute x9, starting transfers between devices, flip(): return lax.ppermute(array, 'ctx', [(i, i ^ mask) for i in range(ranks)])  9.23 us
  transfers between devices with their start and end apart: 14, of which 12 were waited for; matrix products, arithmetic and copies ran while one was open for 4% of the time, Pallas kernels for 23%

profile of v5, /device:TPU:0, one launch (start us, length us, event | category | flops | bytes accessed | tf_op | source)
XLA Modules:
  0.0 200.2 jit_solution(12477052511185910359)
XLA Ops:
  2.2 3.0 %collective-permute-start = (s32[1,2,512]{2,1,0:T(2,128)S(1)}, s32[1,2,512]{2,1,0:T(2,128)S(1)}, u32[]{:S(2)}, u32[]{:S(2)}) collective-permute-start(s32[1,2,512]{2,1,0:T(2,128)S(1)} %add_bitcast_fusion), channel_id=1, source_target_pairs={{0,2},{1,3},{2,0},{3,1},{4,6},{5,7},{6,4},{7,5},{8,10},{9,11},{10,... | collective-permute-start | bytes 12296 | tf_op jit(solution)/shard_map/ppermute | solution.py:738
  6.9 2.1 %collective-permute-start.1 = (s32[2,2,512]{2,1,0:T(2,128)S(1)}, s32[2,2,512]{2,1,0:T(2,128)S(1)}, u32[]{:S(2)}, u32[]{:S(2)}) collective-permute-start(s32[2,2,512]{2,1,0:T(2,128)S(1)} %pad_add_fusion.3), channel_id=1, source_target_pairs={{0,4},{1,5},{2,6},{3,7},{4,0},{5,1},{6,2},{7,3},{8,12},{9,13},{10,... | collective-permute-start | bytes 24584 | tf_op jit(solution)/shard_map/ppermute | solution.py:738
  10.6 3.0 %collective-permute-start.2 = (s32[4,2,512]{2,1,0:T(2,128)S(1)}, s32[4,2,512]{2,1,0:T(2,128)S(1)}, u32[]{:S(2)}, u32[]{:S(2)}) collective-permute-start(s32[4,2,512]{2,1,0:T(2,128)S(1)} %pad_add_fusion.2), channel_id=1, source_target_pairs={{0,8},{1,9},{2,10},{3,11},{4,12},{5,13},{6,14},{7,15},{8,0},{9,1},... | collective-permute-start | bytes 49160 | tf_op jit(solution)/shard_map/ppermute | solution.py:738
  13.6 3.7 %pack_rows.1 = bf16[8,256,384]{2,1,0:T(8,128)(2,1)} custom-call(s32[1,256]{1,0:T(1,128)} %bitcast.15, bf16[256,1024]{1,0:T(8,128)(2,1)} %q_ref.1, bf16[256,1024]{1,0:T(8,128)(2,1)} %k_ref.1, bf16[256,1024]{1,0:T(8,128)(2,1)} %v_ref.1), custom_call_target="tpu_custom_call" | custom-call | tf_op jit(solution)/shard_map/pack_rows/pallas_call | solution.py:71
  17.3 4.3 %all-to-all-start = ((bf16[8,256,384]{2,1,0:T(8,128)(2,1)}), bf16[8,256,384]{2,1,0:T(8,128)(2,1)}, u32[]{:S(2)}, u32[]{:S(2)}) async-start(bf16[8,256,384]{2,1,0:T(8,128)(2,1)} %pack_rows.1), calls=%async_computation | async-start | bytes 3145728 | tf_op jit(solution)/shard_map/all_to_all | solution.py:741
  24.1 9.8 %make_plan.1 = (s32[96,16]{1,0:T(8,128)}, s32[16,1,768]{2,1,0:T(1,128)}, s32[16,1,512]{2,1,0:T(1,128)}, f32[16,144,256]{2,1,0:T(8,128)}) custom-call(f32[16]{0:T(128)} %dynamic-slice_bitcast_fusion.bias.levels, s32[16,2,512]{2,1,0:T(2,128)} %pad_add_fusion.meta_ref), custom_call_target="tpu_custom_call" | custom-call | tf_op jit(solution)/shard_map/make_plan/pallas_call | solution.py:200
  33.9 22.6 %all-to-all-done.refs_0_ = bf16[8,256,384]{2,1,0:T(8,128)(2,1)} async-done(((bf16[8,256,384]{2,1,0:T(8,128)(2,1)}), bf16[8,256,384]{2,1,0:T(8,128)(2,1)}, u32[]{:S(2)}, u32[]{:S(2)}) %all-to-all-start) | async-done | bytes 1572896 | tf_op jit(solution)/shard_map/all_to_all | solution.py:741
  56.5 3.7 %collective-permute-done.4.refs_1_ = bf16[8,256,384]{2,1,0:T(8,128)(2,1)} collective-permute-done((bf16[8,256,384]{2,1,0:T(8,128)(2,1)}, bf16[8,256,384]{2,1,0:T(8,128)(2,1)}, u32[]{:S(2)}, u32[]{:S(2)}) %collective-permute-start.4) | collective-permute-done | bytes 1572896 | tf_op jit(solution)/shard_map/ppermute | solution.py:738
  60.2 14.6 %attend_forward.1 = (bf16[8,256,128]{2,1,0:T(8,128)(2,1)}, bf16[16,256,128]{2,1,0:T(8,128)(2,1)}, bf16[16,512,256]{2,1,0:T(8,128)(2,1)}) custom-call(s32[96,16]{1,0:T(8,128)} %get-tuple-element.34.plan_ref, f32[16]{0:T(128)} %dynamic-slice_bitcast_fusion.bias.levels, s32[16,1,768]{2,1,0:T(1,128)} %get-tuple-element.35.place_ref, ...), custom_call_target="tpu_custom_call" | custom-call | tf_op jit(solution)/shard_map/attend_forward/pallas_call | solution.py:361
  74.8 3.7 %all-to-all-start.1 = ((bf16[8,256,128]{2,1,0:T(8,128)(2,1)}), bf16[8,256,128]{2,1,0:T(8,128)(2,1)S(1)}, u32[]{:S(2)}, u32[]{:S(2)}) async-start(bf16[8,256,128]{2,1,0:T(8,128)(2,1)} %get-tuple-element.39), calls=%async_computation.1 | async-start | bytes 1048576 | tf_op jit(solution)/shard_map/all_to_all | solution.py:741
  78.5 3.3 %convolution_convert_fusion.1.grad_ref = bf16[256,1024]{1,0:T(8,128)(2,1)} fusion(bf16[256,1024]{1,0:T(8,128)(2,1)} %refs_2_.1, bf16[1024,1024]{1,0:T(8,128)(2,1)} %param.15), kind=kOutput, calls=%fused_computation.3 | convolution fusion | flops 537133056 | bytes 3145728 | tf_op jit(solution)/shard_map/dot_general | solution.py:771
  81.8 11.5 %all-to-all-done.1.parts = bf16[8,256,128]{2,1,0:T(8,128)(2,1)S(1)} async-done(((bf16[8,256,128]{2,1,0:T(8,128)(2,1)}), bf16[8,256,128]{2,1,0:T(8,128)(2,1)S(1)}, u32[]{:S(2)}, u32[]{:S(2)}) %all-to-all-start.1) | async-done | bytes 524320 | tf_op jit(solution)/shard_map/all_to_all | solution.py:741
  94.1 3.9 %norm_gate.1 = (bf16[256,1024]{1,0:T(8,128)(2,1)}, bf16[256,1024]{1,0:T(8,128)(2,1)}, bf16[8,256,128]{2,1,0:T(8,128)(2,1)}) custom-call(s32[1,256]{1,0:T(1,128)} %bitcast.16, bf16[256,1024]{1,0:T(8,128)(2,1)} %gate_ref.1, bf16[256,1024]{1,0:T(8,128)(2,1)} %convolution_convert_fusion.1.grad_ref, bf16[8,256,128]{2,1,0:T(8,128)(2,1)} %copy-done.2), custom_call_target="tpu_custom_call" | custom-call | tf_op jit(solution)/shard_map/norm_gate/pallas_call | solution.py:421
  98.0 3.6 %all-to-all-start.2 = ((bf16[8,256,128]{2,1,0:T(8,128)(2,1)}), bf16[8,256,128]{2,1,0:T(8,128)(2,1)S(1)}, u32[]{:S(2)}, u32[]{:S(2)}) async-start(bf16[8,256,128]{2,1,0:T(8,128)(2,1)} %get-tuple-element.43), calls=%async_computation.2 | async-start | bytes 1048576 | tf_op jit(solution)/shard_map/all_to_all | solution.py:741
  104.6 3.8 %weight_parts.1 = bf16[8,64,1024]{2,1,0:T(8,128)(2,1)} custom-call(s32[1]{0:T(128)} %bitcast.6.at, bf16[256,1024]{1,0:T(8,128)(2,1)} %get-tuple-element.40.refs_0_, bf16[256,1024]{1,0:T(8,128)(2,1)} %collective-permute-done.5.refs_1_, bf16[256,1024]{1,0:T(8,128)(2,1)} %refs_2_.1, bf16[256,1024]{1,0:T(8,128)(2,1)} %collective-permute-done.6.refs_3_), custom_call_target="tpu_custom_call" | custom-call | tf_op jit(solution)/shard_map/weight_parts/pallas_call | solution.py:667
  108.4 7.9 %all-to-all-done.2.grad_ref = bf16[8,256,128]{2,1,0:T(8,128)(2,1)S(1)} async-done(((bf16[8,256,128]{2,1,0:T(8,128)(2,1)}), bf16[8,256,128]{2,1,0:T(8,128)(2,1)S(1)}, u32[]{:S(2)}, u32[]{:S(2)}) %all-to-all-start.2) | async-done | bytes 524320 | tf_op jit(solution)/shard_map/all_to_all | solution.py:741
  116.3 4.3 %all-to-all-start.4 = ((bf16[8,64,1024]{2,1,0:T(8,128)(2,1)}), bf16[8,64,1024]{2,1,0:T(8,128)(2,1)}, u32[]{:S(2)}, u32[]{:S(2)}) async-start(bf16[8,64,1024]{2,1,0:T(8,128)(2,1)} %weight_parts.1), calls=%async_computation.4 | async-start | bytes 2097152 | tf_op jit(solution)/shard_map/all_to_all | solution.py:741
  120.6 25.2 %attend_backward.1 = (bf16[8,256,128]{2,1,0:T(8,128)(2,1)}, f32[1,128]{1,0:T(1,128)}, bf16[8,256,256]{2,1,0:T(8,128)(2,1)}, bf16[8,256,256]{2,1,0:T(8,128)(2,1)}) custom-call(s32[96,16]{1,0:T(8,128)} %get-tuple-element.34.plan_ref, f32[16]{0:T(128)} %dynamic-slice_bitcast_fusion.bias.levels, s32[16,1,768]{2,1,0:T(1,128)} %get-tuple-element.35.place_ref, ...), custom_call_target="tpu_custom_call" | custom-call | tf_op jit(solution)/shard_map/attend_backward/pallas_call | solution.py:582
  146.3 1.9 collective-permute-done.7.refs_1_
  148.8 3.2 %join_rows.1 = bf16[8,264,384]{2,1,0:T(8,128)(2,1)} custom-call(bf16[8,256,128]{2,1,0:T(8,128)(2,1)} %get-tuple-element.45.q_ref, bf16[8,256,256]{2,1,0:T(8,128)(2,1)} %get-tuple-element.46.own_ref, f32[1,128]{1,0:T(1,128)} %get-tuple-element.47.refs_0_, f32[1,128]{1,0:T(1,128)} %copy-done.4, bf16[8,256,256]{2,1,0:T(8,128)(2,1)} %collective-permute-done.8.refs_2_), custom_call_target="tpu_custom_call" | custom-call | tf_op jit(solution)/shard_map/join_rows/pallas_call | solution.py:636
  152.0 6.0 %all-to-all-start.3 = ((bf16[8,264,384]{2,1,0:T(8,128)(2,1)}), bf16[8,264,384]{2,1,0:T(8,128)(2,1)}, u32[]{:S(2)}, u32[]{:S(2)}) async-start(bf16[8,264,384]{2,1,0:T(8,128)(2,1)} %join_rows.1), calls=%async_computation.3 | async-start | bytes 3244032 | tf_op jit(solution)/shard_map/all_to_all | solution.py:741
  159.5 2.1 %convert_reduce_fusion = f32[64,1024]{1,0:T(8,128)} fusion(bf16[8,64,1024]{2,1,0:T(8,128)(2,1)} %all-to-all-done.4), kind=kLoop, calls=%fused_computation.1 | loop fusion | flops 983040 | bytes 1310720 | tf_op jit(solution)/shard_map/reduce_sum | solution.py:785
  161.6 34.9 %all-to-all-done.3.pack_ref = bf16[8,264,384]{2,1,0:T(8,128)(2,1)} async-done(((bf16[8,264,384]{2,1,0:T(8,128)(2,1)}), bf16[8,264,384]{2,1,0:T(8,128)(2,1)}, u32[]{:S(2)}, u32[]{:S(2)}) %all-to-all-start.3) | async-done | bytes 1622048 | tf_op jit(solution)/shard_map/all_to_all | solution.py:741
  196.6 3.7 %unpack_rows.1 = (bf16[256,1024]{1,0:T(8,128)(2,1)}, bf16[256,1024]{1,0:T(8,128)(2,1)}, bf16[256,1024]{1,0:T(8,128)(2,1)}, f32[8,16]{1,0:T(8,128)}) custom-call(s32[1,256]{1,0:T(1,128)} %bitcast.17, bf16[8,264,384]{2,1,0:T(8,128)(2,1)} %all-to-all-done.3.pack_ref), custom_call_target="tpu_custom_call" | custom-call | tf_op jit(solution)/shard_map/unpack_rows/pallas_call | solution.py:700
  (39 shorter events, 13.7 us)
Async XLA Ops:
  0.6 21.7 %copy-start = (f32[16,8]{0,1:T(8,128)S(1)}, f32[16,8]{0,1:T(8,128)}, u32[]{:S(2)}) copy-start(f32[16,8]{0,1:T(8,128)} %param.16) | copy-start | bytes 1540
  2.2 4.6 %collective-permute-start = (s32[1,2,512]{2,1,0:T(2,128)S(1)}, s32[1,2,512]{2,1,0:T(2,128)S(1)}, u32[]{:S(2)}, u32[]{:S(2)}) collective-permute-start(s32[1,2,512]{2,1,0:T(2,128)S(1)} %add_bitcast_fusion), channel_id=1, source_target_pairs={{0,2},{1,3},{2,0},{3,1},{4,6},{5,7},{6,4},{7,5},{8,10},{9,11},{10,... | collective-permute-start | bytes 12296 | tf_op jit(solution)/shard_map/ppermute | solution.py:738
  6.9 3.7 %collective-permute-start.1 = (s32[2,2,512]{2,1,0:T(2,128)S(1)}, s32[2,2,512]{2,1,0:T(2,128)S(1)}, u32[]{:S(2)}, u32[]{:S(2)}) collective-permute-start(s32[2,2,512]{2,1,0:T(2,128)S(1)} %pad_add_fusion.3), channel_id=1, source_target_pairs={{0,4},{1,5},{2,6},{3,7},{4,0},{5,1},{6,2},{7,3},{8,12},{9,13},{10,... | collective-permute-start | bytes 24584 | tf_op jit(solution)/shard_map/ppermute | solution.py:738
  10.6 6.7 %collective-permute-start.2 = (s32[4,2,512]{2,1,0:T(2,128)S(1)}, s32[4,2,512]{2,1,0:T(2,128)S(1)}, u32[]{:S(2)}, u32[]{:S(2)}) collective-permute-start(s32[4,2,512]{2,1,0:T(2,128)S(1)} %pad_add_fusion.2), channel_id=1, source_target_pairs={{0,8},{1,9},{2,10},{3,11},{4,12},{5,13},{6,14},{7,15},{8,0},{9,1},... | collective-permute-start | bytes 49160 | tf_op jit(solution)/shard_map/ppermute | solution.py:738
  17.3 39.2 %all-to-all-start = ((bf16[8,256,384]{2,1,0:T(8,128)(2,1)}), bf16[8,256,384]{2,1,0:T(8,128)(2,1)}, u32[]{:S(2)}, u32[]{:S(2)}) async-start(bf16[8,256,384]{2,1,0:T(8,128)(2,1)} %pack_rows.1), calls=%async_computation | async-start | bytes 3145728 | tf_op jit(solution)/shard_map/all_to_all | solution.py:741
  22.2 1.3 collective-permute-start.3
  56.5 3.8 %collective-permute-start.4 = (bf16[8,256,384]{2,1,0:T(8,128)(2,1)}, bf16[8,256,384]{2,1,0:T(8,128)(2,1)}, u32[]{:S(2)}, u32[]{:S(2)}) collective-permute-start(bf16[8,256,384]{2,1,0:T(8,128)(2,1)} %all-to-all-done.refs_0_), channel_id=1, source_target_pairs={{0,1},{1,0},{2,3},{3,2},{4,5},{5,4},{6,7},{7,6},{8,9},{9,8},{10,11... | collective-permute-start | bytes 4718600 | tf_op jit(solution)/shard_map/ppermute | solution.py:738
  74.8 18.5 %all-to-all-start.1 = ((bf16[8,256,128]{2,1,0:T(8,128)(2,1)}), bf16[8,256,128]{2,1,0:T(8,128)(2,1)S(1)}, u32[]{:S(2)}, u32[]{:S(2)}) async-start(bf16[8,256,128]{2,1,0:T(8,128)(2,1)} %get-tuple-element.39), calls=%async_computation.1 | async-start | bytes 1048576 | tf_op jit(solution)/shard_map/all_to_all | solution.py:741
  93.3 0.8 copy-start.2
  98.0 18.3 %all-to-all-start.2 = ((bf16[8,256,128]{2,1,0:T(8,128)(2,1)}), bf16[8,256,128]{2,1,0:T(8,128)(2,1)S(1)}, u32[]{:S(2)}, u32[]{:S(2)}) async-start(bf16[8,256,128]{2,1,0:T(8,128)(2,1)} %get-tuple-element.43), calls=%async_computation.2 | async-start | bytes 1048576 | tf_op jit(solution)/shard_map/all_to_all | solution.py:741
  101.6 2.3 %collective-permute-start.6 = (bf16[256,1024]{1,0:T(8,128)(2,1)}, bf16[256,1024]{1,0:T(8,128)(2,1)}, u32[]{:S(2)}, u32[]{:S(2)}) collective-permute-start(bf16[256,1024]{1,0:T(8,128)(2,1)} %refs_2_.1), channel_id=1, source_target_pairs={{0,1},{1,0},{2,3},{3,2},{4,5},{5,4},{6,7},{7,6},{8,9},{9,8},{10,11... | collective-permute-start | bytes 1572872 | tf_op jit(solution)/shard_map/ppermute | solution.py:738
  101.6 3.0 %collective-permute-start.5 = (bf16[256,1024]{1,0:T(8,128)(2,1)}, bf16[256,1024]{1,0:T(8,128)(2,1)}, u32[]{:S(2)}, u32[]{:S(2)}) collective-permute-start(bf16[256,1024]{1,0:T(8,128)(2,1)} %get-tuple-element.40.refs_0_), channel_id=1, source_target_pairs={{0,1},{1,0},{2,3},{3,2},{4,5},{5,4},{6,7},{7,6},{8,9},{9,8},{10,11... | collective-permute-start | bytes 1572872 | tf_op jit(solution)/shard_map/ppermute | solution.py:738
  116.3 4.3 %copy-start.1 = (bf16[8,256,128]{2,1,0:T(8,128)(2,1)}, bf16[8,256,128]{2,1,0:T(8,128)(2,1)S(1)}, u32[]{:S(2)}) copy-start(bf16[8,256,128]{2,1,0:T(8,128)(2,1)S(1)} %all-to-all-done.2.grad_ref) | copy-start | bytes 1572868
  116.3 35.7 %all-to-all-start.4 = ((bf16[8,64,1024]{2,1,0:T(8,128)(2,1)}), bf16[8,64,1024]{2,1,0:T(8,128)(2,1)}, u32[]{:S(2)}, u32[]{:S(2)}) async-start(bf16[8,64,1024]{2,1,0:T(8,128)(2,1)} %weight_parts.1), calls=%async_computation.4 | async-start | bytes 2097152 | tf_op jit(solution)/shard_map/all_to_all | solution.py:741
  145.8 3.0 %collective-permute-start.8 = (bf16[8,256,256]{2,1,0:T(8,128)(2,1)}, bf16[8,256,256]{2,1,0:T(8,128)(2,1)}, u32[]{:S(2)}, u32[]{:S(2)}) collective-permute-start(bf16[8,256,256]{2,1,0:T(8,128)(2,1)} %get-tuple-element.48), channel_id=1, source_target_pairs={{0,1},{1,0},{2,3},{3,2},{4,5},{5,4},{6,7},{7,6},{8,9},{9,8},{10,11... | collective-permute-start | bytes 3145736 | tf_op jit(solution)/shard_map/ppermute | solution.py:738
  145.8 2.4 %collective-permute-start.7 = (f32[1,128]{1,0:T(1,128)}, f32[1,128]{1,0:T(1,128)S(1)}, u32[]{:S(2)}, u32[]{:S(2)}) collective-permute-start(f32[1,128]{1,0:T(1,128)} %get-tuple-element.47.refs_0_), channel_id=1, source_target_pairs={{0,1},{1,0},{2,3},{3,2},{4,5},{5,4},{6,7},{7,6},{8,9},{9,8},{10,11... | collective-permute-start | bytes 1544 | tf_op jit(solution)/shard_map/ppermute | solution.py:738
  148.2 0.6 copy-start.4
  152.0 6.0 %copy-start.3 = (bf16[256,1024]{1,0:T(8,128)(2,1)S(1)}, bf16[256,1024]{1,0:T(8,128)(2,1)}, u32[]{:S(2)}) copy-start(bf16[256,1024]{1,0:T(8,128)(2,1)} %get-tuple-element.40.refs_0_) | copy-start | bytes 1572868
  152.0 6.0 %copy-start.5 = (bf16[1024,1024]{1,0:T(8,128)(2,1)S(1)}, bf16[1024,1024]{1,0:T(8,128)(2,1)}, u32[]{:S(2)}) copy-start(bf16[1024,1024]{1,0:T(8,128)(2,1)} %param.15) | copy-start | bytes 6291460
  152.0 44.6 %all-to-all-start.3 = ((bf16[8,264,384]{2,1,0:T(8,128)(2,1)}), bf16[8,264,384]{2,1,0:T(8,128)(2,1)}, u32[]{:S(2)}, u32[]{:S(2)}) async-start(bf16[8,264,384]{2,1,0:T(8,128)(2,1)} %join_rows.1), calls=%async_computation.3 | async-start | bytes 3244032 | tf_op jit(solution)/shard_map/all_to_all | solution.py:741
